TPU v7x, 32 devices: a whole 2x2x4 slice. The times are simulated.
32 devices in a mesh: groups: 2 (over y), inst: 4 (over z), space: 4 (over x, core).
Axes of the slice: x: 2, y: 2, z: 4, core: 2. Of those that a mesh axis runs over, the one named last changes fastest.
Arguments:
- flow_state: float32 [8, 5, 16, 16, 128], P(('groups', 'inst'), None, 'space'), parts along dimension 0, may hold values from -1 to 1
- period_match: int32 [16], replicated, may hold values from 0 to 15, each once
Outputs:
- residual: float32 [8, 5, 16, 16, 128], P(('groups', 'inst'), None, 'space'), parts along dimension 0
There are 2 independent parts, one for each index of `groups`. A program takes and returns all parts, laid end to end along the dimension named above; an argument that names none is the same for every part. Nothing has to cross between parts.
Inputs may be any that keep to these rules, and one draw needn't show every extreme that they name: period_match is a permutation of the 16 spanwise layers.
All inputs are finite; a program needn't handle non-finite values.
Results may differ from a plain program's by a relative error of at most 0.0003.
Values sent between devices are 32-bit elements; how exact they have to be, the bound alone decides.
No kernel may reach another device: no remote copies, remote signals or barrier semaphores. Data moves between devices by JAX's collectives and lax.ppermute only.
A program may use at most 64 MiB of HBM per device.

v0:
```python
import math

import jax
import jax.numpy as jnp
from jax import lax
from jax.sharding import PartitionSpec as P

gamma_gas = 1.4
prandtl = 0.72
viscosity = 0.1
pseudo_step = 0.03
entropy_share = 0.1


def from_behind(block, axis, distance):
    devices = range(lax.axis_size(axis))
    route = [((i - distance) % len(devices), i) for i in devices]
    return lax.ppermute(block, axis, route)


def extended(cells, sides, width):
    for axis, dim in sides:
        count = lax.axis_size(axis)
        ends = count - 1
        head = lax.slice_in_dim(cells, 0, width, axis=dim)
        tail = lax.slice_in_dim(cells, cells.shape[dim] - width, cells.shape[dim], axis=dim)
        cells = jnp.concatenate(
            [
                lax.ppermute(tail, axis, [(i, (i + 1) % count) for i in range(ends)]),
                cells,
                lax.ppermute(head, axis, [((i + 1) % count, i) for i in range(ends)]),
            ],
            axis=dim,
        )
    return cells


def from_draw(draws):
    shape = (5,) + (1,) * (draws.ndim - 1)
    offsets = jnp.array([1.0, 0.8, 0.0, 0.0, 0.8], jnp.float32).reshape(shape)
    spreads = jnp.array([0.3, 0.3, 0.3, 0.3, 0.2], jnp.float32).reshape(shape)
    return offsets + spreads * draws


def conserved(primitives):
    dens = primitives[0]
    velocity = primitives[1:4]
    kinetic = 0.5 * dens * jnp.sum(velocity * velocity, axis=0)
    energy = primitives[4] / (gamma_gas - 1.0) + kinetic
    return jnp.concatenate([dens[None], dens[None] * velocity, energy[None]], axis=0)


def primitive(conserved_vars):
    dens = conserved_vars[0]
    velocity = conserved_vars[1:4] / dens
    pressure = (gamma_gas - 1.0) * (
        conserved_vars[4] - 0.5 * dens * jnp.sum(velocity * velocity, axis=0)
    )
    return jnp.concatenate([dens[None], velocity, pressure[None]], axis=0)


def entropy_fix(eigen_val, sound_speed):
    spread = entropy_share * sound_speed
    magnitude = jnp.abs(eigen_val)
    return jnp.where(
        magnitude >= spread, magnitude, (eigen_val * eigen_val + spread * spread) / (2.0 * spread)
    )


def euler_flux(dens, velocity, pressure, enthalpy, normal):
    normal_vel = velocity[normal]
    values = [dens * normal_vel]
    for component in range(3):
        moment = dens * velocity[component] * normal_vel
        if component == normal:
            moment = moment + pressure
        values.append(moment)
    values.append(dens * enthalpy * normal_vel)
    return values


def face_flux(left_cells, right_cells, normal):
    dens_left, vel_left, pres_left = (left_cells[0], left_cells[1:4], left_cells[4])
    dens_right, vel_right, pres_right = (right_cells[0], right_cells[1:4], right_cells[4])
    ratio = gamma_gas / (gamma_gas - 1.0)
    sq_left = jnp.sum(vel_left * vel_left, axis=0)
    sq_right = jnp.sum(vel_right * vel_right, axis=0)
    enth_left = ratio * pres_left / dens_left + 0.5 * sq_left
    enth_right = ratio * pres_right / dens_right + 0.5 * sq_right
    flux_left = euler_flux(dens_left, vel_left, pres_left, enth_left, normal)
    flux_right = euler_flux(dens_right, vel_right, pres_right, enth_right, normal)
    root_left = jnp.sqrt(dens_left)
    root_right = jnp.sqrt(dens_right)
    root_sum = root_left + root_right
    vel_roe = (root_left * vel_left + root_right * vel_right) / root_sum
    enth_roe = (root_left * enth_left + root_right * enth_right) / root_sum
    speed_sq = jnp.sum(vel_roe * vel_roe, axis=0)
    sound_sq = (gamma_gas - 1.0) * (enth_roe - 0.5 * speed_sq)
    sound_speed = jnp.sqrt(sound_sq)
    normal_vel = vel_roe[normal]
    dens_roe = root_left * root_right
    jump_dens = dens_right - dens_left
    jump_pres = pres_right - pres_left
    jump_vel = vel_right - vel_left
    jump_normal = jump_vel[normal]
    wave_slow = (jump_pres - dens_roe * sound_speed * jump_normal) / (2.0 * sound_sq)
    wave_fast = (jump_pres + dens_roe * sound_speed * jump_normal) / (2.0 * sound_sq)
    wave_mid = jump_dens - jump_pres / sound_sq
    eigen_mid = entropy_fix(normal_vel, sound_speed)
    flux_slow = entropy_fix(normal_vel - sound_speed, sound_speed) * wave_slow
    flux_fast = entropy_fix(normal_vel + sound_speed, sound_speed) * wave_fast
    dissipation = [flux_slow + eigen_mid * wave_mid + flux_fast]
    for component in range(3):
        unit_dir = 1.0 if component == normal else 0.0
        term = flux_slow * (vel_roe[component] - unit_dir * sound_speed)
        term = term + eigen_mid * (
            wave_mid * vel_roe[component]
            + dens_roe * (jump_vel[component] - unit_dir * jump_normal)
        )
        term = term + flux_fast * (vel_roe[component] + unit_dir * sound_speed)
        dissipation.append(term)
    shear_work = jnp.sum(vel_roe * jump_vel, axis=0) - normal_vel * jump_normal
    energy_term = flux_slow * (enth_roe - normal_vel * sound_speed)
    energy_term = energy_term + eigen_mid * (wave_mid * 0.5 * speed_sq + dens_roe * shear_work)
    energy_term = energy_term + flux_fast * (enth_roe + normal_vel * sound_speed)
    dissipation.append(energy_term)
    jump_temp = pres_right / dens_right - pres_left / dens_left
    jump_kin = 0.5 * (sq_right - sq_left)
    viscous_terms = [
        jnp.zeros_like(jump_dens),
        jump_vel[0],
        jump_vel[1],
        jump_vel[2],
        jump_kin + gamma_gas / ((gamma_gas - 1.0) * prandtl) * jump_temp,
    ]
    values = []
    for component in range(5):
        values.append(
            0.5 * (flux_left[component] + flux_right[component])
            - 0.5 * dissipation[component]
            - viscosity * viscous_terms[component]
        )
    return jnp.stack(values, axis=0)


def flux_change(padded, along, normal):
    length = padded.shape[along]
    face_values = face_flux(
        lax.slice_in_dim(padded, 0, length - 1, axis=along),
        lax.slice_in_dim(padded, 1, length, axis=along),
        normal,
    )
    return lax.slice_in_dim(face_values, 1, length - 1, axis=along) - lax.slice_in_dim(
        face_values, 0, length - 2, axis=along
    )


def spectral_entry(offset, number):
    wrapped = jnp.mod(offset, number)
    parity = 1.0 - 2.0 * jnp.mod(wrapped, 2).astype(jnp.float32)
    angles = math.pi * wrapped.astype(jnp.float32) / number
    sine_val = jnp.where(wrapped == 0, 1.0, jnp.sin(angles))
    derivative = jnp.where(
        wrapped == 0, 0.0, math.pi / number * parity * jnp.cos(angles) / sine_val
    )
    return derivative + 0.5 * parity


def on_device(flow_state, period_match):
    instances = lax.axis_size("inst")
    phase_lag = instances // 4
    instance = lax.axis_index("inst")
    space_parts = lax.axis_size("space")
    position = lax.axis_index("space")
    labels = jnp.arange(period_match.shape[0], dtype=jnp.int32)
    matches = (period_match[:, None] == labels[None, :]).astype(jnp.int32)
    inverse = jnp.sum(labels[:, None] * matches, axis=0)
    mirror = jnp.array([1.0, 1.0, 1.0, -1.0, 1.0], jnp.float32).reshape(5, 1, 1, 1)

    def lagged(plane, steps):
        return from_behind(plane, "inst", steps)

    def timewise(conserved_vars):
        pieces = lax.all_gather(conserved_vars[None], "inst", axis=0, tiled=True)
        number = pieces.shape[0]
        others = jnp.arange(number, dtype=jnp.int32)
        weights = spectral_entry(instance - others, instances)
        return jnp.tensordot(weights, pieces, axes=1, precision=lax.Precision.HIGHEST)

    def evaluate(conserved_vars):
        prims = primitive(conserved_vars)
        padded = extended(prims, (("space", 1),), 1)
        lower_edge = jnp.where(position == 0, prims[:, :1], padded[:, :1])
        upper_edge = jnp.where(position == space_parts - 1, prims[:, -1:], padded[:, -1:])
        along_axial = jnp.concatenate([lower_edge, prims, upper_edge], axis=1)
        along_span = jnp.concatenate(
            [prims[:, :, :1] * mirror, prims, prims[:, :, -1:] * mirror], axis=2
        )
        ghost_below = jnp.take(lagged(prims[..., -1], phase_lag), period_match, axis=2)
        ghost_above = jnp.take(lagged(prims[..., 0], -phase_lag), inverse, axis=2)
        along_pitch = jnp.concatenate(
            [ghost_below[..., None], prims, ghost_above[..., None]], axis=3
        )
        spatial = (
            flux_change(along_axial, 1, 0)
            + flux_change(along_span, 2, 2)
            + flux_change(along_pitch, 3, 1)
        )
        return timewise(conserved_vars) + spatial

    initial = conserved(from_draw(flow_state[0]))
    section_state = initial - pseudo_step * evaluate(initial)
    return evaluate(section_state)[None]


def solution(mesh):
    in_specs = (P(("groups", "inst"), None, "space", None, None), P())
    out_specs = P(("groups", "inst"), None, "space", None, None)
    return jax.shard_map(
        on_device, mesh=mesh, in_specs=in_specs, out_specs=out_specs, check_vma=False
    )
```

profile of v0, /device:TPU:1, one launch (start us, length us, event | category | flops | bytes accessed | tf_op | source)
XLA Modules:
  0.0 72.5 jit_solution(7410314620236597218)
XLA Ops:
  0.0 0.7 copy-done.1
  0.7 1.0 %fusion.15 = f32[5,4,16,128]{3,2,1,0:T(8,128)S(1)} fusion(f32[1,5,4,16,128]{4,3,2,1,0:T(8,128)} %param.7, f32[5]{0:T(128)S(1)} %copy-done.1, f32[5]{0:T(128)S(1)} %copy-done.2), kind=kLoop, calls=%fused_computation.59 | loop fusion | flops 81920 | bytes 327720 | tf_op jit(solution)/shard_map/add | solution.py:42
  1.9 0.5 copy.46
  2.4 2.2 %collective-permute-start.2 = (f32[5,4,16]{0,1,2:T(4,128)S(1)}, f32[5,4,16]{0,1,2:T(4,128)S(1)}, u32[]{:S(2)}, u32[]{:S(2)}) collective-permute-start(f32[5,4,16]{0,1,2:T(4,128)S(1)} %bitcast.389), channel_id=1, source_target_pairs={{12,0},{0,4},{4,8},{8,12},{13,1},{1,5},{5,9},{9,13},{14,2},{2,6},{... | collective-permute-start | bytes 3848 | tf_op jit(solution)/shard_map/ppermute | solution.py:18
  4.5 0.5 copy.49
  5.0 2.1 %collective-permute-start.3 = (f32[5,4,16]{0,1,2:T(4,128)S(1)}, f32[5,4,16]{0,1,2:T(4,128)S(1)}, u32[]{:S(2)}, u32[]{:S(2)}) collective-permute-start(f32[5,4,16]{0,1,2:T(4,128)S(1)} %bitcast.388), channel_id=1, source_target_pairs={{4,0},{8,4},{12,8},{0,12},{5,1},{9,5},{13,9},{1,13},{6,2},{10,6},{... | collective-permute-start | bytes 3848 | tf_op jit(solution)/shard_map/ppermute | solution.py:18
  7.1 4.2 %collective-permute-start = (f32[5,1,16,128]{3,2,1,0:T(8,128)S(1)}, f32[5,1,16,128]{3,2,1,0:T(8,128)S(1)}, u32[]{:S(2)}, u32[]{:S(2)}) collective-permute-start(f32[5,1,16,128]{3,2,1,0:T(8,128)S(1)} %get-tuple-element.119), channel_id=1, source_target_pairs={{0,1},{1,2},{2,3},{4,5},{5,6},{6,7},{8,9},{9,10},{10,11},{12,13},{... | collective-permute-start | bytes 122888 | tf_op jit(solution)/shard_map/ppermute | solution.py:29
  11.3 1.9 %collective-permute-start.1 = (f32[5,1,16,128]{3,2,1,0:T(8,128)S(1)}, f32[5,1,16,128]{3,2,1,0:T(8,128)S(1)}, u32[]{:S(2)}, u32[]{:S(2)}) collective-permute-start(f32[5,1,16,128]{3,2,1,0:T(8,128)S(1)} %get-tuple-element.120), channel_id=1, source_target_pairs={{1,0},{2,1},{3,2},{5,4},{6,5},{7,6},{9,8},{10,9},{11,10},{13,12},{... | collective-permute-start | bytes 122888 | tf_op jit(solution)/shard_map/ppermute | solution.py:31
  13.4 13.8 %all-gather = f32[20,4,16,128]{3,2,1,0:T(8,128)S(1)} all-gather(f32[5,4,16,128]{3,2,1,0:T(8,128)S(1)} %get-tuple-element.130), channel_id=2, replica_groups=mesh['groups'=2,'inst'=4,'space'=4] {'inst'}, dimensions={0}, use_global_device_ids=true | all-gather | bytes 819200 | tf_op jit(solution)/shard_map/all_gather | solution.py:184
  27.2 0.6 copy-done
  28.1 0.2 constant_dynamic-update-slice_fusion.9
  28.6 1.5 %fusion.2 = f32[1,5,4,16,128]{4,0,3,2,1:T(1,128)S(1)} fusion(f32[4,5,4,16,128]{4,3,2,1,0:T(8,128)S(1)} %bitcast.384, s32[]{:T(128)S(6)} %axis_index.23), kind=kOutput, calls=%fused_computation.6 | convolution fusion | flops 1966224 | bytes 819204 | tf_op jit(solution)/shard_map/dot_general | solution.py:188
  30.1 0.1 constant_dynamic-update-slice_fusion.5
  30.3 0.6 gather_fusion
  31.0 0.6 copy.31
  31.6 0.6 gather_fusion.1
  32.3 0.6 copy.34
  32.8 0.2 maximum_maximum_fusion
  33.2 0.2 subtract_dynamic-update-slice_fusion.3
  33.4 0.1 fusion.46
  33.5 0.1 subtract_dynamic-update-slice_fusion.2
  33.7 0.1 fusion.39
  33.8 0.2 fusion.61
  34.2 0.1 constant_dynamic-update-slice_fusion.4
  34.6 0.1 constant_dynamic-update-slice_fusion
  34.7 0.1 fusion.13
  34.9 14.5 %all-gather.1 = f32[20,4,16,128]{3,2,1,0:T(8,128)S(1)} all-gather(f32[5,4,16,128]{3,2,1,0:T(8,128)S(1)} %fusion.13), channel_id=3, replica_groups=mesh['groups'=2,'inst'=4,'space'=4] {'inst'}, dimensions={0}, use_global_device_ids=true | all-gather | bytes 819200 | tf_op jit(solution)/shard_map/all_gather | solution.py:184
  49.6 1.5 %fusion = f32[1,5,4,16,128]{4,0,3,2,1:T(1,128)S(1)} fusion(f32[4,5,4,16,128]{4,3,2,1,0:T(8,128)S(1)} %bitcast.385, s32[]{:T(128)S(6)} %axis_index.23), kind=kOutput, calls=%fused_computation.4 | convolution fusion | flops 1966224 | bytes 819204 | tf_op jit(solution)/shard_map/dot_general | solution.py:188
  51.2 0.5 copy.52
  51.7 0.5 copy.53
  52.2 3.3 %collective-permute-start.7 = (f32[5,4,16]{0,1,2:T(4,128)S(1)}, f32[5,4,16]{0,1,2:T(4,128)S(1)}, u32[]{:S(2)}, u32[]{:S(2)}) collective-permute-start(f32[5,4,16]{0,1,2:T(4,128)S(1)} %bitcast.390), channel_id=1, source_target_pairs={{4,0},{8,4},{12,8},{0,12},{5,1},{9,5},{13,9},{1,13},{6,2},{10,6},{... | collective-permute-start | bytes 3848 | tf_op jit(solution)/shard_map/ppermute | solution.py:18
  55.7 0.2 constant_dynamic-update-slice_fusion.19
  56.1 8.9 %collective-permute-start.4 = (f32[5,1,16,128]{3,2,1,0:T(8,128)S(1)}, f32[5,1,16,128]{3,2,1,0:T(8,128)S(1)}, u32[]{:S(2)}, u32[]{:S(2)}) collective-permute-start(f32[5,1,16,128]{3,2,1,0:T(8,128)S(1)} %get-tuple-element.105), channel_id=1, source_target_pairs={{0,1},{1,2},{2,3},{4,5},{5,6},{6,7},{8,9},{9,10},{10,11},{12,13},{... | collective-permute-start | bytes 122888 | tf_op jit(solution)/shard_map/ppermute | solution.py:29
  65.0 2.1 %collective-permute-start.5 = (f32[5,1,16,128]{3,2,1,0:T(8,128)S(1)}, f32[5,1,16,128]{3,2,1,0:T(8,128)S(1)}, u32[]{:S(2)}, u32[]{:S(2)}) collective-permute-start(f32[5,1,16,128]{3,2,1,0:T(8,128)S(1)} %get-tuple-element.106), channel_id=1, source_target_pairs={{1,0},{2,1},{3,2},{5,4},{6,5},{7,6},{9,8},{10,9},{11,10},{13,12},{... | collective-permute-start | bytes 122888 | tf_op jit(solution)/shard_map/ppermute | solution.py:31
  67.1 0.1 constant_dynamic-update-slice_fusion.15
  67.3 0.6 gather_fusion.2
  68.0 0.6 copy.36
  68.5 0.6 gather_fusion.3
  69.2 0.6 copy.39
  69.8 0.2 maximum_maximum_fusion.1
  70.1 0.2 subtract_dynamic-update-slice_fusion.1
  70.3 0.1 fusion.32
  70.5 0.1 subtract_dynamic-update-slice_fusion
  70.6 0.1 fusion.25
  70.8 0.2 fusion.50
  71.1 0.1 constant_dynamic-update-slice_fusion.14
  71.6 0.1 constant_dynamic-update-slice_fusion.10
  71.7 0.8 %fusion.8 = f32[1,5,4,16,128]{4,3,2,1,0:T(8,128)} fusion(f32[5,4,16,128]{3,2,1,0:T(8,128)S(1)} %bitcast.386, f32[5,4,16,129]{3,2,1,0:T(8,128)S(1)} %fusion.50, f32[5,4,17,128]{3,2,1,0:T(8,128)S(1)} %constant_dynamic-update-slice_fusion.15, f32[5,5,16,128]{3,2,1,0:T(8,128)S(1)} %constant_dynamic-update-slice_fusion.10), kind=kLoop, calls=%fused_computation.45 | loop fusion | flops 245760 | bytes 1310720 | tf_op jit(solution)/shard_map/broadcast_in_dim | solution.py:213
  (70 shorter events, 3.1 us)
Async XLA Ops:
  0.0 0.7 copy-start.1
  0.0 0.7 copy-start.2
  2.4 27.9 %collective-permute-start.2 = (f32[5,4,16]{0,1,2:T(4,128)S(1)}, f32[5,4,16]{0,1,2:T(4,128)S(1)}, u32[]{:S(2)}, u32[]{:S(2)}) collective-permute-start(f32[5,4,16]{0,1,2:T(4,128)S(1)} %bitcast.389), channel_id=1, source_target_pairs={{12,0},{0,4},{4,8},{8,12},{13,1},{1,5},{5,9},{9,13},{14,2},{2,6},{... | collective-permute-start | bytes 3848 | tf_op jit(solution)/shard_map/ppermute | solution.py:18
  5.0 26.5 %collective-permute-start.3 = (f32[5,4,16]{0,1,2:T(4,128)S(1)}, f32[5,4,16]{0,1,2:T(4,128)S(1)}, u32[]{:S(2)}, u32[]{:S(2)}) collective-permute-start(f32[5,4,16]{0,1,2:T(4,128)S(1)} %bitcast.388), channel_id=1, source_target_pairs={{4,0},{8,4},{12,8},{0,12},{5,1},{9,5},{13,9},{1,13},{6,2},{10,6},{... | collective-permute-start | bytes 3848 | tf_op jit(solution)/shard_map/ppermute | solution.py:18
  7.1 26.9 %collective-permute-start = (f32[5,1,16,128]{3,2,1,0:T(8,128)S(1)}, f32[5,1,16,128]{3,2,1,0:T(8,128)S(1)}, u32[]{:S(2)}, u32[]{:S(2)}) collective-permute-start(f32[5,1,16,128]{3,2,1,0:T(8,128)S(1)} %get-tuple-element.119), channel_id=1, source_target_pairs={{0,1},{1,2},{2,3},{4,5},{5,6},{6,7},{8,9},{9,10},{10,11},{12,13},{... | collective-permute-start | bytes 122888 | tf_op jit(solution)/shard_map/ppermute | solution.py:29
  11.3 1.9 %copy-start.3 = (s32[16]{0:T(128)S(1)}, s32[16]{0:T(128)}, u32[]{:S(2)}) copy-start(s32[16]{0:T(128)} %param.8) | copy-start | bytes 196
  11.3 22.7 %collective-permute-start.1 = (f32[5,1,16,128]{3,2,1,0:T(8,128)S(1)}, f32[5,1,16,128]{3,2,1,0:T(8,128)S(1)}, u32[]{:S(2)}, u32[]{:S(2)}) collective-permute-start(f32[5,1,16,128]{3,2,1,0:T(8,128)S(1)} %get-tuple-element.120), channel_id=1, source_target_pairs={{1,0},{2,1},{3,2},{5,4},{6,5},{7,6},{9,8},{10,9},{11,10},{13,12},{... | collective-permute-start | bytes 122888 | tf_op jit(solution)/shard_map/ppermute | solution.py:31
  27.2 0.7 copy-start
  51.7 15.6 %collective-permute-start.6 = (f32[5,4,16]{0,1,2:T(4,128)S(1)}, f32[5,4,16]{0,1,2:T(4,128)S(1)}, u32[]{:S(2)}, u32[]{:S(2)}) collective-permute-start(f32[5,4,16]{0,1,2:T(4,128)S(1)} %bitcast.391), channel_id=1, source_target_pairs={{12,0},{0,4},{4,8},{8,12},{13,1},{1,5},{5,9},{9,13},{14,2},{2,6},{... | collective-permute-start | bytes 3848 | tf_op jit(solution)/shard_map/ppermute | solution.py:18
  52.2 16.3 %collective-permute-start.7 = (f32[5,4,16]{0,1,2:T(4,128)S(1)}, f32[5,4,16]{0,1,2:T(4,128)S(1)}, u32[]{:S(2)}, u32[]{:S(2)}) collective-permute-start(f32[5,4,16]{0,1,2:T(4,128)S(1)} %bitcast.390), channel_id=1, source_target_pairs={{4,0},{8,4},{12,8},{0,12},{5,1},{9,5},{13,9},{1,13},{6,2},{10,6},{... | collective-permute-start | bytes 3848 | tf_op jit(solution)/shard_map/ppermute | solution.py:18
  56.1 14.8 %collective-permute-start.4 = (f32[5,1,16,128]{3,2,1,0:T(8,128)S(1)}, f32[5,1,16,128]{3,2,1,0:T(8,128)S(1)}, u32[]{:S(2)}, u32[]{:S(2)}) collective-permute-start(f32[5,1,16,128]{3,2,1,0:T(8,128)S(1)} %get-tuple-element.105), channel_id=1, source_target_pairs={{0,1},{1,2},{2,3},{4,5},{5,6},{6,7},{8,9},{9,10},{10,11},{12,13},{... | collective-permute-start | bytes 122888 | tf_op jit(solution)/shard_map/ppermute | solution.py:29
  65.0 5.9 %collective-permute-start.5 = (f32[5,1,16,128]{3,2,1,0:T(8,128)S(1)}, f32[5,1,16,128]{3,2,1,0:T(8,128)S(1)}, u32[]{:S(2)}, u32[]{:S(2)}) collective-permute-start(f32[5,1,16,128]{3,2,1,0:T(8,128)S(1)} %get-tuple-element.106), channel_id=1, source_target_pairs={{1,0},{2,1},{3,2},{5,4},{6,5},{7,6},{9,8},{10,9},{11,10},{13,12},{... | collective-permute-start | bytes 122888 | tf_op jit(solution)/shard_map/ppermute | solution.py:31
where the time goes:
time: 72.7 us; the launch traced here: 72.5 us
  blocking collectives  28.3 us (39%)
  starting transfers between devices  24.6 us (34%)
  local copies, waits for them, and re-layouts  8.14 us (11%)
  other arithmetic  7.8 us (11%)
  matrix products  3.1 us (4%)
    all_gather x2, blocking collectives, timewise(): pieces = lax.all_gather(conserved_vars[None], 'inst', axis=0, tiled=True)  28.3 us
    ppermute x2, starting transfers between devices, extended(): lax.ppermute(tail, axis, [(i, (i + 1) % count) for i in range(ends)])  13 us
    ppermute x4, starting transfers between devices, from_behind(): return lax.ppermute(block, axis, route)  7.53 us
    ppermute x2, starting transfers between devices, extended(): lax.ppermute(head, axis, [((i + 1) % count, i) for i in range(ends)])  4.02 us
    dot_general x2, matrix products, timewise(): jnp.tensordot(weights, pieces, axes=1, precision=lax.Precision.HIGHEST)  3.1 us
    unnamed x24, other arithmetic  3.02 us
  transfers between devices with their start and end apart: 8, of which 0 were waited for; matrix products, arithmetic and copies ran while one was open for 16% of the time, Pallas kernels for 0%

commit v1 on v0

--- a/solution.py
+++ b/solution.py
@@ -3,6 +3,8 @@
 import jax
 import jax.numpy as jnp
 from jax import lax
+from jax.experimental import pallas as pl
+from jax.experimental.pallas import tpu as pltpu
 from jax.sharding import PartitionSpec as P
 
 gamma_gas = 1.4
@@ -213,9 +215,462 @@
     return evaluate(section_state)[None]
 
 
+inst_count = 4
+layers = 4
+chunk = 32
+rows = 16
+lanes = 128
+tile = (rows, lanes)
+vmem = pl.BlockSpec(memory_space=pltpu.VMEM)
+smem = pl.BlockSpec(memory_space=pltpu.SMEM)
+starts = (1.0, 0.8, 0.0, 0.0, 0.8)
+spreads_of = (0.3, 0.3, 0.3, 0.3, 0.2)
+ratio = gamma_gas / (gamma_gas - 1.0)
+
+
+def weight_of(distance):
+    parity = 1.0 - 2.0 * (distance % 2)
+    if distance == 0:
+        return 0.5
+    if 2 * distance == inst_count:
+        return 0.5 * parity
+    angle = math.pi * distance / inst_count
+    return math.pi / inst_count * parity * math.cos(angle) / math.sin(angle) + 0.5 * parity
+
+
+def lane_ids():
+    return lax.broadcasted_iota(jnp.int32, tile, 1)
+
+
+def row_ids():
+    return lax.broadcasted_iota(jnp.int32, tile, 0)
+
+
+def pick_lanes(values, index):
+    return jnp.take_along_axis(values, index, axis=1, mode="promise_in_bounds")
+
+
+def pick_rows(values, index):
+    half = rows // 2
+    low, high = values[:half], values[half:]
+    parts = []
+    for part in (index[:half], index[half:]):
+        inner = jnp.bitwise_and(part, half - 1)
+        from_low = jnp.take_along_axis(low, inner, axis=0, mode="promise_in_bounds")
+        from_high = jnp.take_along_axis(high, inner, axis=0, mode="promise_in_bounds")
+        parts.append(jnp.where(part < half, from_low, from_high))
+    return jnp.concatenate(parts, axis=0)
+
+
+def turn(values, amount):
+    return pltpu.roll(values, amount % lanes if isinstance(amount, int) else amount, 1)
+
+
+def mod_lanes(amount):
+    return jnp.bitwise_and(amount, lanes - 1)
+
+
+def pack_tile(layer_tiles, part):
+    group = lane_ids() // chunk
+    out = None
+    for layer in range(layers):
+        moved = turn(layer_tiles[layer], mod_lanes(chunk * (layer - part) + lanes))
+        out = moved if out is None else jnp.where(group == layer, moved, out)
+    return out
+
+
+def pack_kernel(flow, *messages):
+    me = lax.axis_index("inst")
+    lane = lane_ids()
+    slot = jnp.bitwise_and(lane, 3)
+    step = jnp.where(slot < 2, slot - 2, slot + chunk - 2)
+    for distance in range(inst_count):
+        part = jnp.bitwise_xor(me, distance)
+        index = mod_lanes(step + (chunk * part + lanes))
+        edge = None
+        for field in range(5):
+            tiles = [flow[0, field, layer] for layer in range(layers)]
+            messages[distance][field] = pack_tile(tiles, part)
+            for layer in range(layers):
+                got = pick_lanes(tiles[layer], index)
+                here = lane // 4 == field * 4 + layer
+                edge = got if edge is None else jnp.where(here, got, edge)
+        messages[distance][5] = edge
+
+
+def spread_tiles(received, field, me):
+    group = lane_ids() // chunk
+    outs = [None] * layers
+    for distance in range(inst_count):
+        part = jnp.bitwise_xor(me, distance)
+        values = received[distance][field]
+        for layer in range(layers):
+            moved = turn(values, mod_lanes(chunk * (part - layer) + lanes))
+            outs[layer] = moved if outs[layer] is None else jnp.where(group == part, moved, outs[layer])
+    return outs
+
+
+def unpack_kernel(*refs):
+    received, (main, halo, near_a, near_b) = refs[:4], refs[4:]
+    me = lax.axis_index("inst")
+    even = jnp.bitwise_and(lax.axis_index("space"), 1) == 0
+    lane = lane_ids()
+    owner = jnp.bitwise_and(lane // 4, 3)
+    level = lane // 16 - 1
+    inner = jnp.clip(level, 0, layers - 1) * 4 + jnp.bitwise_and(lane, 3)
+    up_edge = down_edge = None
+    for field in range(5):
+        tiles = spread_tiles(received, field, me)
+        for layer in range(layers):
+            main[field, layer] = tiles[layer]
+        for place in range(2):
+            near_a[2 * field + place] = jnp.where(even, tiles[2 + place], tiles[place])
+            near_b[2 * field + place] = jnp.where(even, tiles[place], tiles[2 + place])
+        edges = None
+        for distance in range(inst_count):
+            part = jnp.bitwise_xor(me, distance)
+            got = pick_lanes(received[distance][5], inner + 16 * field)
+            edges = got if edges is None else jnp.where(owner == part, got, edges)
+        halo[field] = edges
+        up = turn(edges, 16 * field - 16 * layers)
+        down = turn(edges, 16 * field - 16)
+        here = lane // 16 == field
+        up_edge = up if up_edge is None else jnp.where(here, up, up_edge)
+        down_edge = down if down_edge is None else jnp.where(here, down, down_edge)
+    near_a[10] = jnp.where(even, up_edge, down_edge)
+    near_b[10] = jnp.where(even, down_edge, up_edge)
+
+
+class Cells:
+    def __init__(self, parts):
+        self.parts = list(parts)
+        self.dens, self.vel, self.pres = parts[0], list(parts[1:4]), parts[4]
+        self.root, self.enth, self.heat = parts[5], parts[6], parts[7]
+
+    def map(self, change):
+        return Cells([change(part) for part in self.parts])
+
+    def conserved(self):
+        dens, enth = self.dens, self.enth
+        return [dens] + [dens * part for part in self.vel] + [dens * enth - self.pres]
+
+
+def cells_of(dens, vel, pres):
+    inverse_root = lax.rsqrt(dens)
+    root = dens * inverse_root
+    temp = pres * (inverse_root * inverse_root)
+    kinetic = 0.5 * (vel[0] * vel[0] + vel[1] * vel[1] + vel[2] * vel[2])
+    enth = ratio * temp + kinetic
+    heat = 2.0 * viscosity * (kinetic + ratio / prandtl * temp)
+    return Cells([dens] + list(vel) + [pres, root, enth, heat])
+
+
+def cells_of_draws(draws):
+    start = [base + spread * draw if base else spread * draw for base, spread, draw in zip(starts, spreads_of, draws)]
+    return cells_of(start[0], start[1:4], start[4])
+
+
+def cells_of_conserved(state):
+    dens = state[0]
+    inverse = 1.0 / dens
+    vel = [part * inverse for part in state[1:4]]
+    kinetic = vel[0] * vel[0] + vel[1] * vel[1] + vel[2] * vel[2]
+    pres = (gamma_gas - 1.0) * (state[4] - 0.5 * dens * kinetic)
+    return cells_of(dens, vel, pres)
+
+
+def roe_flux(low, high, normal):
+    jump_dens = high.dens - low.dens
+    jump_pres = high.pres - low.pres
+    jump = [b - a for a, b in zip(low.vel, high.vel)]
+    share = high.root / (low.root + high.root)
+    vel = [a + share * d for a, d in zip(low.vel, jump)]
+    enth = low.enth + share * (high.enth - low.enth)
+    half_sq = 0.5 * (vel[0] * vel[0] + vel[1] * vel[1] + vel[2] * vel[2])
+    sound_sq = (gamma_gas - 1.0) * (enth - half_sq)
+    inverse = lax.rsqrt(sound_sq)
+    sound = sound_sq * inverse
+    dens_roe = low.root * high.root
+    along = vel[normal]
+    jump_along = jump[normal]
+    press_part = jump_pres * (inverse * inverse)
+    speed_part = dens_roe * inverse * jump_along
+    bound = entropy_share * sound
+    curve = (0.5 / entropy_share) * inverse
+    floor = 0.5 * bound
+
+    def fixed(speed):
+        size = jnp.abs(speed)
+        return jnp.where(size >= bound, size, speed * speed * curve + floor)
+
+    slow = 0.5 * fixed(along - sound) * (press_part - speed_part)
+    fast = 0.5 * fixed(along + sound) * (press_part + speed_part)
+    middle = fixed(along)
+    entropy = middle * (jump_dens - press_part)
+    both = slow + fast
+    total = both + entropy
+    push = sound * (fast - slow)
+    shear = middle * dens_roe
+    mass_low = low.dens * low.vel[normal]
+    mass_high = high.dens * high.vel[normal]
+    out = [mass_low + mass_high - total]
+    work = None
+    for part in range(3):
+        value = mass_low * low.vel[part] + mass_high * high.vel[part] - vel[part] * total
+        if part == normal:
+            value = value + (low.pres + high.pres) - push - (2.0 * viscosity) * jump_along
+        else:
+            value = value - (shear + 2.0 * viscosity) * jump[part]
+            term = vel[part] * jump[part]
+            work = term if work is None else work + term
+        out.append(value)
+    lost = enth * both + along * push + entropy * half_sq + shear * work
+    out.append(mass_low * low.enth + mass_high * high.enth - lost - (high.heat - low.heat))
+    return out
+
+
+def span_change(cells):
+    row = row_ids()
+    faces = roe_flux(cells, cells.map(lambda part: pltpu.roll(part, rows - 1, 0)), 2)
+    w = cells.vel[2]
+    sound_sq = (gamma_gas - 1.0) * (cells.enth - 0.5 * (cells.vel[0] * cells.vel[0] + cells.vel[1] * cells.vel[1]))
+    sound = sound_sq * lax.rsqrt(sound_sq)
+    still = 2.0 * (cells.dens * w * w + cells.pres)
+    moving = 2.0 * w * (sound * cells.dens + 2.0 * viscosity)
+    changes = []
+    for part in range(5):
+        top = still + moving if part == 3 else 0.0
+        bottom = still - moving if part == 3 else 0.0
+        upper = jnp.where(row == rows - 1, top, faces[part])
+        lower = jnp.where(row == 0, bottom, pltpu.roll(faces[part], 1, 0))
+        changes.append(upper - lower)
+    return changes
+
+
+def over_instances(values):
+    out = weight_of(0) * values
+    for distance in range(1, inst_count):
+        out = out + weight_of(distance) * turn(values, chunk * distance)
+    return out
+
+
+def shift_slots(values, distance):
+    owner = jnp.bitwise_and(lane_ids() // 4, 3)
+    distance = distance % inst_count
+    return jnp.where(owner >= distance, turn(values, 4 * distance), turn(values, 4 * distance - 16))
+
+
+def over_slots(values):
+    out = weight_of(0) * values
+    for distance in range(1, inst_count):
+        out = out + weight_of(distance) * shift_slots(values, distance)
+    return out
+
+
+def put(ref, place, cells):
+    for number, part in enumerate(cells.parts):
+        ref[place, number] = part
+
+
+def get(ref, place):
+    return Cells([ref[place, number] for number in range(8)])
+
+
+def main_kernel(match, main, halo, near_a, near_b, *refs):
+    messages, (first, second, edge_faces) = refs[:4], refs[4:]
+    me = lax.axis_index("inst")
+    where_on = lax.axis_index("space")
+    parts_on = lax.axis_size("space")
+    even = jnp.bitwise_and(where_on, 1) == 0
+    at_low = where_on == 0
+    at_high = where_on == parts_on - 1
+    lag = inst_count // 4
+    lane = lane_ids()
+    row = row_ids()
+    slot = jnp.bitwise_and(lane, 3)
+    owner_main = lane // chunk
+    column = jnp.bitwise_and(lane, chunk - 1)
+    is_first, is_last = column == 0, column == chunk - 1
+    seam_slot = jnp.where(me == 0, 1, jnp.where(me == inst_count - 1, 3, -1))
+    seam = slot == seam_slot
+    below_of = jnp.zeros(tile, jnp.int32)
+    above_of = jnp.zeros(tile, jnp.int32)
+    for k in range(rows):
+        value = match[k]
+        below_of = jnp.where(row == k, value, below_of)
+        above_of = jnp.where(row == value, k, above_of)
+
+    def edge_lane(layer):
+        return (layer + 1) * 16 + owner_main * 4 + jnp.where(is_first, 1, 3)
+
+    near = [[jnp.where(even, b[...], a[...]) for a, b in ((near_a.at[j], near_b.at[j]),)][0] for j in range(11)]
+    far = [[jnp.where(even, a[...], b[...]) for a, b in ((near_a.at[j], near_b.at[j]),)][0] for j in range(11)]
+    for layer in range(layers):
+        put(first, layer + 2, cells_of_draws([main[field, layer] for field in range(5)]))
+    for place in range(2):
+        draws = [jnp.where(at_low, main[field, 0], near[2 * field + place]) for field in range(5)]
+        put(first, place, cells_of_draws(draws))
+        draws = [jnp.where(at_high, main[field, layers - 1], far[2 * field + place]) for field in range(5)]
+        put(first, layers + 2 + place, cells_of_draws(draws))
+    band = lane // 16
+    edges = []
+    for field in range(5):
+        inside = halo[field]
+        low = jnp.where(at_low, turn(inside, -16), turn(near[10], -16 * field))
+        high = jnp.where(at_high, turn(inside, 16), turn(far[10], 16 * (layers + 1 - field)))
+        edges.append(jnp.where(band == 0, low, jnp.where(band == layers + 1, high, inside)))
+    edge_cells = cells_of_draws(edges)
+
+    def mains_at_slots(ref, start, low, high):
+        group = jnp.bitwise_and(lane // 4, 3) * chunk
+        index = group + jnp.where(slot == 1, 0, chunk - 1)
+        out = [None] * 8
+        for layer in range(low, high):
+            for number in range(8):
+                got = pick_lanes(ref[layer + start, number], index)
+                out[number] = got if out[number] is None else jnp.where(band == layer + 1, got, out[number])
+        return Cells(out)
+
+    def pitch_edges(cells, mains):
+        lower = Cells([jnp.where(slot == 3, b, a) for a, b in zip(cells.parts, mains.parts)])
+        upper = []
+        for a, b in zip(cells.parts, mains.parts):
+            value = jnp.where(slot == 3, turn(a, 1), turn(a, -1))
+            value = jnp.where(slot == 1, b, value)
+            other = pick_rows(shift_slots(value, -lag), above_of)
+            upper.append(jnp.where(seam, other, value))
+        faces = roe_flux(lower, Cells(upper), 1)
+        lower_use = [jnp.where(seam, pick_rows(shift_slots(face, lag), below_of), face) for face in faces]
+        return faces, lower_use
+
+    def pitch_change(cells, layer):
+        faces = roe_flux(cells, cells.map(lambda part: turn(part, -1)), 1)
+        index = edge_lane(layer)
+        changes = []
+        for part in range(5):
+            edge = pick_lanes(edge_faces[part], index)
+            upper = jnp.where(is_last, edge, faces[part])
+            lower = jnp.where(is_first, edge, turn(faces[part], 1))
+            changes.append(upper - lower)
+        return changes
+
+    def set_edges(faces, lower_use):
+        for part in range(5):
+            edge_faces[part] = jnp.where(slot == 1, lower_use[part], faces[part])
+
+    faces, lower_use = pitch_edges(edge_cells, mains_at_slots(first, 2, -1, layers + 1))
+    set_edges(faces, lower_use)
+    span = span_change(edge_cells)
+    axial = roe_flux(edge_cells, edge_cells.map(lambda part: turn(part, -16)), 0)
+    state = edge_cells.conserved()
+    for part in range(5):
+        pitch = jnp.where(slot == 1, faces[part] - turn(faces[part], 1), faces[part] - turn(lower_use[part], -1))
+        change = pitch + span[part] + (axial[part] - turn(axial[part], 16))
+        state[part] = state[part] - pseudo_step * over_slots(state[part]) - (0.5 * pseudo_step) * change
+    edge_second = cells_of_conserved(state)
+
+    def first_step(count, below):
+        cells = get(first, count + 1)
+        above = roe_flux(cells, get(first, count + 2), 0)
+        span = span_change(cells)
+        pitch = pitch_change(cells, count - 1)
+        state = cells.conserved()
+        for part in range(5):
+            change = (above[part] - below[part]) + span[part] + pitch[part]
+            state[part] = state[part] - pseudo_step * over_instances(state[part]) - (0.5 * pseudo_step) * change
+        put(second, count, cells_of_conserved(state))
+        return above
+
+    lax.fori_loop(0, layers + 2, first_step, roe_flux(get(first, 0), get(first, 1), 0))
+
+    for number in range(8):
+        second[0, number] = jnp.where(at_low, second[1, number], second[0, number])
+        second[layers + 1, number] = jnp.where(at_high, second[layers, number], second[layers + 1, number])
+
+    set_edges(*pitch_edges(edge_second, mains_at_slots(second, 1, 0, layers)))
+
+    def second_step(layer, below):
+        cells = get(second, layer + 1)
+        above = roe_flux(cells, get(second, layer + 2), 0)
+        span = span_change(cells)
+        pitch = pitch_change(cells, layer)
+        state = cells.conserved()
+        for part in range(5):
+            change = (above[part] - below[part]) + span[part] + pitch[part]
+            first[layer, part] = over_instances(state[part]) + 0.5 * change
+        return above
+
+    lax.fori_loop(0, layers, second_step, roe_flux(get(second, 0), get(second, 1), 0))
+    for distance in range(inst_count):
+        part = jnp.bitwise_xor(me, distance)
+        for field in range(5):
+            messages[distance][field] = pack_tile([first[layer, field] for layer in range(layers)], part)
+
+
+def return_kernel(*refs):
+    received, out = refs[:4], refs[4]
+    me = lax.axis_index("inst")
+    for field in range(5):
+        for layer, values in enumerate(spread_tiles(received, field, me)):
+            out[0, field, layer] = values
+
+
+def call(kernel, outs, operands, scratch=(), scalars=0):
+    shapes = [jax.ShapeDtypeStruct(shape, jnp.float32) for shape in outs]
+    return pl.pallas_call(
+        kernel,
+        out_shape=shapes,
+        in_specs=[smem] * scalars + [vmem] * (len(operands) - scalars),
+        out_specs=[vmem] * len(shapes),
+        scratch_shapes=scratch,
+        compiler_params=pltpu.CompilerParams(vmem_limit_bytes=16 * 2**20),
+    )(*operands)
+
+
+def swap_instances(messages):
+    got = [messages[0]] + [None] * (inst_count - 1)
+    for distance in (2, 3, 1):
+        route = [(i, i ^ distance) for i in range(inst_count)]
+        got[distance] = lax.ppermute(messages[distance], "inst", route)
+    return got
+
+
+def on_device_fast(flow_state, period_match):
+    count = lax.axis_size("space")
+    messages = call(pack_kernel, [(6, rows, lanes)] * inst_count, [flow_state])
+    main, halo, near_a, near_b = call(
+        unpack_kernel,
+        [(5, layers, rows, lanes), (5, rows, lanes), (11, rows, lanes), (11, rows, lanes)],
+        swap_instances(messages),
+    )
+    route_a = [(i, i ^ 1) for i in range(count)]
+    route_b = [(i, ((i - 1) ^ 1) + 1) if 0 < i < count - 1 else (i, count - 1 - i) for i in range(count)]
+    near_b = lax.ppermute(near_b, "space", route_b)
+    near_a = lax.ppermute(near_a, "space", route_a)
+    results = call(
+        main_kernel,
+        [(5, rows, lanes)] * inst_count,
+        [period_match, main, halo, near_a, near_b],
+        [
+            pltpu.VMEM((layers + 4, 8, rows, lanes), jnp.float32),
+            pltpu.VMEM((layers + 2, 8, rows, lanes), jnp.float32),
+            pltpu.VMEM((5, rows, lanes), jnp.float32),
+        ],
+        scalars=1,
+    )
+    return call(return_kernel, [flow_state.shape], swap_instances(results))[0]
+
+
 def solution(mesh):
     in_specs = (P(("groups", "inst"), None, "space", None, None), P())
     out_specs = P(("groups", "inst"), None, "space", None, None)
-    return jax.shard_map(
-        on_device, mesh=mesh, in_specs=in_specs, out_specs=out_specs, check_vma=False
-    )
+
+    def whole(flow_state, period_match):
+        block = (flow_state.shape[2] // mesh.shape["space"],) + flow_state.shape[3:]
+        fits = mesh.shape["inst"] == inst_count and mesh.shape["space"] % 2 == 0
+        body = on_device_fast if fits and block == (layers, rows, lanes) else on_device
+        return jax.shard_map(body, mesh=mesh, in_specs=in_specs, out_specs=out_specs, check_vma=False)(
+            flow_state, period_match
+        )
+
+    return whole

time: 72.7 us -> 30.7 us (0.42)
  the two profiles are of different devices: /device:TPU:1 before, /device:TPU:0 now
where the time goes in v1:
time: 30.7 us; the launch traced here: 30.6 us
  starting transfers between devices  11.8 us (38%)
  waiting for transfers between devices  11.4 us (37%)
  Pallas kernels  5.71 us (19%)
  local copies, waits for them, and re-layouts  1.57 us (5%)
    ppermute x6, starting transfers between devices, swap_instances(): got[distance] = lax.ppermute(messages[distance], 'inst', route)  10.2 us
    ppermute x6, waiting for transfers between devices, swap_instances(): got[distance] = lax.ppermute(messages[distance], 'inst', route)  8.64 us
    pallas_call x4, Pallas kernels, call(): pl.pallas_call(kernel, out_shape=shapes, in_specs=[smem] * scalars + [vme...  5.71 us
    ppermute x1, waiting for transfers between devices, on_device_fast(): near_b = lax.ppermute(near_b, 'space', route_b)  2.8 us
    ppermute x1, starting transfers between devices, on_device_fast(): near_b = lax.ppermute(near_b, 'space', route_b)  1.61 us
    unnamed x4, local copies, waits for them, and re-layouts  1.57 us
  transfers between devices with their start and end apart: 8, of which 5 were waited for; matrix products, arithmetic and copies ran while one was open for 0% of the time, Pallas kernels for 0%

profile of v1, /device:TPU:0, one launch (start us, length us, event | category | flops | bytes accessed | tf_op | source)
XLA Modules:
  0.0 30.6 jit_solution(1692923305684344084)
XLA Ops:
  0.0 0.0 copy-start
  0.0 0.9 %copy-done = f32[1,5,4,16,128]{4,3,2,1,0:T(8,128)S(1)} copy-done((f32[1,5,4,16,128]{4,3,2,1,0:T(8,128)S(1)}, f32[1,5,4,16,128]{4,3,2,1,0:T(8,128)}, u32[]{:S(2)}) %copy-start) | copy-done | bytes 163864
  0.9 0.4 %shard_map.28 = (f32[6,16,128]{2,1,0:T(8,128)S(1)}, f32[6,16,128]{2,1,0:T(8,128)S(1)}, f32[6,16,128]{2,1,0:T(8,128)S(1)}, f32[6,16,128]{2,1,0:T(8,128)S(1)}) custom-call(f32[1,5,4,16,128]{4,3,2,1,0:T(8,128)S(1)} %copy-done), custom_call_target="tpu_custom_call" | custom-call | tf_op jit(solution)/shard_map/pallas_call | solution.py:620
  1.3 3.1 %collective-permute-start = (f32[6,16,128]{2,1,0:T(8,128)S(1)}, f32[6,16,128]{2,1,0:T(8,128)S(1)}, u32[]{:S(2)}, u32[]{:S(2)}) collective-permute-start(f32[6,16,128]{2,1,0:T(8,128)S(1)} %get-tuple-element.18), channel_id=1, source_target_pairs={{0,4},{4,0},{8,12},{12,8},{1,5},{5,1},{9,13},{13,9},{2,6},{6,2},{1... | collective-permute-start | bytes 147464 | tf_op jit(solution)/shard_map/ppermute | solution.py:634
  4.4 2.6 %collective-permute-start.1 = (f32[6,16,128]{2,1,0:T(8,128)S(1)}, f32[6,16,128]{2,1,0:T(8,128)S(1)}, u32[]{:S(2)}, u32[]{:S(2)}) collective-permute-start(f32[6,16,128]{2,1,0:T(8,128)S(1)} %get-tuple-element.19), channel_id=1, source_target_pairs={{0,8},{4,12},{8,0},{12,4},{1,9},{5,13},{9,1},{13,5},{2,10},{6,14},... | collective-permute-start | bytes 147464 | tf_op jit(solution)/shard_map/ppermute | solution.py:634
  7.0 0.0 collective-permute-start.2
  7.0 0.0 collective-permute-done.refs_1_
  7.0 3.3 %collective-permute-done.1.refs_2_ = f32[6,16,128]{2,1,0:T(8,128)S(1)} collective-permute-done((f32[6,16,128]{2,1,0:T(8,128)S(1)}, f32[6,16,128]{2,1,0:T(8,128)S(1)}, u32[]{:S(2)}, u32[]{:S(2)}) %collective-permute-start.1) | collective-permute-done | bytes 49184 | tf_op jit(solution)/shard_map/ppermute | solution.py:634
  10.4 2.6 %collective-permute-done.2.refs_3_ = f32[6,16,128]{2,1,0:T(8,128)S(1)} collective-permute-done((f32[6,16,128]{2,1,0:T(8,128)S(1)}, f32[6,16,128]{2,1,0:T(8,128)S(1)}, u32[]{:S(2)}, u32[]{:S(2)}) %collective-permute-start.2) | collective-permute-done | bytes 49184 | tf_op jit(solution)/shard_map/ppermute | solution.py:634
  12.9 0.5 %shard_map.29 = (f32[5,4,16,128]{3,2,1,0:T(8,128)S(1)}, f32[5,16,128]{2,1,0:T(8,128)S(1)}, f32[11,16,128]{2,1,0:T(8,128)S(1)}, f32[11,16,128]{2,1,0:T(8,128)S(1)}) custom-call(f32[6,16,128]{2,1,0:T(8,128)S(1)} %get-tuple-element.17.refs_0_, f32[6,16,128]{2,1,0:T(8,128)S(1)} %collective-permute-done.refs_1_, ...), custom_call_target="tpu_custom_call" | custom-call | tf_op jit(solution)/shard_map/pallas_call | solution.py:620
  13.5 0.1 collective-permute-start.3
  13.5 1.6 %collective-permute-start.4 = (f32[11,16,128]{2,1,0:T(8,128)S(1)}, f32[11,16,128]{2,1,0:T(8,128)S(1)}, u32[]{:S(2)}, u32[]{:S(2)}) collective-permute-start(f32[11,16,128]{2,1,0:T(8,128)S(1)} %get-tuple-element.24), channel_id=1, source_target_pairs={{0,3},{1,2},{2,1},{3,0},{4,7},{5,6},{6,5},{7,4},{8,11},{9,10},{10,... | collective-permute-start | bytes 270344 | tf_op jit(solution)/shard_map/ppermute | solution.py:648
  15.1 0.0 collective-permute-done.3.near_a
  15.1 2.8 %collective-permute-done.4.near_b = f32[11,16,128]{2,1,0:T(8,128)S(1)} collective-permute-done((f32[11,16,128]{2,1,0:T(8,128)S(1)}, f32[11,16,128]{2,1,0:T(8,128)S(1)}, u32[]{:S(2)}, u32[]{:S(2)}) %collective-permute-start.4) | collective-permute-done | bytes 90144 | tf_op jit(solution)/shard_map/ppermute | solution.py:648
  18.0 0.0 copy-start.1
  18.0 0.7 %copy-done.1 = s32[16]{0:T(128)S(1)} copy-done((s32[16]{0:T(128)S(1)}, s32[16]{0:T(128)}, u32[]{:S(2)}) %copy-start.1) | copy-done | bytes 88
  18.6 3.8 %shard_map.30 = (f32[5,16,128]{2,1,0:T(8,128)S(1)}, f32[5,16,128]{2,1,0:T(8,128)S(1)}, f32[5,16,128]{2,1,0:T(8,128)S(1)}, f32[5,16,128]{2,1,0:T(8,128)S(1)}) custom-call(s32[16]{0:T(128)S(1)} %copy-done.1, f32[5,4,16,128]{3,2,1,0:T(8,128)S(1)} %get-tuple-element.21.main, f32[5,16,128]{2,1,0:T(8,128)S(1)} %get-tuple-element.22.halo, ...), custom_call_target="tpu_custom_call" | custom-call | tf_op jit(solution)/shard_map/pallas_call | solution.py:620
  22.5 0.1 collective-permute-start.5
  22.5 1.3 %collective-permute-start.6 = (f32[5,16,128]{2,1,0:T(8,128)S(1)}, f32[5,16,128]{2,1,0:T(8,128)S(1)}, u32[]{:S(2)}, u32[]{:S(2)}) collective-permute-start(f32[5,16,128]{2,1,0:T(8,128)S(1)} %get-tuple-element.27), channel_id=1, source_target_pairs={{0,8},{4,12},{8,0},{12,4},{1,9},{5,13},{9,1},{13,5},{2,10},{6,14},... | collective-permute-start | bytes 122888 | tf_op jit(solution)/shard_map/ppermute | solution.py:634
  23.8 3.1 %collective-permute-start.7 = (f32[5,16,128]{2,1,0:T(8,128)S(1)}, f32[5,16,128]{2,1,0:T(8,128)S(1)}, u32[]{:S(2)}, u32[]{:S(2)}) collective-permute-start(f32[5,16,128]{2,1,0:T(8,128)S(1)} %get-tuple-element.28), channel_id=1, source_target_pairs={{0,12},{4,8},{8,4},{12,0},{1,13},{5,9},{9,5},{13,1},{2,14},{6,10},... | collective-permute-start | bytes 122888 | tf_op jit(solution)/shard_map/ppermute | solution.py:634
  26.9 0.0 collective-permute-done.5.refs_1_
  26.9 2.2 %collective-permute-done.6.refs_2_ = f32[5,16,128]{2,1,0:T(8,128)S(1)} collective-permute-done((f32[5,16,128]{2,1,0:T(8,128)S(1)}, f32[5,16,128]{2,1,0:T(8,128)S(1)}, u32[]{:S(2)}, u32[]{:S(2)}) %collective-permute-start.6) | collective-permute-done | bytes 40992 | tf_op jit(solution)/shard_map/ppermute | solution.py:634
  29.1 0.6 %collective-permute-done.7.refs_3_ = f32[5,16,128]{2,1,0:T(8,128)S(1)} collective-permute-done((f32[5,16,128]{2,1,0:T(8,128)S(1)}, f32[5,16,128]{2,1,0:T(8,128)S(1)}, u32[]{:S(2)}, u32[]{:S(2)}) %collective-permute-start.7) | collective-permute-done | bytes 40992 | tf_op jit(solution)/shard_map/ppermute | solution.py:634
  29.7 0.9 %shard_map.31 = f32[1,5,4,16,128]{4,3,2,1,0:T(8,128)} custom-call(f32[5,16,128]{2,1,0:T(8,128)S(1)} %get-tuple-element.25.refs_0_, f32[5,16,128]{2,1,0:T(8,128)S(1)} %collective-permute-done.5.refs_1_, f32[5,16,128]{2,1,0:T(8,128)S(1)} %collective-permute-done.6.refs_2_, f32[5,16,128]{2,1,0:T(8,128)S(1)} %collective-permute-done.7.refs_3_), custom_call_target="tpu_custom_call" | custom-call | tf_op jit(solution)/shard_map/pallas_call | solution.py:620
Async XLA Ops:
  0.0 0.9 %copy-start = (f32[1,5,4,16,128]{4,3,2,1,0:T(8,128)S(1)}, f32[1,5,4,16,128]{4,3,2,1,0:T(8,128)}, u32[]{:S(2)}) copy-start(f32[1,5,4,16,128]{4,3,2,1,0:T(8,128)} %flow.1) | copy-start | bytes 491524
  1.3 5.7 %collective-permute-start = (f32[6,16,128]{2,1,0:T(8,128)S(1)}, f32[6,16,128]{2,1,0:T(8,128)S(1)}, u32[]{:S(2)}, u32[]{:S(2)}) collective-permute-start(f32[6,16,128]{2,1,0:T(8,128)S(1)} %get-tuple-element.18), channel_id=1, source_target_pairs={{0,4},{4,0},{8,12},{12,8},{1,5},{5,1},{9,13},{13,9},{2,6},{6,2},{1... | collective-permute-start | bytes 147464 | tf_op jit(solution)/shard_map/ppermute | solution.py:634
  4.4 5.9 %collective-permute-start.1 = (f32[6,16,128]{2,1,0:T(8,128)S(1)}, f32[6,16,128]{2,1,0:T(8,128)S(1)}, u32[]{:S(2)}, u32[]{:S(2)}) collective-permute-start(f32[6,16,128]{2,1,0:T(8,128)S(1)} %get-tuple-element.19), channel_id=1, source_target_pairs={{0,8},{4,12},{8,0},{12,4},{1,9},{5,13},{9,1},{13,5},{2,10},{6,14},... | collective-permute-start | bytes 147464 | tf_op jit(solution)/shard_map/ppermute | solution.py:634
  7.0 5.9 %collective-permute-start.2 = (f32[6,16,128]{2,1,0:T(8,128)S(1)}, f32[6,16,128]{2,1,0:T(8,128)S(1)}, u32[]{:S(2)}, u32[]{:S(2)}) collective-permute-start(f32[6,16,128]{2,1,0:T(8,128)S(1)} %get-tuple-element.20), channel_id=1, source_target_pairs={{0,12},{4,8},{8,4},{12,0},{1,13},{5,9},{9,5},{13,1},{2,14},{6,10},... | collective-permute-start | bytes 147464 | tf_op jit(solution)/shard_map/ppermute | solution.py:634
  13.5 1.7 %collective-permute-start.3 = (f32[11,16,128]{2,1,0:T(8,128)S(1)}, f32[11,16,128]{2,1,0:T(8,128)S(1)}, u32[]{:S(2)}, u32[]{:S(2)}) collective-permute-start(f32[11,16,128]{2,1,0:T(8,128)S(1)} %get-tuple-element.23), channel_id=1, source_target_pairs={{0,1},{1,0},{2,3},{3,2},{4,5},{5,4},{6,7},{7,6},{8,9},{9,8},{10,11... | collective-permute-start | bytes 270344 | tf_op jit(solution)/shard_map/ppermute | solution.py:649
  13.5 4.4 %collective-permute-start.4 = (f32[11,16,128]{2,1,0:T(8,128)S(1)}, f32[11,16,128]{2,1,0:T(8,128)S(1)}, u32[]{:S(2)}, u32[]{:S(2)}) collective-permute-start(f32[11,16,128]{2,1,0:T(8,128)S(1)} %get-tuple-element.24), channel_id=1, source_target_pairs={{0,3},{1,2},{2,1},{3,0},{4,7},{5,6},{6,5},{7,4},{8,11},{9,10},{10,... | collective-permute-start | bytes 270344 | tf_op jit(solution)/shard_map/ppermute | solution.py:648
  18.0 0.7 %copy-start.1 = (s32[16]{0:T(128)S(1)}, s32[16]{0:T(128)}, u32[]{:S(2)}) copy-start(s32[16]{0:T(128)} %match.1) | copy-start | bytes 196
  22.5 4.5 %collective-permute-start.5 = (f32[5,16,128]{2,1,0:T(8,128)S(1)}, f32[5,16,128]{2,1,0:T(8,128)S(1)}, u32[]{:S(2)}, u32[]{:S(2)}) collective-permute-start(f32[5,16,128]{2,1,0:T(8,128)S(1)} %get-tuple-element.26), channel_id=1, source_target_pairs={{0,4},{4,0},{8,12},{12,8},{1,5},{5,1},{9,13},{13,9},{2,6},{6,2},{1... | collective-permute-start | bytes 122888 | tf_op jit(solution)/shard_map/ppermute | solution.py:634
  22.5 6.6 %collective-permute-start.6 = (f32[5,16,128]{2,1,0:T(8,128)S(1)}, f32[5,16,128]{2,1,0:T(8,128)S(1)}, u32[]{:S(2)}, u32[]{:S(2)}) collective-permute-start(f32[5,16,128]{2,1,0:T(8,128)S(1)} %get-tuple-element.27), channel_id=1, source_target_pairs={{0,8},{4,12},{8,0},{12,4},{1,9},{5,13},{9,1},{13,5},{2,10},{6,14},... | collective-permute-start | bytes 122888 | tf_op jit(solution)/shard_map/ppermute | solution.py:634
  23.8 5.8 %collective-permute-start.7 = (f32[5,16,128]{2,1,0:T(8,128)S(1)}, f32[5,16,128]{2,1,0:T(8,128)S(1)}, u32[]{:S(2)}, u32[]{:S(2)}) collective-permute-start(f32[5,16,128]{2,1,0:T(8,128)S(1)} %get-tuple-element.28), channel_id=1, source_target_pairs={{0,12},{4,8},{8,4},{12,0},{1,13},{5,9},{9,5},{13,1},{2,14},{6,10},... | collective-permute-start | bytes 122888 | tf_op jit(solution)/shard_map/ppermute | solution.py:634

commit v2 on v1

--- a/solution.py
+++ b/solution.py
@@ -238,6 +238,19 @@
     return math.pi / inst_count * parity * math.cos(angle) / math.sin(angle) + 0.5 * parity
 
 
+order = (2, 3, 1, 0)
+
+
+def in_order(items):
+    return [items[order.index(distance)] for distance in range(inst_count)]
+
+
+def unrolled(count, body, carry=None):
+    for number in range(count):
+        carry = body(number, carry)
+    return carry
+
+
 def lane_ids():
     return lax.broadcasted_iota(jnp.int32, tile, 1)
 
@@ -279,23 +292,28 @@
     return out
 
 
-def pack_kernel(flow, *messages):
+def pack_kernel(flow, *refs):
+    messages = in_order(refs)
     me = lax.axis_index("inst")
     lane = lane_ids()
     slot = jnp.bitwise_and(lane, 3)
     step = jnp.where(slot < 2, slot - 2, slot + chunk - 2)
-    for distance in range(inst_count):
-        part = jnp.bitwise_xor(me, distance)
-        index = mod_lanes(step + (chunk * part + lanes))
-        edge = None
-        for field in range(5):
-            tiles = [flow[0, field, layer] for layer in range(layers)]
+    parts = [jnp.bitwise_xor(me, distance) for distance in range(inst_count)]
+    index = [mod_lanes(step + (chunk * part + lanes)) for part in parts]
+
+    def one_field(field, edges):
+        tiles = [flow[0, field, layer] for layer in range(layers)]
+        edges = list(edges)
+        for distance, part in enumerate(parts):
             messages[distance][field] = pack_tile(tiles, part)
             for layer in range(layers):
-                got = pick_lanes(tiles[layer], index)
                 here = lane // 4 == field * 4 + layer
-                edge = got if edge is None else jnp.where(here, got, edge)
-        messages[distance][5] = edge
+                edges[distance] = jnp.where(here, pick_lanes(tiles[layer], index[distance]), edges[distance])
+        return tuple(edges)
+
+    edges = unrolled(5, one_field, (jnp.zeros(tile, jnp.float32),) * inst_count)
+    for distance in range(inst_count):
+        messages[distance][5] = edges[distance]
 
 
 def spread_tiles(received, field, me):
@@ -311,15 +329,15 @@
 
 
 def unpack_kernel(*refs):
-    received, (main, halo, near_a, near_b) = refs[:4], refs[4:]
+    received, (near_b, near_a, main, halo) = in_order(refs[:4]), refs[4:]
     me = lax.axis_index("inst")
     even = jnp.bitwise_and(lax.axis_index("space"), 1) == 0
     lane = lane_ids()
     owner = jnp.bitwise_and(lane // 4, 3)
     level = lane // 16 - 1
     inner = jnp.clip(level, 0, layers - 1) * 4 + jnp.bitwise_and(lane, 3)
-    up_edge = down_edge = None
-    for field in range(5):
+
+    def one_field(field, ends):
         tiles = spread_tiles(received, field, me)
         for layer in range(layers):
             main[field, layer] = tiles[layer]
@@ -332,11 +350,12 @@
             got = pick_lanes(received[distance][5], inner + 16 * field)
             edges = got if edges is None else jnp.where(owner == part, got, edges)
         halo[field] = edges
-        up = turn(edges, 16 * field - 16 * layers)
-        down = turn(edges, 16 * field - 16)
         here = lane // 16 == field
-        up_edge = up if up_edge is None else jnp.where(here, up, up_edge)
-        down_edge = down if down_edge is None else jnp.where(here, down, down_edge)
+        up = turn(edges, mod_lanes(16 * field - 16 * layers + lanes))
+        down = turn(edges, mod_lanes(16 * field - 16 + lanes))
+        return jnp.where(here, up, ends[0]), jnp.where(here, down, ends[1])
+
+    up_edge, down_edge = unrolled(5, one_field, (jnp.zeros(tile, jnp.float32),) * 2)
     near_a[10] = jnp.where(even, up_edge, down_edge)
     near_b[10] = jnp.where(even, down_edge, up_edge)
 
@@ -476,189 +495,260 @@
     return Cells([ref[place, number] for number in range(8)])
 
 
-def main_kernel(match, main, halo, near_a, near_b, *refs):
-    messages, (first, second, edge_faces) = refs[:4], refs[4:]
-    me = lax.axis_index("inst")
-    where_on = lax.axis_index("space")
-    parts_on = lax.axis_size("space")
-    even = jnp.bitwise_and(where_on, 1) == 0
-    at_low = where_on == 0
-    at_high = where_on == parts_on - 1
-    lag = inst_count // 4
-    lane = lane_ids()
+class Pitch:
+    def __init__(self, above, below, edge_faces):
+        self.above, self.below, self.edge_faces = above, below, edge_faces
+        self.lag = inst_count // 4
+        me = lax.axis_index("inst")
+        lane = lane_ids()
+        self.slot = jnp.bitwise_and(lane, 3)
+        self.band = lane // 16
+        column = jnp.bitwise_and(lane, chunk - 1)
+        self.is_first, self.is_last = column == 0, column == chunk - 1
+        self.seam = self.slot == jnp.where(me == 0, 1, jnp.where(me == inst_count - 1, 3, -1))
+        self.to_main = (lane // chunk) * 4 + jnp.where(self.is_first, 1, 3)
+        self.from_main = jnp.bitwise_and(lane // 4, 3) * chunk + jnp.where(self.slot == 1, 0, chunk - 1)
+
+    def mains(self, ref, places):
+        out = [None] * 8
+        for layer, place in places:
+            for number in range(8):
+                got = pick_lanes(ref[place, number], self.from_main)
+                out[number] = got if out[number] is None else jnp.where(self.band == layer + 1, got, out[number])
+        return Cells(out)
+
+    def edges(self, cells, mains):
+        slot = self.slot
+        lower = Cells([jnp.where(slot == 3, b, a) for a, b in zip(cells.parts, mains.parts)])
+        upper = []
+        for a, b in zip(cells.parts, mains.parts):
+            value = jnp.where(slot == 3, turn(a, 1), turn(a, -1))
+            value = jnp.where(slot == 1, b, value)
+            other = pick_rows(shift_slots(value, -self.lag), self.above)
+            upper.append(jnp.where(self.seam, other, value))
+        faces = roe_flux(lower, Cells(upper), 1)
+        lower_use = [jnp.where(self.seam, pick_rows(shift_slots(face, self.lag), self.below), face) for face in faces]
+        for part in range(5):
+            self.edge_faces[part] = jnp.where(slot == 1, lower_use[part], faces[part])
+        return faces, lower_use
+
+    def change(self, cells, layer):
+        faces = roe_flux(cells, cells.map(lambda part: turn(part, -1)), 1)
+        index = (layer + 1) * 16 + self.to_main
+        changes = []
+        for part in range(5):
+            edge = pick_lanes(self.edge_faces[part], index)
+            upper = jnp.where(self.is_last, edge, faces[part])
+            lower = jnp.where(self.is_first, edge, turn(faces[part], 1))
+            changes.append(upper - lower)
+        return changes
+
+
+def inner_kernel(match, main, halo, first, edge_first, part_main, part_edge, above, below, edge_faces):
     row = row_ids()
-    slot = jnp.bitwise_and(lane, 3)
-    owner_main = lane // chunk
-    column = jnp.bitwise_and(lane, chunk - 1)
-    is_first, is_last = column == 0, column == chunk - 1
-    seam_slot = jnp.where(me == 0, 1, jnp.where(me == inst_count - 1, 3, -1))
-    seam = slot == seam_slot
     below_of = jnp.zeros(tile, jnp.int32)
     above_of = jnp.zeros(tile, jnp.int32)
     for k in range(rows):
         value = match[k]
         below_of = jnp.where(row == k, value, below_of)
         above_of = jnp.where(row == value, k, above_of)
-
-    def edge_lane(layer):
-        return (layer + 1) * 16 + owner_main * 4 + jnp.where(is_first, 1, 3)
-
-    near = [[jnp.where(even, b[...], a[...]) for a, b in ((near_a.at[j], near_b.at[j]),)][0] for j in range(11)]
-    far = [[jnp.where(even, a[...], b[...]) for a, b in ((near_a.at[j], near_b.at[j]),)][0] for j in range(11)]
-    for layer in range(layers):
-        put(first, layer + 2, cells_of_draws([main[field, layer] for field in range(5)]))
-    for place in range(2):
-        draws = [jnp.where(at_low, main[field, 0], near[2 * field + place]) for field in range(5)]
-        put(first, place, cells_of_draws(draws))
-        draws = [jnp.where(at_high, main[field, layers - 1], far[2 * field + place]) for field in range(5)]
-        put(first, layers + 2 + place, cells_of_draws(draws))
-    band = lane // 16
-    edges = []
+    below[...], above[...] = below_of, above_of
+    pitch = Pitch(above_of, below_of, edge_faces)
+    slot = pitch.slot
+
+    def start(layer, carry):
+        put(first, layer, cells_of_draws([main[field, layer] for field in range(5)]))
+        return carry
+
+    unrolled(layers, start)
+    cells = cells_of_draws([halo[field] for field in range(5)])
+    for number, part in enumerate(cells.parts):
+        edge_first[number] = part
+    faces, lower_use = pitch.edges(cells, pitch.mains(first, [(layer, layer) for layer in range(layers)]))
+    span = span_change(cells)
+    state = cells.conserved()
+    for part in range(5):
+        along = jnp.where(slot == 1, faces[part] - turn(faces[part], 1), faces[part] - turn(lower_use[part], -1))
+        part_edge[part] = over_slots(state[part]) + 0.5 * (along + span[part])
+
+    def step(layer, below_faces):
+        cells = get(first, layer)
+        above_faces = roe_flux(cells, get(first, jnp.minimum(layer + 1, layers - 1)), 0)
+        span = span_change(cells)
+        along = pitch.change(cells, layer)
+        state = cells.conserved()
+        outs = []
+        for part in range(5):
+            upper = jnp.where(layer == layers - 1, 0.0, above_faces[part])
+            part_main[layer, part] = over_instances(state[part]) + 0.5 * (
+                (upper - below_faces[part]) + span[part] + along[part]
+            )
+            outs.append(upper)
+        return tuple(outs)
+
+    lax.fori_loop(0, layers, step, (jnp.zeros(tile, jnp.float32),) * 5)
+
+
+def outer_kernel(first, edge_first, part_main, part_edge, above, below, halo, near_b, near_a, *refs):
+    messages, (ends, second, change, edge_faces) = in_order(refs[:4]), refs[4:]
+    where_on = lax.axis_index("space")
+    even = jnp.bitwise_and(where_on, 1) == 0
+    at_low = where_on == 0
+    at_high = where_on == lax.axis_size("space") - 1
+    pitch = Pitch(above[...], below[...], edge_faces)
+    band = pitch.band
+
+    for number in range(8):
+        ends[2, number] = first[0, number]
+        ends[3, number] = first[layers - 1, number]
+
+    def bring(count, carry):
+        high = count // 2
+        place = jnp.bitwise_and(count, 1)
+        from_a = jnp.logical_xor(even, high == 0)
+        closed = jnp.logical_or(jnp.logical_and(at_low, high == 0), jnp.logical_and(at_high, high == 1))
+        draws = [jnp.where(from_a, near_a[2 * field + place], near_b[2 * field + place]) for field in range(5)]
+        cells = cells_of_draws(draws)
+        own = get(first, high * (layers - 1))
+        put(ends, count + 2 * high, Cells([jnp.where(closed, a, b) for a, b in zip(own.parts, cells.parts)]))
+        return carry
+
+    unrolled(4, bring)
+    low_tile = jnp.where(even, near_b[10], near_a[10])
+    high_tile = jnp.where(even, near_a[10], near_b[10])
+    outside = []
     for field in range(5):
         inside = halo[field]
-        low = jnp.where(at_low, turn(inside, -16), turn(near[10], -16 * field))
-        high = jnp.where(at_high, turn(inside, 16), turn(far[10], 16 * (layers + 1 - field)))
-        edges.append(jnp.where(band == 0, low, jnp.where(band == layers + 1, high, inside)))
-    edge_cells = cells_of_draws(edges)
-
-    def mains_at_slots(ref, start, low, high):
-        group = jnp.bitwise_and(lane // 4, 3) * chunk
-        index = group + jnp.where(slot == 1, 0, chunk - 1)
-        out = [None] * 8
-        for layer in range(low, high):
-            for number in range(8):
-                got = pick_lanes(ref[layer + start, number], index)
-                out[number] = got if out[number] is None else jnp.where(band == layer + 1, got, out[number])
-        return Cells(out)
-
-    def pitch_edges(cells, mains):
-        lower = Cells([jnp.where(slot == 3, b, a) for a, b in zip(cells.parts, mains.parts)])
-        upper = []
-        for a, b in zip(cells.parts, mains.parts):
-            value = jnp.where(slot == 3, turn(a, 1), turn(a, -1))
-            value = jnp.where(slot == 1, b, value)
-            other = pick_rows(shift_slots(value, -lag), above_of)
-            upper.append(jnp.where(seam, other, value))
-        faces = roe_flux(lower, Cells(upper), 1)
-        lower_use = [jnp.where(seam, pick_rows(shift_slots(face, lag), below_of), face) for face in faces]
-        return faces, lower_use
-
-    def pitch_change(cells, layer):
-        faces = roe_flux(cells, cells.map(lambda part: turn(part, -1)), 1)
-        index = edge_lane(layer)
-        changes = []
-        for part in range(5):
-            edge = pick_lanes(edge_faces[part], index)
-            upper = jnp.where(is_last, edge, faces[part])
-            lower = jnp.where(is_first, edge, turn(faces[part], 1))
-            changes.append(upper - lower)
-        return changes
-
-    def set_edges(faces, lower_use):
-        for part in range(5):
-            edge_faces[part] = jnp.where(slot == 1, lower_use[part], faces[part])
-
-    faces, lower_use = pitch_edges(edge_cells, mains_at_slots(first, 2, -1, layers + 1))
-    set_edges(faces, lower_use)
-    span = span_change(edge_cells)
+        low = jnp.where(at_low, turn(inside, -16), turn(low_tile, -16 * field))
+        high = jnp.where(at_high, turn(inside, 16), turn(high_tile, 16 * (layers + 1 - field)))
+        outside.append(jnp.where(band == 0, low, high))
+    within = jnp.logical_and(band > 0, band < layers + 1)
+    edge_cells = cells_of_draws(outside)
+    edge_cells = Cells([jnp.where(within, edge_first[number], edge_cells.parts[number]) for number in range(8)])
+    pitch.edges(edge_cells, pitch.mains(ends, [(-1, 1), (layers, 4)]))
     axial = roe_flux(edge_cells, edge_cells.map(lambda part: turn(part, -16)), 0)
     state = edge_cells.conserved()
     for part in range(5):
-        pitch = jnp.where(slot == 1, faces[part] - turn(faces[part], 1), faces[part] - turn(lower_use[part], -1))
-        change = pitch + span[part] + (axial[part] - turn(axial[part], 16))
-        state[part] = state[part] - pseudo_step * over_slots(state[part]) - (0.5 * pseudo_step) * change
+        value = part_edge[part] + 0.5 * (axial[part] - turn(axial[part], 16))
+        state[part] = state[part] - pseudo_step * value
     edge_second = cells_of_conserved(state)
 
-    def first_step(count, below):
-        cells = get(first, count + 1)
-        above = roe_flux(cells, get(first, count + 2), 0)
+    def end_step(high, carry):
+        base = 3 * high
+        cells = get(ends, base + 1)
+        lower = roe_flux(get(ends, base), cells, 0)
+        upper = roe_flux(cells, get(ends, base + 2), 0)
         span = span_change(cells)
-        pitch = pitch_change(cells, count - 1)
+        along = pitch.change(cells, high * (layers + 1) - 1)
         state = cells.conserved()
         for part in range(5):
-            change = (above[part] - below[part]) + span[part] + pitch[part]
-            state[part] = state[part] - pseudo_step * over_instances(state[part]) - (0.5 * pseudo_step) * change
-        put(second, count, cells_of_conserved(state))
-        return above
-
-    lax.fori_loop(0, layers + 2, first_step, roe_flux(get(first, 0), get(first, 1), 0))
-
+            value = over_instances(state[part]) + 0.5 * ((upper[part] - lower[part]) + span[part] + along[part])
+            state[part] = state[part] - pseudo_step * value
+            change[high, part] = jnp.where(high == 0, -upper[part], lower[part])
+        put(second, high * (layers + 1), cells_of_conserved(state))
+        return carry
+
+    unrolled(2, end_step)
+
+    def section(layer, carry):
+        state = get(first, layer).conserved()
+        for part in range(5):
+            more = jnp.where(layer == 0, change[0, part], jnp.where(layer == layers - 1, change[1, part], 0.0))
+            state[part] = state[part] - pseudo_step * (part_main[layer, part] + 0.5 * more)
+        put(second, layer + 1, cells_of_conserved(state))
+        return carry
+
+    unrolled(layers, section)
     for number in range(8):
         second[0, number] = jnp.where(at_low, second[1, number], second[0, number])
         second[layers + 1, number] = jnp.where(at_high, second[layers, number], second[layers + 1, number])
 
-    set_edges(*pitch_edges(edge_second, mains_at_slots(second, 1, 0, layers)))
-
-    def second_step(layer, below):
+    pitch.edges(edge_second, pitch.mains(second, [(layer, layer + 1) for layer in range(layers)]))
+
+    def second_step(layer, below_faces):
         cells = get(second, layer + 1)
-        above = roe_flux(cells, get(second, layer + 2), 0)
+        above_faces = roe_flux(cells, get(second, layer + 2), 0)
         span = span_change(cells)
-        pitch = pitch_change(cells, layer)
+        along = pitch.change(cells, layer)
         state = cells.conserved()
         for part in range(5):
-            change = (above[part] - below[part]) + span[part] + pitch[part]
-            first[layer, part] = over_instances(state[part]) + 0.5 * change
-        return above
-
-    lax.fori_loop(0, layers, second_step, roe_flux(get(second, 0), get(second, 1), 0))
-    for distance in range(inst_count):
-        part = jnp.bitwise_xor(me, distance)
-        for field in range(5):
-            messages[distance][field] = pack_tile([first[layer, field] for layer in range(layers)], part)
+            value = (above_faces[part] - below_faces[part]) + span[part] + along[part]
+            ends[layer, part] = over_instances(state[part]) + 0.5 * value
+        return tuple(above_faces)
+
+    lax.fori_loop(0, layers, second_step, tuple(roe_flux(get(second, 0), get(second, 1), 0)))
+    me = lax.axis_index("inst")
+
+    def send(field, carry):
+        tiles = [ends[layer, field] for layer in range(layers)]
+        for distance in range(inst_count):
+            messages[distance][field] = pack_tile(tiles, jnp.bitwise_xor(me, distance))
+        return carry
+
+    unrolled(5, send)
 
 
 def return_kernel(*refs):
-    received, out = refs[:4], refs[4]
+    received, out = in_order(refs[:4]), refs[4]
     me = lax.axis_index("inst")
-    for field in range(5):
+
+    def one_field(field, carry):
         for layer, values in enumerate(spread_tiles(received, field, me)):
             out[0, field, layer] = values
+        return carry
+
+    unrolled(5, one_field)
 
 
 def call(kernel, outs, operands, scratch=(), scalars=0):
-    shapes = [jax.ShapeDtypeStruct(shape, jnp.float32) for shape in outs]
+    shapes = [jax.ShapeDtypeStruct(shape, kind) for shape, kind in outs]
     return pl.pallas_call(
         kernel,
         out_shape=shapes,
         in_specs=[smem] * scalars + [vmem] * (len(operands) - scalars),
         out_specs=[vmem] * len(shapes),
-        scratch_shapes=scratch,
+        scratch_shapes=[pltpu.VMEM(shape, jnp.float32) for shape in scratch],
         compiler_params=pltpu.CompilerParams(vmem_limit_bytes=16 * 2**20),
     )(*operands)
 
 
+def floats(*shape):
+    return shape + tile, jnp.float32
+
+
 def swap_instances(messages):
-    got = [messages[0]] + [None] * (inst_count - 1)
-    for distance in (2, 3, 1):
+    got = []
+    for distance, message in zip(order, messages):
         route = [(i, i ^ distance) for i in range(inst_count)]
-        got[distance] = lax.ppermute(messages[distance], "inst", route)
+        got.append(lax.ppermute(message, "inst", route) if distance else message)
     return got
 
 
 def on_device_fast(flow_state, period_match):
     count = lax.axis_size("space")
-    messages = call(pack_kernel, [(6, rows, lanes)] * inst_count, [flow_state])
-    main, halo, near_a, near_b = call(
-        unpack_kernel,
-        [(5, layers, rows, lanes), (5, rows, lanes), (11, rows, lanes), (11, rows, lanes)],
-        swap_instances(messages),
+    messages = call(pack_kernel, [floats(6)] * inst_count, [flow_state])
+    near_b, near_a, main, halo = call(
+        unpack_kernel, [floats(11), floats(11), floats(5, layers), floats(5)], swap_instances(messages)
     )
     route_a = [(i, i ^ 1) for i in range(count)]
     route_b = [(i, ((i - 1) ^ 1) + 1) if 0 < i < count - 1 else (i, count - 1 - i) for i in range(count)]
     near_b = lax.ppermute(near_b, "space", route_b)
     near_a = lax.ppermute(near_a, "space", route_a)
-    results = call(
-        main_kernel,
-        [(5, rows, lanes)] * inst_count,
-        [period_match, main, halo, near_a, near_b],
-        [
-            pltpu.VMEM((layers + 4, 8, rows, lanes), jnp.float32),
-            pltpu.VMEM((layers + 2, 8, rows, lanes), jnp.float32),
-            pltpu.VMEM((5, rows, lanes), jnp.float32),
-        ],
+    integers = (tile, jnp.int32)
+    inner = call(
+        inner_kernel,
+        [floats(layers, 8), floats(8), floats(layers, 5), floats(5), integers, integers],
+        [period_match, main, halo],
+        [(5,) + tile],
         scalars=1,
     )
-    return call(return_kernel, [flow_state.shape], swap_instances(results))[0]
+    results = call(
+        outer_kernel,
+        [floats(5)] * inst_count,
+        [*inner, halo, near_b, near_a],
+        [(6, 8) + tile, (layers + 2, 8) + tile, (2, 5) + tile, (5,) + tile],
+    )
+    return call(return_kernel, [(flow_state.shape, jnp.float32)], swap_instances(results))[0]
 
 
 def solution(mesh):

time: 30.7 us -> 27.6 us (0.90)
  waiting for transfers between devices: 11.4 us -> 9.08 us
  starting transfers between devices: 11.8 us -> 10.9 us
    ppermute x1, waiting for transfers between devices: 2.8 us -> 0.81 us  [on_device_fast(): near_b = lax.ppermute(near_b, 'space', route_b)]
    ppermute x1, starting transfers between devices: 1.61 us -> 0.07 us  [on_device_fast(): near_b = lax.ppermute(near_b, 'space', route_b)]
    ppermute x1, starting transfers between devices: 0.07 us -> 1.59 us  [on_device_fast(): near_a = lax.ppermute(near_a, 'space', route_a)]
    ppermute x6, starting transfers between devices: 10.2 us -> 9.23 us  [swap_instances(): got.append(lax.ppermute(message, 'inst', route) if distance else message)]
    ppermute x6, waiting for transfers between devices: 8.64 us -> 8.27 us  [swap_instances(): got.append(lax.ppermute(message, 'inst', route) if distance else message)]
    pallas_call x4 -> x5, Pallas kernels: 5.71 us -> 5.84 us  [call(): pl.pallas_call(kernel, out_shape=shapes, in_specs=[smem] * scalars + [vme...]
  transfers between devices with their start and end apart: 8 -> 8, of which waited for: 5 -> 5; matrix products, arithmetic and copies ran while one was open for 0% -> 0% of each run, Pallas kernels for 0% -> 7%
where the time goes in v2:
time: 27.6 us; the launch traced here: 27.4 us
  starting transfers between devices  10.9 us (39%)
  waiting for transfers between devices  9.08 us (33%)
  Pallas kernels  5.84 us (21%)
  local copies, waits for them, and re-layouts  1.57 us (6%)
    ppermute x6, starting transfers between devices, swap_instances(): got.append(lax.ppermute(message, 'inst', route) if distance else message)  9.23 us
    ppermute x6, waiting for transfers between devices, swap_instances(): got.append(lax.ppermute(message, 'inst', route) if distance else message)  8.27 us
    pallas_call x5, Pallas kernels, call(): pl.pallas_call(kernel, out_shape=shapes, in_specs=[smem] * scalars + [vme...  5.84 us
    ppermute x1, starting transfers between devices, on_device_fast(): near_a = lax.ppermute(near_a, 'space', route_a)  1.59 us
    unnamed x4, local copies, waits for them, and re-layouts  1.57 us
    ppermute x1, waiting for transfers between devices, on_device_fast(): near_b = lax.ppermute(near_b, 'space', route_b)  0.81 us
  transfers between devices with their start and end apart: 8, of which 5 were waited for; matrix products, arithmetic and copies ran while one was open for 0% of the time, Pallas kernels for 7%

profile of v2, /device:TPU:0, one launch (start us, length us, event | category | flops | bytes accessed | tf_op | source)
XLA Modules:
  0.0 27.4 jit_solution(2288307649947546706)
XLA Ops:
  0.0 0.0 copy-start
  0.0 0.9 %copy-done = f32[1,5,4,16,128]{4,3,2,1,0:T(8,128)S(1)} copy-done((f32[1,5,4,16,128]{4,3,2,1,0:T(8,128)S(1)}, f32[1,5,4,16,128]{4,3,2,1,0:T(8,128)}, u32[]{:S(2)}) %copy-start) | copy-done | bytes 163864
  0.9 0.5 %shard_map.28 = (f32[6,16,128]{2,1,0:T(8,128)S(1)}, f32[6,16,128]{2,1,0:T(8,128)S(1)}, f32[6,16,128]{2,1,0:T(8,128)S(1)}, f32[6,16,128]{2,1,0:T(8,128)S(1)}) custom-call(f32[1,5,4,16,128]{4,3,2,1,0:T(8,128)S(1)} %copy-done), custom_call_target="tpu_custom_call" | custom-call | tf_op jit(solution)/shard_map/pallas_call | solution.py:705
  1.4 4.1 %collective-permute-start = (f32[6,16,128]{2,1,0:T(8,128)S(1)}, f32[6,16,128]{2,1,0:T(8,128)S(1)}, u32[]{:S(2)}, u32[]{:S(2)}) collective-permute-start(f32[6,16,128]{2,1,0:T(8,128)S(1)} %get-tuple-element.23), channel_id=1, source_target_pairs={{0,8},{4,12},{8,0},{12,4},{1,9},{5,13},{9,1},{13,5},{2,10},{6,14},... | collective-permute-start | bytes 147464 | tf_op jit(solution)/shard_map/ppermute | solution.py:723
  5.5 1.3 %collective-permute-start.1 = (f32[6,16,128]{2,1,0:T(8,128)S(1)}, f32[6,16,128]{2,1,0:T(8,128)S(1)}, u32[]{:S(2)}, u32[]{:S(2)}) collective-permute-start(f32[6,16,128]{2,1,0:T(8,128)S(1)} %get-tuple-element.24), channel_id=1, source_target_pairs={{0,12},{4,8},{8,4},{12,0},{1,13},{5,9},{9,5},{13,1},{2,14},{6,10},... | collective-permute-start | bytes 147464 | tf_op jit(solution)/shard_map/ppermute | solution.py:723
  6.9 0.2 collective-permute-start.2
  7.1 1.0 %collective-permute-done.refs_0_ = f32[6,16,128]{2,1,0:T(8,128)S(1)} collective-permute-done((f32[6,16,128]{2,1,0:T(8,128)S(1)}, f32[6,16,128]{2,1,0:T(8,128)S(1)}, u32[]{:S(2)}, u32[]{:S(2)}) %collective-permute-start) | collective-permute-done | bytes 49184 | tf_op jit(solution)/shard_map/ppermute | solution.py:723
  8.1 3.4 %collective-permute-done.1.refs_1_ = f32[6,16,128]{2,1,0:T(8,128)S(1)} collective-permute-done((f32[6,16,128]{2,1,0:T(8,128)S(1)}, f32[6,16,128]{2,1,0:T(8,128)S(1)}, u32[]{:S(2)}, u32[]{:S(2)}) %collective-permute-start.1) | collective-permute-done | bytes 49184 | tf_op jit(solution)/shard_map/ppermute | solution.py:723
  11.5 0.0 collective-permute-done.2.refs_2_
  11.5 0.5 %shard_map.29 = (f32[11,16,128]{2,1,0:T(8,128)S(1)}, f32[11,16,128]{2,1,0:T(8,128)S(1)}, f32[5,4,16,128]{3,2,1,0:T(8,128)S(1)}, f32[5,16,128]{2,1,0:T(8,128)S(1)}) custom-call(f32[6,16,128]{2,1,0:T(8,128)S(1)} %collective-permute-done.refs_0_, f32[6,16,128]{2,1,0:T(8,128)S(1)} %collective-permute-done.1.refs_1_, ...), custom_call_target="tpu_custom_call" | custom-call | tf_op jit(solution)/shard_map/pallas_call | solution.py:705
  12.0 0.1 collective-permute-start.3
  12.1 1.6 %collective-permute-start.4 = (f32[11,16,128]{2,1,0:T(8,128)S(1)}, f32[11,16,128]{2,1,0:T(8,128)S(1)}, u32[]{:S(2)}, u32[]{:S(2)}) collective-permute-start(f32[11,16,128]{2,1,0:T(8,128)S(1)} %get-tuple-element.36), channel_id=1, source_target_pairs={{0,1},{1,0},{2,3},{3,2},{4,5},{5,4},{6,7},{7,6},{8,9},{9,8},{10,11... | collective-permute-start | bytes 270344 | tf_op jit(solution)/shard_map/ppermute | solution.py:736
  13.7 0.0 copy-start.1
  13.7 0.7 %copy-done.1 = s32[16]{0:T(128)S(1)} copy-done((s32[16]{0:T(128)S(1)}, s32[16]{0:T(128)}, u32[]{:S(2)}) %copy-start.1) | copy-done | bytes 88
  14.4 1.8 %shard_map.30 = (f32[4,8,16,128]{3,2,1,0:T(8,128)S(1)}, f32[8,16,128]{2,1,0:T(8,128)S(1)}, f32[4,5,16,128]{3,2,1,0:T(8,128)S(1)}, f32[5,16,128]{2,1,0:T(8,128)S(...) custom-call(s32[16]{0:T(128)S(1)} %copy-done.1, f32[5,4,16,128]{3,2,1,0:T(8,128)S(1)} %get-tuple-element.27.main, ...), custom_call_target="tpu_custom_call" | custom-call | tf_op jit(solution)/shard_map/pallas_call | solution.py:705
  16.2 0.8 %collective-permute-done.3.near_b = f32[11,16,128]{2,1,0:T(8,128)S(1)} collective-permute-done((f32[11,16,128]{2,1,0:T(8,128)S(1)}, f32[11,16,128]{2,1,0:T(8,128)S(1)}, u32[]{:S(2)}, u32[]{:S(2)}) %collective-permute-start.3) | collective-permute-done | bytes 90144 | tf_op jit(solution)/shard_map/ppermute | solution.py:735
  17.0 0.0 collective-permute-done.4.near_a
  17.0 2.1 %shard_map.31 = (f32[5,16,128]{2,1,0:T(8,128)S(1)}, f32[5,16,128]{2,1,0:T(8,128)S(1)}, f32[5,16,128]{2,1,0:T(8,128)S(1)}, f32[5,16,128]{2,1,0:T(8,128)S(1)}) custom-call(f32[4,8,16,128]{3,2,1,0:T(8,128)S(1)} %get-tuple-element.29.first, f32[8,16,128]{2,1,0:T(8,128)S(1)} %get-tuple-element.30.edge_first, f32[4,5,16,128]{3,2,1,0:T(8,128)S(1)} %get-tuple-element.31.part_main, ...), custom_call_target="tpu_custom_call" | custom-call | tf_op jit(solution)/shard_map/pallas_call | solution.py:705
  19.1 1.6 %collective-permute-start.5 = (f32[5,16,128]{2,1,0:T(8,128)S(1)}, f32[5,16,128]{2,1,0:T(8,128)S(1)}, u32[]{:S(2)}, u32[]{:S(2)}) collective-permute-start(f32[5,16,128]{2,1,0:T(8,128)S(1)} %get-tuple-element.37), channel_id=1, source_target_pairs={{0,8},{4,12},{8,0},{12,4},{1,9},{5,13},{9,1},{13,5},{2,10},{6,14},... | collective-permute-start | bytes 122888 | tf_op jit(solution)/shard_map/ppermute | solution.py:723
  20.7 1.0 %collective-permute-start.6 = (f32[5,16,128]{2,1,0:T(8,128)S(1)}, f32[5,16,128]{2,1,0:T(8,128)S(1)}, u32[]{:S(2)}, u32[]{:S(2)}) collective-permute-start(f32[5,16,128]{2,1,0:T(8,128)S(1)} %get-tuple-element.38), channel_id=1, source_target_pairs={{0,12},{4,8},{8,4},{12,0},{1,13},{5,9},{9,5},{13,1},{2,14},{6,10},... | collective-permute-start | bytes 122888 | tf_op jit(solution)/shard_map/ppermute | solution.py:723
  21.7 0.9 %collective-permute-start.7 = (f32[5,16,128]{2,1,0:T(8,128)S(1)}, f32[5,16,128]{2,1,0:T(8,128)S(1)}, u32[]{:S(2)}, u32[]{:S(2)}) collective-permute-start(f32[5,16,128]{2,1,0:T(8,128)S(1)} %get-tuple-element.39), channel_id=1, source_target_pairs={{0,4},{4,0},{8,12},{12,8},{1,5},{5,1},{9,13},{13,9},{2,6},{6,2},{1... | collective-permute-start | bytes 122888 | tf_op jit(solution)/shard_map/ppermute | solution.py:723
  22.6 1.8 %collective-permute-done.5.refs_0_ = f32[5,16,128]{2,1,0:T(8,128)S(1)} collective-permute-done((f32[5,16,128]{2,1,0:T(8,128)S(1)}, f32[5,16,128]{2,1,0:T(8,128)S(1)}, u32[]{:S(2)}, u32[]{:S(2)}) %collective-permute-start.5) | collective-permute-done | bytes 40992 | tf_op jit(solution)/shard_map/ppermute | solution.py:723
  24.5 2.0 %collective-permute-done.6.refs_1_ = f32[5,16,128]{2,1,0:T(8,128)S(1)} collective-permute-done((f32[5,16,128]{2,1,0:T(8,128)S(1)}, f32[5,16,128]{2,1,0:T(8,128)S(1)}, u32[]{:S(2)}, u32[]{:S(2)}) %collective-permute-start.6) | collective-permute-done | bytes 40992 | tf_op jit(solution)/shard_map/ppermute | solution.py:723
  26.5 0.0 collective-permute-done.7.refs_2_
  26.5 0.9 %shard_map.32 = f32[1,5,4,16,128]{4,3,2,1,0:T(8,128)} custom-call(f32[5,16,128]{2,1,0:T(8,128)S(1)} %collective-permute-done.5.refs_0_, f32[5,16,128]{2,1,0:T(8,128)S(1)} %collective-permute-done.6.refs_1_, f32[5,16,128]{2,1,0:T(8,128)S(1)} %collective-permute-done.7.refs_2_, f32[5,16,128]{2,1,0:T(8,128)S(1)} %get-tuple-element.40.refs_3_), custom_call_target="tpu_custom_call" | custom-call | tf_op jit(solution)/shard_map/pallas_call | solution.py:705
Async XLA Ops:
  0.0 0.9 %copy-start = (f32[1,5,4,16,128]{4,3,2,1,0:T(8,128)S(1)}, f32[1,5,4,16,128]{4,3,2,1,0:T(8,128)}, u32[]{:S(2)}) copy-start(f32[1,5,4,16,128]{4,3,2,1,0:T(8,128)} %flow.1) | copy-start | bytes 491524
  1.4 6.7 %collective-permute-start = (f32[6,16,128]{2,1,0:T(8,128)S(1)}, f32[6,16,128]{2,1,0:T(8,128)S(1)}, u32[]{:S(2)}, u32[]{:S(2)}) collective-permute-start(f32[6,16,128]{2,1,0:T(8,128)S(1)} %get-tuple-element.23), channel_id=1, source_target_pairs={{0,8},{4,12},{8,0},{12,4},{1,9},{5,13},{9,1},{13,5},{2,10},{6,14},... | collective-permute-start | bytes 147464 | tf_op jit(solution)/shard_map/ppermute | solution.py:723
  5.5 6.0 %collective-permute-start.1 = (f32[6,16,128]{2,1,0:T(8,128)S(1)}, f32[6,16,128]{2,1,0:T(8,128)S(1)}, u32[]{:S(2)}, u32[]{:S(2)}) collective-permute-start(f32[6,16,128]{2,1,0:T(8,128)S(1)} %get-tuple-element.24), channel_id=1, source_target_pairs={{0,12},{4,8},{8,4},{12,0},{1,13},{5,9},{9,5},{13,1},{2,14},{6,10},... | collective-permute-start | bytes 147464 | tf_op jit(solution)/shard_map/ppermute | solution.py:723
  6.9 4.6 %collective-permute-start.2 = (f32[6,16,128]{2,1,0:T(8,128)S(1)}, f32[6,16,128]{2,1,0:T(8,128)S(1)}, u32[]{:S(2)}, u32[]{:S(2)}) collective-permute-start(f32[6,16,128]{2,1,0:T(8,128)S(1)} %get-tuple-element.25), channel_id=1, source_target_pairs={{0,4},{4,0},{8,12},{12,8},{1,5},{5,1},{9,13},{13,9},{2,6},{6,2},{1... | collective-permute-start | bytes 147464 | tf_op jit(solution)/shard_map/ppermute | solution.py:723
  12.0 4.9 %collective-permute-start.3 = (f32[11,16,128]{2,1,0:T(8,128)S(1)}, f32[11,16,128]{2,1,0:T(8,128)S(1)}, u32[]{:S(2)}, u32[]{:S(2)}) collective-permute-start(f32[11,16,128]{2,1,0:T(8,128)S(1)} %get-tuple-element.35), channel_id=1, source_target_pairs={{0,3},{1,2},{2,1},{3,0},{4,7},{5,6},{6,5},{7,4},{8,11},{9,10},{10,... | collective-permute-start | bytes 270344 | tf_op jit(solution)/shard_map/ppermute | solution.py:735
  12.1 4.9 %collective-permute-start.4 = (f32[11,16,128]{2,1,0:T(8,128)S(1)}, f32[11,16,128]{2,1,0:T(8,128)S(1)}, u32[]{:S(2)}, u32[]{:S(2)}) collective-permute-start(f32[11,16,128]{2,1,0:T(8,128)S(1)} %get-tuple-element.36), channel_id=1, source_target_pairs={{0,1},{1,0},{2,3},{3,2},{4,5},{5,4},{6,7},{7,6},{8,9},{9,8},{10,11... | collective-permute-start | bytes 270344 | tf_op jit(solution)/shard_map/ppermute | solution.py:736
  13.7 0.7 %copy-start.1 = (s32[16]{0:T(128)S(1)}, s32[16]{0:T(128)}, u32[]{:S(2)}) copy-start(s32[16]{0:T(128)} %match.1) | copy-start | bytes 196
  19.1 5.4 %collective-permute-start.5 = (f32[5,16,128]{2,1,0:T(8,128)S(1)}, f32[5,16,128]{2,1,0:T(8,128)S(1)}, u32[]{:S(2)}, u32[]{:S(2)}) collective-permute-start(f32[5,16,128]{2,1,0:T(8,128)S(1)} %get-tuple-element.37), channel_id=1, source_target_pairs={{0,8},{4,12},{8,0},{12,4},{1,9},{5,13},{9,1},{13,5},{2,10},{6,14},... | collective-permute-start | bytes 122888 | tf_op jit(solution)/shard_map/ppermute | solution.py:723
  20.7 5.8 %collective-permute-start.6 = (f32[5,16,128]{2,1,0:T(8,128)S(1)}, f32[5,16,128]{2,1,0:T(8,128)S(1)}, u32[]{:S(2)}, u32[]{:S(2)}) collective-permute-start(f32[5,16,128]{2,1,0:T(8,128)S(1)} %get-tuple-element.38), channel_id=1, source_target_pairs={{0,12},{4,8},{8,4},{12,0},{1,13},{5,9},{9,5},{13,1},{2,14},{6,10},... | collective-permute-start | bytes 122888 | tf_op jit(solution)/shard_map/ppermute | solution.py:723
  21.7 4.8 %collective-permute-start.7 = (f32[5,16,128]{2,1,0:T(8,128)S(1)}, f32[5,16,128]{2,1,0:T(8,128)S(1)}, u32[]{:S(2)}, u32[]{:S(2)}) collective-permute-start(f32[5,16,128]{2,1,0:T(8,128)S(1)} %get-tuple-element.39), channel_id=1, source_target_pairs={{0,4},{4,0},{8,12},{12,8},{1,5},{5,1},{9,13},{13,9},{2,6},{6,2},{1... | collective-permute-start | bytes 122888 | tf_op jit(solution)/shard_map/ppermute | solution.py:723

commit v3 on v2

--- a/solution.py
+++ b/solution.py
@@ -329,7 +329,7 @@
 
 
 def unpack_kernel(*refs):
-    received, (near_b, near_a, main, halo) = in_order(refs[:4]), refs[4:]
+    received, (near_b, near_a, main, halo) = in_order(refs[:4]), refs[5:]
     me = lax.axis_index("inst")
     even = jnp.bitwise_and(lax.axis_index("space"), 1) == 0
     lane = lane_ids()
@@ -544,7 +544,7 @@
         return changes
 
 
-def inner_kernel(match, main, halo, first, edge_first, part_main, part_edge, above, below, edge_faces):
+def index_kernel(match, behind, above, below):
     row = row_ids()
     below_of = jnp.zeros(tile, jnp.int32)
     above_of = jnp.zeros(tile, jnp.int32)
@@ -553,23 +553,28 @@
         below_of = jnp.where(row == k, value, below_of)
         above_of = jnp.where(row == value, k, above_of)
     below[...], above[...] = below_of, above_of
-    pitch = Pitch(above_of, below_of, edge_faces)
+
+
+def inner_kernel(above, below, main, halo, first, edge_first, part_first, part_edge, second, part_second, edge_faces):
+    pitch = Pitch(above[...], below[...], edge_faces)
     slot = pitch.slot
-
-    def start(layer, carry):
+    middle = range(1, layers - 1)
+    for layer in range(layers):
         put(first, layer, cells_of_draws([main[field, layer] for field in range(5)]))
-        return carry
-
-    unrolled(layers, start)
     cells = cells_of_draws([halo[field] for field in range(5)])
     for number, part in enumerate(cells.parts):
         edge_first[number] = part
     faces, lower_use = pitch.edges(cells, pitch.mains(first, [(layer, layer) for layer in range(layers)]))
     span = span_change(cells)
+    axial = roe_flux(cells, cells.map(lambda part: turn(part, -16)), 0)
     state = cells.conserved()
     for part in range(5):
         along = jnp.where(slot == 1, faces[part] - turn(faces[part], 1), faces[part] - turn(lower_use[part], -1))
-        part_edge[part] = over_slots(state[part]) + 0.5 * (along + span[part])
+        value = over_slots(state[part]) + 0.5 * (along + span[part])
+        part_edge[part] = value
+        value = value + 0.5 * (axial[part] - turn(axial[part], 16))
+        state[part] = state[part] - pseudo_step * value
+    edge_second = cells_of_conserved(state)
 
     def step(layer, below_faces):
         cells = get(first, layer)
@@ -580,7 +585,7 @@
         outs = []
         for part in range(5):
             upper = jnp.where(layer == layers - 1, 0.0, above_faces[part])
-            part_main[layer, part] = over_instances(state[part]) + 0.5 * (
+            part_first[layer, part] = over_instances(state[part]) + 0.5 * (
                 (upper - below_faces[part]) + span[part] + along[part]
             )
             outs.append(upper)
@@ -588,8 +593,32 @@
 
     lax.fori_loop(0, layers, step, (jnp.zeros(tile, jnp.float32),) * 5)
 
-
-def outer_kernel(first, edge_first, part_main, part_edge, above, below, halo, near_b, near_a, *refs):
+    for place, layer in enumerate(middle):
+        state = get(first, layer).conserved()
+        state = [value - pseudo_step * part_first[layer, part] for part, value in enumerate(state)]
+        put(second, place, cells_of_conserved(state))
+    pitch.edges(edge_second, pitch.mains(second, [(layer, place) for place, layer in enumerate(middle)]))
+    between = roe_flux(get(second, 0), get(second, 1), 0)
+    for part in range(5):
+        part_second[0, part] = between[part]
+        part_second[1, part] = -between[part]
+
+    def second_step(place, carry):
+        cells = get(second, place)
+        span = span_change(cells)
+        along = pitch.change(cells, place + 1)
+        state = cells.conserved()
+        for part in range(5):
+            value = part_second[place, part] + span[part] + along[part]
+            part_second[place, part] = over_instances(state[part]) + 0.5 * value
+        return carry
+
+    lax.fori_loop(0, layers - 2, second_step, 0)
+
+
+def outer_kernel(
+    first, edge_first, part_first, part_edge, second_middle, part_second, above, below, halo, near_b, near_a, *refs
+):
     messages, (ends, second, change, edge_faces) = in_order(refs[:4]), refs[4:]
     where_on = lax.axis_index("space")
     even = jnp.bitwise_and(where_on, 1) == 0
@@ -601,19 +630,18 @@
     for number in range(8):
         ends[2, number] = first[0, number]
         ends[3, number] = first[layers - 1, number]
-
-    def bring(count, carry):
-        high = count // 2
-        place = jnp.bitwise_and(count, 1)
-        from_a = jnp.logical_xor(even, high == 0)
-        closed = jnp.logical_or(jnp.logical_and(at_low, high == 0), jnp.logical_and(at_high, high == 1))
-        draws = [jnp.where(from_a, near_a[2 * field + place], near_b[2 * field + place]) for field in range(5)]
-        cells = cells_of_draws(draws)
+        second[2, number] = second_middle[0, number]
+        second[layers - 1, number] = second_middle[layers - 3, number]
+
+    for high in range(2):
         own = get(first, high * (layers - 1))
-        put(ends, count + 2 * high, Cells([jnp.where(closed, a, b) for a, b in zip(own.parts, cells.parts)]))
-        return carry
-
-    unrolled(4, bring)
+        closed, from_a = (at_high, even) if high else (at_low, jnp.logical_not(even))
+        for place in range(2):
+            draws = [jnp.where(from_a, near_a[2 * field + place], near_b[2 * field + place]) for field in range(5)]
+            cells = cells_of_draws(draws)
+            pairs = zip(own.parts, cells.parts)
+            put(ends, place + 4 * high, Cells([jnp.where(closed, a, b) for a, b in pairs]))
+
     low_tile = jnp.where(even, near_b[10], near_a[10])
     high_tile = jnp.where(even, near_a[10], near_b[10])
     outside = []
@@ -633,59 +661,55 @@
         state[part] = state[part] - pseudo_step * value
     edge_second = cells_of_conserved(state)
 
-    def end_step(high, carry):
+    def end_values(ref, high, layer):
         base = 3 * high
-        cells = get(ends, base + 1)
-        lower = roe_flux(get(ends, base), cells, 0)
-        upper = roe_flux(cells, get(ends, base + 2), 0)
+        cells = get(ref, base + 1)
+        lower = roe_flux(get(ref, base), cells, 0)
+        upper = roe_flux(cells, get(ref, base + 2), 0)
         span = span_change(cells)
-        along = pitch.change(cells, high * (layers + 1) - 1)
+        along = pitch.change(cells, layer)
         state = cells.conserved()
+        values = []
         for part in range(5):
-            value = over_instances(state[part]) + 0.5 * ((upper[part] - lower[part]) + span[part] + along[part])
-            state[part] = state[part] - pseudo_step * value
+            value = (upper[part] - lower[part]) + span[part] + along[part]
+            values.append(over_instances(state[part]) + 0.5 * value)
             change[high, part] = jnp.where(high == 0, -upper[part], lower[part])
+        return state, values
+
+    def first_step(high, carry):
+        state, values = end_values(ends, high, high * (layers + 1) - 1)
+        state = [a - pseudo_step * b for a, b in zip(state, values)]
         put(second, high * (layers + 1), cells_of_conserved(state))
         return carry
 
-    unrolled(2, end_step)
-
-    def section(layer, carry):
+    unrolled(2, first_step)
+
+    for high in range(2):
+        layer = high * (layers - 1)
         state = get(first, layer).conserved()
         for part in range(5):
-            more = jnp.where(layer == 0, change[0, part], jnp.where(layer == layers - 1, change[1, part], 0.0))
-            state[part] = state[part] - pseudo_step * (part_main[layer, part] + 0.5 * more)
+            state[part] = state[part] - pseudo_step * (part_first[layer, part] + 0.5 * change[high, part])
         put(second, layer + 1, cells_of_conserved(state))
-        return carry
-
-    unrolled(layers, section)
     for number in range(8):
         second[0, number] = jnp.where(at_low, second[1, number], second[0, number])
         second[layers + 1, number] = jnp.where(at_high, second[layers, number], second[layers + 1, number])
 
-    pitch.edges(edge_second, pitch.mains(second, [(layer, layer + 1) for layer in range(layers)]))
-
-    def second_step(layer, below_faces):
-        cells = get(second, layer + 1)
-        above_faces = roe_flux(cells, get(second, layer + 2), 0)
-        span = span_change(cells)
-        along = pitch.change(cells, layer)
-        state = cells.conserved()
+    pitch.edges(edge_second, pitch.mains(second, [(0, 1), (layers - 1, layers)]))
+
+    def second_step(high, carry):
+        _, values = end_values(second, high, high * (layers - 1))
         for part in range(5):
-            value = (above_faces[part] - below_faces[part]) + span[part] + along[part]
-            ends[layer, part] = over_instances(state[part]) + 0.5 * value
-        return tuple(above_faces)
-
-    lax.fori_loop(0, layers, second_step, tuple(roe_flux(get(second, 0), get(second, 1), 0)))
+            ends[high, part] = values[part]
+        return carry
+
+    lax.fori_loop(0, 2, second_step, 0)
+
     me = lax.axis_index("inst")
-
-    def send(field, carry):
-        tiles = [ends[layer, field] for layer in range(layers)]
+    for field in range(5):
+        tiles = [ends[0, field], part_second[0, field] + 0.5 * change[0, field]]
+        tiles += [part_second[1, field] + 0.5 * change[1, field], ends[1, field]]
         for distance in range(inst_count):
             messages[distance][field] = pack_tile(tiles, jnp.bitwise_xor(me, distance))
-        return carry
-
-    unrolled(5, send)
 
 
 def return_kernel(*refs):
@@ -727,25 +751,29 @@
 def on_device_fast(flow_state, period_match):
     count = lax.axis_size("space")
     messages = call(pack_kernel, [floats(6)] * inst_count, [flow_state])
+    integers = (tile, jnp.int32)
+    above, below = call(index_kernel, [integers, integers], [period_match, messages[-1]], scalars=1)
     near_b, near_a, main, halo = call(
-        unpack_kernel, [floats(11), floats(11), floats(5, layers), floats(5)], swap_instances(messages)
+        unpack_kernel, [floats(11), floats(11), floats(5, layers), floats(5)], [*swap_instances(messages), above]
     )
     route_a = [(i, i ^ 1) for i in range(count)]
-    route_b = [(i, ((i - 1) ^ 1) + 1) if 0 < i < count - 1 else (i, count - 1 - i) for i in range(count)]
-    near_b = lax.ppermute(near_b, "space", route_b)
+    route_b = []
+    for n in range(inst_count):
+        for i in range(count):
+            far = (n, ((i - 1) ^ 1) + 1) if 0 < i < count - 1 else (n ^ 1, i)
+            route_b.append((n * count + i, far[0] * count + far[1]))
+    near_b = lax.ppermute(near_b, ("inst", "space"), route_b)
     near_a = lax.ppermute(near_a, "space", route_a)
-    integers = (tile, jnp.int32)
     inner = call(
         inner_kernel,
-        [floats(layers, 8), floats(8), floats(layers, 5), floats(5), integers, integers],
-        [period_match, main, halo],
+        [floats(layers, 8), floats(8), floats(layers, 5), floats(5), floats(layers - 2, 8), floats(layers - 2, 5)],
+        [above, below, main, halo],
         [(5,) + tile],
-        scalars=1,
     )
     results = call(
         outer_kernel,
         [floats(5)] * inst_count,
-        [*inner, halo, near_b, near_a],
+        [*inner, above, below, halo, near_b, near_a],
         [(6, 8) + tile, (layers + 2, 8) + tile, (2, 5) + tile, (5,) + tile],
     )
     return call(return_kernel, [(flow_state.shape, jnp.float32)], swap_instances(results))[0]

time: 27.6 us -> 26.8 us (0.971)
  waiting for transfers between devices: 9.08 us -> 8.15 us
  Pallas kernels: 5.84 us -> 6.24 us
    ppermute x6, waiting for transfers between devices: 8.27 us -> 7.28 us  [swap_instances(): got.append(lax.ppermute(message, 'inst', route) if distance else message)]
    pallas_call x5 -> x6, Pallas kernels: 5.84 us -> 6.24 us  [call(): pl.pallas_call(kernel, out_shape=shapes, in_specs=[smem] * scalars + [vme...]
  transfers between devices with their start and end apart: 8 -> 8, of which waited for: 5 -> 4; matrix products, arithmetic and copies ran while one was open for 0% -> 0% of each run, Pallas kernels for 7% -> 10%
where the time goes in v3:
time: 26.8 us; the launch traced here: 26.7 us
  starting transfers between devices  10.9 us (41%)
  waiting for transfers between devices  8.15 us (30%)
  Pallas kernels  6.24 us (23%)
  local copies, waits for them, and re-layouts  1.34 us (5%)
    ppermute x6, starting transfers between devices, swap_instances(): got.append(lax.ppermute(message, 'inst', route) if distance else message)  9.23 us
    ppermute x6, waiting for transfers between devices, swap_instances(): got.append(lax.ppermute(message, 'inst', route) if distance else message)  7.28 us
    pallas_call x6, Pallas kernels, call(): pl.pallas_call(kernel, out_shape=shapes, in_specs=[smem] * scalars + [vme...  6.24 us
    ppermute x1, starting transfers between devices, on_device_fast(): near_a = lax.ppermute(near_a, 'space', route_a)  1.38 us
    unnamed x4, local copies, waits for them, and re-layouts  1.34 us
    ppermute x1, waiting for transfers between devices, on_device_fast(): near_b = lax.ppermute(near_b, ('inst', 'space'), route_b)  0.86 us
  transfers between devices with their start and end apart: 8, of which 4 were waited for; matrix products, arithmetic and copies ran while one was open for 0% of the time, Pallas kernels for 10%

profile of v3, /device:TPU:0, one launch (start us, length us, event | category | flops | bytes accessed | tf_op | source)
XLA Modules:
  0.0 26.7 jit_solution(10221392638130507115)
XLA Ops:
  0.0 0.0 copy-start
  0.0 0.9 %copy-done = f32[1,5,4,16,128]{4,3,2,1,0:T(8,128)S(1)} copy-done((f32[1,5,4,16,128]{4,3,2,1,0:T(8,128)S(1)}, f32[1,5,4,16,128]{4,3,2,1,0:T(8,128)}, u32[]{:S(2)}) %copy-start) | copy-done | bytes 163864
  0.9 0.5 %shard_map.28 = (f32[6,16,128]{2,1,0:T(8,128)S(1)}, f32[6,16,128]{2,1,0:T(8,128)S(1)}, f32[6,16,128]{2,1,0:T(8,128)S(1)}, f32[6,16,128]{2,1,0:T(8,128)S(1)}) custom-call(f32[1,5,4,16,128]{4,3,2,1,0:T(8,128)S(1)} %copy-done), custom_call_target="tpu_custom_call" | custom-call | tf_op jit(solution)/shard_map/pallas_call | solution.py:729
  1.4 4.1 %collective-permute-start = (f32[6,16,128]{2,1,0:T(8,128)S(1)}, f32[6,16,128]{2,1,0:T(8,128)S(1)}, u32[]{:S(2)}, u32[]{:S(2)}) collective-permute-start(f32[6,16,128]{2,1,0:T(8,128)S(1)} %get-tuple-element.28), channel_id=1, source_target_pairs={{0,8},{4,12},{8,0},{12,4},{1,9},{5,13},{9,1},{13,5},{2,10},{6,14},... | collective-permute-start | bytes 147464 | tf_op jit(solution)/shard_map/ppermute | solution.py:747
  5.5 1.3 %collective-permute-start.1 = (f32[6,16,128]{2,1,0:T(8,128)S(1)}, f32[6,16,128]{2,1,0:T(8,128)S(1)}, u32[]{:S(2)}, u32[]{:S(2)}) collective-permute-start(f32[6,16,128]{2,1,0:T(8,128)S(1)} %get-tuple-element.29), channel_id=1, source_target_pairs={{0,12},{4,8},{8,4},{12,0},{1,13},{5,9},{9,5},{13,1},{2,14},{6,10},... | collective-permute-start | bytes 147464 | tf_op jit(solution)/shard_map/ppermute | solution.py:747
  6.9 0.0 copy-start.1
  6.9 0.2 collective-permute-start.2
  7.1 0.4 %copy-done.1 = s32[16]{0:T(128)S(1)} copy-done((s32[16]{0:T(128)S(1)}, s32[16]{0:T(128)}, u32[]{:S(2)}) %copy-start.1) | copy-done | bytes 88
  7.5 0.6 %shard_map.29 = (s32[16,128]{1,0:T(8,128)S(1)}, s32[16,128]{1,0:T(8,128)S(1)}) custom-call(s32[16]{0:T(128)S(1)} %copy-done.1, f32[6,16,128]{2,1,0:T(8,128)S(1)} %get-tuple-element.25.behind.refs_3_), custom_call_target="tpu_custom_call" | custom-call | tf_op jit(solution)/shard_map/pallas_call | solution.py:729
  8.1 0.0 collective-permute-done.refs_0_
  8.1 3.4 %collective-permute-done.1.refs_1_ = f32[6,16,128]{2,1,0:T(8,128)S(1)} collective-permute-done((f32[6,16,128]{2,1,0:T(8,128)S(1)}, f32[6,16,128]{2,1,0:T(8,128)S(1)}, u32[]{:S(2)}, u32[]{:S(2)}) %collective-permute-start.1) | collective-permute-done | bytes 49184 | tf_op jit(solution)/shard_map/ppermute | solution.py:747
  11.5 0.0 collective-permute-done.2.refs_2_
  11.5 0.5 %shard_map.30 = (f32[11,16,128]{2,1,0:T(8,128)S(1)}, f32[11,16,128]{2,1,0:T(8,128)S(1)}, f32[5,4,16,128]{3,2,1,0:T(8,128)S(1)}, f32[5,16,128]{2,1,0:T(8,128)S(1)}) custom-call(f32[6,16,128]{2,1,0:T(8,128)S(1)} %collective-permute-done.refs_0_, f32[6,16,128]{2,1,0:T(8,128)S(1)} %collective-permute-done.1.refs_1_, ...), custom_call_target="tpu_custom_call" | custom-call | tf_op jit(solution)/shard_map/pallas_call | solution.py:729
  12.0 0.3 %collective-permute-start.3 = (f32[11,16,128]{2,1,0:T(8,128)S(1)}, f32[11,16,128]{2,1,0:T(8,128)S(1)}, u32[]{:S(2)}, u32[]{:S(2)}) collective-permute-start(f32[11,16,128]{2,1,0:T(8,128)S(1)} %get-tuple-element.39), channel_id=1, source_target_pairs={{0,4},{1,2},{2,1},{3,7},{4,0},{5,6},{6,5},{7,3},{8,12},{9,10},{10,... | collective-permute-start | bytes 270344 | tf_op jit(solution)/shard_map/ppermute | solution.py:765
  12.3 1.4 %collective-permute-start.4 = (f32[11,16,128]{2,1,0:T(8,128)S(1)}, f32[11,16,128]{2,1,0:T(8,128)S(1)}, u32[]{:S(2)}, u32[]{:S(2)}) collective-permute-start(f32[11,16,128]{2,1,0:T(8,128)S(1)} %get-tuple-element.40), channel_id=1, source_target_pairs={{0,1},{1,0},{2,3},{3,2},{4,5},{5,4},{6,7},{7,6},{8,9},{9,8},{10,11... | collective-permute-start | bytes 270344 | tf_op jit(solution)/shard_map/ppermute | solution.py:766
  13.7 2.1 %shard_map.31 = (f32[4,8,16,128]{3,2,1,0:T(8,128)S(1)}, f32[8,16,128]{2,1,0:T(8,128)S(1)}, f32[4,5,16,128]{3,2,1,0:T(8,128)S(1)}, f32[5,16,128]{2,1,0:T(8,128)S(...) custom-call(s32[16,128]{1,0:T(8,128)S(1)} %get-tuple-element.26.refs_4_.above, ...), custom_call_target="tpu_custom_call" | custom-call | tf_op jit(solution)/shard_map/pallas_call | solution.py:729
  15.8 0.9 %collective-permute-done.3.near_b = f32[11,16,128]{2,1,0:T(8,128)S(1)} collective-permute-done((f32[11,16,128]{2,1,0:T(8,128)S(1)}, f32[11,16,128]{2,1,0:T(8,128)S(1)}, u32[]{:S(2)}, u32[]{:S(2)}) %collective-permute-start.3) | collective-permute-done | bytes 90144 | tf_op jit(solution)/shard_map/ppermute | solution.py:765
  16.6 0.0 collective-permute-done.4.near_a
  16.6 1.7 %shard_map.32 = (f32[5,16,128]{2,1,0:T(8,128)S(1)}, f32[5,16,128]{2,1,0:T(8,128)S(1)}, f32[5,16,128]{2,1,0:T(8,128)S(1)}, f32[5,16,128]{2,1,0:T(8,128)S(1)}) custom-call(f32[4,8,16,128]{3,2,1,0:T(8,128)S(1)} %get-tuple-element.33.first, f32[8,16,128]{2,1,0:T(8,128)S(1)} %get-tuple-element.34.edge_first, f32[4,5,16,128]{3,2,1,0:T(8,128)S(1)} %get-tuple-element.35.part_first, ...), custom_call_target="tpu_custom_call" | custom-call | tf_op jit(solution)/shard_map/pallas_call | solution.py:729
  18.3 1.6 %collective-permute-start.5 = (f32[5,16,128]{2,1,0:T(8,128)S(1)}, f32[5,16,128]{2,1,0:T(8,128)S(1)}, u32[]{:S(2)}, u32[]{:S(2)}) collective-permute-start(f32[5,16,128]{2,1,0:T(8,128)S(1)} %get-tuple-element.41), channel_id=1, source_target_pairs={{0,8},{4,12},{8,0},{12,4},{1,9},{5,13},{9,1},{13,5},{2,10},{6,14},... | collective-permute-start | bytes 122888 | tf_op jit(solution)/shard_map/ppermute | solution.py:747
  20.0 1.0 %collective-permute-start.6 = (f32[5,16,128]{2,1,0:T(8,128)S(1)}, f32[5,16,128]{2,1,0:T(8,128)S(1)}, u32[]{:S(2)}, u32[]{:S(2)}) collective-permute-start(f32[5,16,128]{2,1,0:T(8,128)S(1)} %get-tuple-element.42), channel_id=1, source_target_pairs={{0,12},{4,8},{8,4},{12,0},{1,13},{5,9},{9,5},{13,1},{2,14},{6,10},... | collective-permute-start | bytes 122888 | tf_op jit(solution)/shard_map/ppermute | solution.py:747
  21.0 0.9 %collective-permute-start.7 = (f32[5,16,128]{2,1,0:T(8,128)S(1)}, f32[5,16,128]{2,1,0:T(8,128)S(1)}, u32[]{:S(2)}, u32[]{:S(2)}) collective-permute-start(f32[5,16,128]{2,1,0:T(8,128)S(1)} %get-tuple-element.43), channel_id=1, source_target_pairs={{0,4},{4,0},{8,12},{12,8},{1,5},{5,1},{9,13},{13,9},{2,6},{6,2},{1... | collective-permute-start | bytes 122888 | tf_op jit(solution)/shard_map/ppermute | solution.py:747
  21.9 2.4 %collective-permute-done.5.refs_0_ = f32[5,16,128]{2,1,0:T(8,128)S(1)} collective-permute-done((f32[5,16,128]{2,1,0:T(8,128)S(1)}, f32[5,16,128]{2,1,0:T(8,128)S(1)}, u32[]{:S(2)}, u32[]{:S(2)}) %collective-permute-start.5) | collective-permute-done | bytes 40992 | tf_op jit(solution)/shard_map/ppermute | solution.py:747
  24.3 1.5 %collective-permute-done.6.refs_1_ = f32[5,16,128]{2,1,0:T(8,128)S(1)} collective-permute-done((f32[5,16,128]{2,1,0:T(8,128)S(1)}, f32[5,16,128]{2,1,0:T(8,128)S(1)}, u32[]{:S(2)}, u32[]{:S(2)}) %collective-permute-start.6) | collective-permute-done | bytes 40992 | tf_op jit(solution)/shard_map/ppermute | solution.py:747
  25.8 0.0 collective-permute-done.7.refs_2_
  25.8 0.9 %shard_map.33 = f32[1,5,4,16,128]{4,3,2,1,0:T(8,128)} custom-call(f32[5,16,128]{2,1,0:T(8,128)S(1)} %collective-permute-done.5.refs_0_, f32[5,16,128]{2,1,0:T(8,128)S(1)} %collective-permute-done.6.refs_1_, f32[5,16,128]{2,1,0:T(8,128)S(1)} %collective-permute-done.7.refs_2_, f32[5,16,128]{2,1,0:T(8,128)S(1)} %get-tuple-element.44.refs_3_), custom_call_target="tpu_custom_call" | custom-call | tf_op jit(solution)/shard_map/pallas_call | solution.py:729
Async XLA Ops:
  0.0 0.9 %copy-start = (f32[1,5,4,16,128]{4,3,2,1,0:T(8,128)S(1)}, f32[1,5,4,16,128]{4,3,2,1,0:T(8,128)}, u32[]{:S(2)}) copy-start(f32[1,5,4,16,128]{4,3,2,1,0:T(8,128)} %flow.1) | copy-start | bytes 491524
  1.4 6.7 %collective-permute-start = (f32[6,16,128]{2,1,0:T(8,128)S(1)}, f32[6,16,128]{2,1,0:T(8,128)S(1)}, u32[]{:S(2)}, u32[]{:S(2)}) collective-permute-start(f32[6,16,128]{2,1,0:T(8,128)S(1)} %get-tuple-element.28), channel_id=1, source_target_pairs={{0,8},{4,12},{8,0},{12,4},{1,9},{5,13},{9,1},{13,5},{2,10},{6,14},... | collective-permute-start | bytes 147464 | tf_op jit(solution)/shard_map/ppermute | solution.py:747
  5.5 6.0 %collective-permute-start.1 = (f32[6,16,128]{2,1,0:T(8,128)S(1)}, f32[6,16,128]{2,1,0:T(8,128)S(1)}, u32[]{:S(2)}, u32[]{:S(2)}) collective-permute-start(f32[6,16,128]{2,1,0:T(8,128)S(1)} %get-tuple-element.29), channel_id=1, source_target_pairs={{0,12},{4,8},{8,4},{12,0},{1,13},{5,9},{9,5},{13,1},{2,14},{6,10},... | collective-permute-start | bytes 147464 | tf_op jit(solution)/shard_map/ppermute | solution.py:747
  6.9 0.7 %copy-start.1 = (s32[16]{0:T(128)S(1)}, s32[16]{0:T(128)}, u32[]{:S(2)}) copy-start(s32[16]{0:T(128)} %match.1) | copy-start | bytes 196
  6.9 4.6 %collective-permute-start.2 = (f32[6,16,128]{2,1,0:T(8,128)S(1)}, f32[6,16,128]{2,1,0:T(8,128)S(1)}, u32[]{:S(2)}, u32[]{:S(2)}) collective-permute-start(f32[6,16,128]{2,1,0:T(8,128)S(1)} %get-tuple-element.30), channel_id=1, source_target_pairs={{0,4},{4,0},{8,12},{12,8},{1,5},{5,1},{9,13},{13,9},{2,6},{6,2},{1... | collective-permute-start | bytes 147464 | tf_op jit(solution)/shard_map/ppermute | solution.py:747
  12.0 4.6 %collective-permute-start.3 = (f32[11,16,128]{2,1,0:T(8,128)S(1)}, f32[11,16,128]{2,1,0:T(8,128)S(1)}, u32[]{:S(2)}, u32[]{:S(2)}) collective-permute-start(f32[11,16,128]{2,1,0:T(8,128)S(1)} %get-tuple-element.39), channel_id=1, source_target_pairs={{0,4},{1,2},{2,1},{3,7},{4,0},{5,6},{6,5},{7,3},{8,12},{9,10},{10,... | collective-permute-start | bytes 270344 | tf_op jit(solution)/shard_map/ppermute | solution.py:765
  12.3 4.3 %collective-permute-start.4 = (f32[11,16,128]{2,1,0:T(8,128)S(1)}, f32[11,16,128]{2,1,0:T(8,128)S(1)}, u32[]{:S(2)}, u32[]{:S(2)}) collective-permute-start(f32[11,16,128]{2,1,0:T(8,128)S(1)} %get-tuple-element.40), channel_id=1, source_target_pairs={{0,1},{1,0},{2,3},{3,2},{4,5},{5,4},{6,7},{7,6},{8,9},{9,8},{10,11... | collective-permute-start | bytes 270344 | tf_op jit(solution)/shard_map/ppermute | solution.py:766
  18.3 5.9 %collective-permute-start.5 = (f32[5,16,128]{2,1,0:T(8,128)S(1)}, f32[5,16,128]{2,1,0:T(8,128)S(1)}, u32[]{:S(2)}, u32[]{:S(2)}) collective-permute-start(f32[5,16,128]{2,1,0:T(8,128)S(1)} %get-tuple-element.41), channel_id=1, source_target_pairs={{0,8},{4,12},{8,0},{12,4},{1,9},{5,13},{9,1},{13,5},{2,10},{6,14},... | collective-permute-start | bytes 122888 | tf_op jit(solution)/shard_map/ppermute | solution.py:747
  20.0 5.8 %collective-permute-start.6 = (f32[5,16,128]{2,1,0:T(8,128)S(1)}, f32[5,16,128]{2,1,0:T(8,128)S(1)}, u32[]{:S(2)}, u32[]{:S(2)}) collective-permute-start(f32[5,16,128]{2,1,0:T(8,128)S(1)} %get-tuple-element.42), channel_id=1, source_target_pairs={{0,12},{4,8},{8,4},{12,0},{1,13},{5,9},{9,5},{13,1},{2,14},{6,10},... | collective-permute-start | bytes 122888 | tf_op jit(solution)/shard_map/ppermute | solution.py:747
  21.0 4.8 %collective-permute-start.7 = (f32[5,16,128]{2,1,0:T(8,128)S(1)}, f32[5,16,128]{2,1,0:T(8,128)S(1)}, u32[]{:S(2)}, u32[]{:S(2)}) collective-permute-start(f32[5,16,128]{2,1,0:T(8,128)S(1)} %get-tuple-element.43), channel_id=1, source_target_pairs={{0,4},{4,0},{8,12},{12,8},{1,5},{5,1},{9,13},{13,9},{2,6},{6,2},{1... | collective-permute-start | bytes 122888 | tf_op jit(solution)/shard_map/ppermute | solution.py:747

commit v4 on v3

--- a/solution.py
+++ b/solution.py
@@ -259,6 +259,10 @@
     return lax.broadcasted_iota(jnp.int32, tile, 0)
 
 
+def band_ids():
+    return jnp.bitwise_and(lane_ids() // 4, 7)
+
+
 def pick_lanes(values, index):
     return jnp.take_along_axis(values, index, axis=1, mode="promise_in_bounds")
 
@@ -283,12 +287,27 @@
     return jnp.bitwise_and(amount, lanes - 1)
 
 
-def pack_tile(layer_tiles, part):
-    group = lane_ids() // chunk
-    out = None
-    for layer in range(layers):
-        moved = turn(layer_tiles[layer], mod_lanes(chunk * (layer - part) + lanes))
-        out = moved if out is None else jnp.where(group == layer, moved, out)
+def group_ids():
+    return lane_ids() // chunk
+
+
+def turn_groups(tiles):
+    low_half = lane_ids() < lanes // 2
+    even_group = jnp.bitwise_and(group_ids(), 1) == 0
+    out = list(tiles)
+    for a, b, mask, width in ((0, 2, low_half, 2), (1, 3, low_half, 2), (0, 1, even_group, 1), (2, 3, even_group, 1)):
+        first, second = out[a], out[b]
+        out[a] = jnp.where(mask, first, turn(second, chunk * width))
+        out[b] = jnp.where(mask, turn(first, -chunk * width), second)
+    return out
+
+
+def by_distance(items, me):
+    out = list(items)
+    for bit, pairs in ((1, ((0, 1), (2, 3))), (2, ((0, 2), (1, 3)))):
+        is_set = jnp.bitwise_and(me, bit) != 0
+        for a, b in pairs:
+            out[a], out[b] = jnp.where(is_set, out[b], out[a]), jnp.where(is_set, out[a], out[b])
     return out
 
 
@@ -296,36 +315,27 @@
     messages = in_order(refs)
     me = lax.axis_index("inst")
     lane = lane_ids()
+    place = lane // 4
     slot = jnp.bitwise_and(lane, 3)
     step = jnp.where(slot < 2, slot - 2, slot + chunk - 2)
-    parts = [jnp.bitwise_xor(me, distance) for distance in range(inst_count)]
-    index = [mod_lanes(step + (chunk * part + lanes)) for part in parts]
-
-    def one_field(field, edges):
+    part_at = jnp.bitwise_and(place, 3)
+    index = [mod_lanes(step + (chunk * jnp.bitwise_xor(part_at, layer) + lanes)) for layer in range(layers)]
+    edges = [jnp.zeros(tile, jnp.float32)] * inst_count
+    for field in range(5):
         tiles = [flow[0, field, layer] for layer in range(layers)]
-        edges = list(edges)
-        for distance, part in enumerate(parts):
-            messages[distance][field] = pack_tile(tiles, part)
-            for layer in range(layers):
-                here = lane // 4 == field * 4 + layer
-                edges[distance] = jnp.where(here, pick_lanes(tiles[layer], index[distance]), edges[distance])
-        return tuple(edges)
-
-    edges = unrolled(5, one_field, (jnp.zeros(tile, jnp.float32),) * inst_count)
+        for distance, values in enumerate(by_distance(turn_groups(tiles), me)):
+            messages[distance][field] = values
+        for layer in range(layers):
+            got = pick_lanes(tiles[layer], index[layer])
+            for distance in range(inst_count):
+                here = place == field * 4 + jnp.bitwise_xor(me, distance ^ layer)
+                edges[distance] = jnp.where(here, got, edges[distance])
     for distance in range(inst_count):
         messages[distance][5] = edges[distance]
 
 
 def spread_tiles(received, field, me):
-    group = lane_ids() // chunk
-    outs = [None] * layers
-    for distance in range(inst_count):
-        part = jnp.bitwise_xor(me, distance)
-        values = received[distance][field]
-        for layer in range(layers):
-            moved = turn(values, mod_lanes(chunk * (part - layer) + lanes))
-            outs[layer] = moved if outs[layer] is None else jnp.where(group == part, moved, outs[layer])
-    return outs
+    return turn_groups(by_distance([message[field] for message in received], me))
 
 
 def unpack_kernel(*refs):
@@ -333,11 +343,12 @@
     me = lax.axis_index("inst")
     even = jnp.bitwise_and(lax.axis_index("space"), 1) == 0
     lane = lane_ids()
-    owner = jnp.bitwise_and(lane // 4, 3)
-    level = lane // 16 - 1
-    inner = jnp.clip(level, 0, layers - 1) * 4 + jnp.bitwise_and(lane, 3)
-
-    def one_field(field, ends):
+    owner = group_ids()
+    band = band_ids()
+    level = jnp.clip(band - 1, 0, layers - 1)
+    inner = jnp.bitwise_xor(level, me) * 4 + jnp.bitwise_and(lane, 3)
+    up_edge = down_edge = jnp.zeros(tile, jnp.float32)
+    for field in range(5):
         tiles = spread_tiles(received, field, me)
         for layer in range(layers):
             main[field, layer] = tiles[layer]
@@ -346,16 +357,11 @@
             near_b[2 * field + place] = jnp.where(even, tiles[place], tiles[2 + place])
         edges = None
         for distance in range(inst_count):
-            part = jnp.bitwise_xor(me, distance)
             got = pick_lanes(received[distance][5], inner + 16 * field)
-            edges = got if edges is None else jnp.where(owner == part, got, edges)
+            edges = got if edges is None else jnp.where(owner == jnp.bitwise_xor(me, distance), got, edges)
         halo[field] = edges
-        here = lane // 16 == field
-        up = turn(edges, mod_lanes(16 * field - 16 * layers + lanes))
-        down = turn(edges, mod_lanes(16 * field - 16 + lanes))
-        return jnp.where(here, up, ends[0]), jnp.where(here, down, ends[1])
-
-    up_edge, down_edge = unrolled(5, one_field, (jnp.zeros(tile, jnp.float32),) * 2)
+        up_edge = jnp.where(band == field, turn(edges, 4 * (field - layers)), up_edge)
+        down_edge = jnp.where(band == field, turn(edges, 4 * (field - 1)), down_edge)
     near_a[10] = jnp.where(even, up_edge, down_edge)
     near_b[10] = jnp.where(even, down_edge, up_edge)
 
@@ -363,25 +369,30 @@
 class Cells:
     def __init__(self, parts):
         self.parts = list(parts)
-        self.dens, self.vel, self.pres = parts[0], list(parts[1:4]), parts[4]
-        self.root, self.enth, self.heat = parts[5], parts[6], parts[7]
+        self.root, self.vel, self.temp = parts[0], list(parts[1:4]), parts[4]
+        if len(parts) == 5:
+            dens = self.root * self.root
+            kinetic = 0.5 * (self.vel[0] * self.vel[0] + self.vel[1] * self.vel[1] + self.vel[2] * self.vel[2])
+            enth = ratio * self.temp + kinetic
+            heat = 2.0 * viscosity * (kinetic + ratio / prandtl * self.temp)
+            self.parts += [dens, dens * self.temp, enth, heat]
+        self.dens, self.pres, self.enth, self.heat = self.parts[5:]
+        self.base = self.parts[:5]
 
     def map(self, change):
-        return Cells([change(part) for part in self.parts])
+        return Cells([change(part) for part in self.base])
 
     def conserved(self):
         dens, enth = self.dens, self.enth
         return [dens] + [dens * part for part in self.vel] + [dens * enth - self.pres]
 
 
+fields_kept = 9
+
+
 def cells_of(dens, vel, pres):
     inverse_root = lax.rsqrt(dens)
-    root = dens * inverse_root
-    temp = pres * (inverse_root * inverse_root)
-    kinetic = 0.5 * (vel[0] * vel[0] + vel[1] * vel[1] + vel[2] * vel[2])
-    enth = ratio * temp + kinetic
-    heat = 2.0 * viscosity * (kinetic + ratio / prandtl * temp)
-    return Cells([dens] + list(vel) + [pres, root, enth, heat])
+    return Cells([dens * inverse_root] + list(vel) + [pres * (inverse_root * inverse_root)])
 
 
 def cells_of_draws(draws):
@@ -467,23 +478,9 @@
 
 
 def over_instances(values):
-    out = weight_of(0) * values
-    for distance in range(1, inst_count):
-        out = out + weight_of(distance) * turn(values, chunk * distance)
-    return out
-
-
-def shift_slots(values, distance):
-    owner = jnp.bitwise_and(lane_ids() // 4, 3)
-    distance = distance % inst_count
-    return jnp.where(owner >= distance, turn(values, 4 * distance), turn(values, 4 * distance - 16))
-
-
-def over_slots(values):
-    out = weight_of(0) * values
-    for distance in range(1, inst_count):
-        out = out + weight_of(distance) * shift_slots(values, distance)
-    return out
+    weights = [weight_of(distance) for distance in range(inst_count)]
+    across = turn(values, 2 * chunk)
+    return (weights[0] * values + weights[2] * across) + turn(weights[1] * values + weights[3] * across, chunk)
 
 
 def put(ref, place, cells):
@@ -492,7 +489,7 @@
 
 
 def get(ref, place):
-    return Cells([ref[place, number] for number in range(8)])
+    return Cells([ref[place, number] for number in range(fields_kept)])
 
 
 class Pitch:
@@ -502,39 +499,40 @@
         me = lax.axis_index("inst")
         lane = lane_ids()
         self.slot = jnp.bitwise_and(lane, 3)
-        self.band = lane // 16
+        self.band = band_ids()
         column = jnp.bitwise_and(lane, chunk - 1)
         self.is_first, self.is_last = column == 0, column == chunk - 1
         self.seam = self.slot == jnp.where(me == 0, 1, jnp.where(me == inst_count - 1, 3, -1))
-        self.to_main = (lane // chunk) * 4 + jnp.where(self.is_first, 1, 3)
-        self.from_main = jnp.bitwise_and(lane // 4, 3) * chunk + jnp.where(self.slot == 1, 0, chunk - 1)
+        start = group_ids() * chunk
+        self.to_main = start + jnp.where(self.is_first, 1, 3)
+        self.from_main = start + jnp.where(self.slot == 1, 0, chunk - 1)
+        self.beside = lane + jnp.where(self.slot == 3, -1, 1)
 
     def mains(self, ref, places):
-        out = [None] * 8
+        out = [None] * 5
         for layer, place in places:
-            for number in range(8):
+            for number in range(5):
                 got = pick_lanes(ref[place, number], self.from_main)
                 out[number] = got if out[number] is None else jnp.where(self.band == layer + 1, got, out[number])
-        return Cells(out)
+        return out
 
     def edges(self, cells, mains):
         slot = self.slot
-        lower = Cells([jnp.where(slot == 3, b, a) for a, b in zip(cells.parts, mains.parts)])
+        lower = Cells([jnp.where(slot == 3, b, a) for a, b in zip(cells.base, mains)])
         upper = []
-        for a, b in zip(cells.parts, mains.parts):
-            value = jnp.where(slot == 3, turn(a, 1), turn(a, -1))
-            value = jnp.where(slot == 1, b, value)
-            other = pick_rows(shift_slots(value, -self.lag), self.above)
+        for a, b in zip(cells.base, mains):
+            value = jnp.where(slot == 1, b, pick_lanes(a, self.beside))
+            other = pick_rows(turn(value, -chunk * self.lag), self.above)
             upper.append(jnp.where(self.seam, other, value))
         faces = roe_flux(lower, Cells(upper), 1)
-        lower_use = [jnp.where(self.seam, pick_rows(shift_slots(face, self.lag), self.below), face) for face in faces]
+        lower_use = [jnp.where(self.seam, pick_rows(turn(face, chunk * self.lag), self.below), face) for face in faces]
         for part in range(5):
             self.edge_faces[part] = jnp.where(slot == 1, lower_use[part], faces[part])
         return faces, lower_use
 
     def change(self, cells, layer):
         faces = roe_flux(cells, cells.map(lambda part: turn(part, -1)), 1)
-        index = (layer + 1) * 16 + self.to_main
+        index = (layer + 1) * 4 + self.to_main
         changes = []
         for part in range(5):
             edge = pick_lanes(self.edge_faces[part], index)
@@ -566,13 +564,13 @@
         edge_first[number] = part
     faces, lower_use = pitch.edges(cells, pitch.mains(first, [(layer, layer) for layer in range(layers)]))
     span = span_change(cells)
-    axial = roe_flux(cells, cells.map(lambda part: turn(part, -16)), 0)
+    axial = roe_flux(cells, cells.map(lambda part: turn(part, -4)), 0)
     state = cells.conserved()
     for part in range(5):
         along = jnp.where(slot == 1, faces[part] - turn(faces[part], 1), faces[part] - turn(lower_use[part], -1))
-        value = over_slots(state[part]) + 0.5 * (along + span[part])
+        value = over_instances(state[part]) + 0.5 * (along + span[part])
         part_edge[part] = value
-        value = value + 0.5 * (axial[part] - turn(axial[part], 16))
+        value = value + 0.5 * (axial[part] - turn(axial[part], 4))
         state[part] = state[part] - pseudo_step * value
     edge_second = cells_of_conserved(state)
 
@@ -627,7 +625,7 @@
     pitch = Pitch(above[...], below[...], edge_faces)
     band = pitch.band
 
-    for number in range(8):
+    for number in range(fields_kept):
         ends[2, number] = first[0, number]
         ends[3, number] = first[layers - 1, number]
         second[2, number] = second_middle[0, number]
@@ -647,17 +645,17 @@
     outside = []
     for field in range(5):
         inside = halo[field]
-        low = jnp.where(at_low, turn(inside, -16), turn(low_tile, -16 * field))
-        high = jnp.where(at_high, turn(inside, 16), turn(high_tile, 16 * (layers + 1 - field)))
+        low = jnp.where(at_low, inside, turn(low_tile, -4 * field))
+        high = jnp.where(at_high, inside, turn(high_tile, 4 * (layers + 1 - field)))
         outside.append(jnp.where(band == 0, low, high))
     within = jnp.logical_and(band > 0, band < layers + 1)
     edge_cells = cells_of_draws(outside)
-    edge_cells = Cells([jnp.where(within, edge_first[number], edge_cells.parts[number]) for number in range(8)])
+    edge_cells = Cells([jnp.where(within, edge_first[number], edge_cells.parts[number]) for number in range(fields_kept)])
     pitch.edges(edge_cells, pitch.mains(ends, [(-1, 1), (layers, 4)]))
-    axial = roe_flux(edge_cells, edge_cells.map(lambda part: turn(part, -16)), 0)
+    axial = roe_flux(edge_cells, edge_cells.map(lambda part: turn(part, -4)), 0)
     state = edge_cells.conserved()
     for part in range(5):
-        value = part_edge[part] + 0.5 * (axial[part] - turn(axial[part], 16))
+        value = part_edge[part] + 0.5 * (axial[part] - turn(axial[part], 4))
         state[part] = state[part] - pseudo_step * value
     edge_second = cells_of_conserved(state)
 
@@ -690,7 +688,7 @@
         for part in range(5):
             state[part] = state[part] - pseudo_step * (part_first[layer, part] + 0.5 * change[high, part])
         put(second, layer + 1, cells_of_conserved(state))
-    for number in range(8):
+    for number in range(fields_kept):
         second[0, number] = jnp.where(at_low, second[1, number], second[0, number])
         second[layers + 1, number] = jnp.where(at_high, second[layers, number], second[layers + 1, number])
 
@@ -708,8 +706,8 @@
     for field in range(5):
         tiles = [ends[0, field], part_second[0, field] + 0.5 * change[0, field]]
         tiles += [part_second[1, field] + 0.5 * change[1, field], ends[1, field]]
-        for distance in range(inst_count):
-            messages[distance][field] = pack_tile(tiles, jnp.bitwise_xor(me, distance))
+        for distance, values in enumerate(by_distance(turn_groups(tiles), me)):
+            messages[distance][field] = values
 
 
 def return_kernel(*refs):
@@ -766,7 +764,14 @@
     near_a = lax.ppermute(near_a, "space", route_a)
     inner = call(
         inner_kernel,
-        [floats(layers, 8), floats(8), floats(layers, 5), floats(5), floats(layers - 2, 8), floats(layers - 2, 5)],
+        [
+            floats(layers, fields_kept),
+            floats(fields_kept),
+            floats(layers, 5),
+            floats(5),
+            floats(layers - 2, fields_kept),
+            floats(layers - 2, 5),
+        ],
         [above, below, main, halo],
         [(5,) + tile],
     )
@@ -774,7 +779,7 @@
         outer_kernel,
         [floats(5)] * inst_count,
         [*inner, above, below, halo, near_b, near_a],
-        [(6, 8) + tile, (layers + 2, 8) + tile, (2, 5) + tile, (5,) + tile],
+        [(6, fields_kept) + tile, (layers + 2, fields_kept) + tile, (2, 5) + tile, (5,) + tile],
     )
     return call(return_kernel, [(flow_state.shape, jnp.float32)], swap_instances(results))[0]
 

time: 26.8 us -> 26.1 us (0.974)
  Pallas kernels: 6.24 us -> 5.39 us
    pallas_call x6, Pallas kernels: 6.24 us -> 5.39 us  [call(): pl.pallas_call(kernel, out_shape=shapes, in_specs=[smem] * scalars + [vme...]
  transfers between devices with their start and end apart: 8 -> 8, of which waited for: 4 -> 4; matrix products, arithmetic and copies ran while one was open for 0% -> 0% of each run, Pallas kernels for 10% -> 9%
where the time goes in v4:
time: 26.1 us; the launch traced here: 26 us
  starting transfers between devices  10.9 us (42%)
  waiting for transfers between devices  8.29 us (32%)
  Pallas kernels  5.39 us (21%)
  local copies, waits for them, and re-layouts  1.34 us (5%)
    ppermute x6, starting transfers between devices, swap_instances(): got.append(lax.ppermute(message, 'inst', route) if distance else message)  9.23 us
    ppermute x6, waiting for transfers between devices, swap_instances(): got.append(lax.ppermute(message, 'inst', route) if distance else message)  7.28 us
    pallas_call x6, Pallas kernels, call(): pl.pallas_call(kernel, out_shape=shapes, in_specs=[smem] * scalars + [vme...  5.39 us
    ppermute x1, starting transfers between devices, on_device_fast(): near_a = lax.ppermute(near_a, 'space', route_a)  1.38 us
    unnamed x4, local copies, waits for them, and re-layouts  1.34 us
    ppermute x1, waiting for transfers between devices, on_device_fast(): near_b = lax.ppermute(near_b, ('inst', 'space'), route_b)  1.01 us
  transfers between devices with their start and end apart: 8, of which 4 were waited for; matrix products, arithmetic and copies ran while one was open for 0% of the time, Pallas kernels for 9%

profile of v4, /device:TPU:0, one launch (start us, length us, event | category | flops | bytes accessed | tf_op | source)
XLA Modules:
  0.0 26.0 jit_solution(15724473812396813918)
XLA Ops:
  0.0 0.0 copy-start
  0.0 0.9 %copy-done = f32[1,5,4,16,128]{4,3,2,1,0:T(8,128)S(1)} copy-done((f32[1,5,4,16,128]{4,3,2,1,0:T(8,128)S(1)}, f32[1,5,4,16,128]{4,3,2,1,0:T(8,128)}, u32[]{:S(2)}) %copy-start) | copy-done | bytes 163864
  0.9 0.3 %shard_map.28 = (f32[6,16,128]{2,1,0:T(8,128)S(1)}, f32[6,16,128]{2,1,0:T(8,128)S(1)}, f32[6,16,128]{2,1,0:T(8,128)S(1)}, f32[6,16,128]{2,1,0:T(8,128)S(1)}) custom-call(f32[1,5,4,16,128]{4,3,2,1,0:T(8,128)S(1)} %copy-done), custom_call_target="tpu_custom_call" | custom-call | tf_op jit(solution)/shard_map/pallas_call | solution.py:727
  1.3 4.1 %collective-permute-start = (f32[6,16,128]{2,1,0:T(8,128)S(1)}, f32[6,16,128]{2,1,0:T(8,128)S(1)}, u32[]{:S(2)}, u32[]{:S(2)}) collective-permute-start(f32[6,16,128]{2,1,0:T(8,128)S(1)} %get-tuple-element.28), channel_id=1, source_target_pairs={{0,8},{4,12},{8,0},{12,4},{1,9},{5,13},{9,1},{13,5},{2,10},{6,14},... | collective-permute-start | bytes 147464 | tf_op jit(solution)/shard_map/ppermute | solution.py:745
  5.4 1.3 %collective-permute-start.1 = (f32[6,16,128]{2,1,0:T(8,128)S(1)}, f32[6,16,128]{2,1,0:T(8,128)S(1)}, u32[]{:S(2)}, u32[]{:S(2)}) collective-permute-start(f32[6,16,128]{2,1,0:T(8,128)S(1)} %get-tuple-element.29), channel_id=1, source_target_pairs={{0,12},{4,8},{8,4},{12,0},{1,13},{5,9},{9,5},{13,1},{2,14},{6,10},... | collective-permute-start | bytes 147464 | tf_op jit(solution)/shard_map/ppermute | solution.py:745
  6.7 0.0 copy-start.1
  6.7 0.2 collective-permute-start.2
  7.0 0.4 %copy-done.1 = s32[16]{0:T(128)S(1)} copy-done((s32[16]{0:T(128)S(1)}, s32[16]{0:T(128)}, u32[]{:S(2)}) %copy-start.1) | copy-done | bytes 88
  7.4 0.6 %shard_map.29 = (s32[16,128]{1,0:T(8,128)S(1)}, s32[16,128]{1,0:T(8,128)S(1)}) custom-call(s32[16]{0:T(128)S(1)} %copy-done.1, f32[6,16,128]{2,1,0:T(8,128)S(1)} %get-tuple-element.25.behind.refs_3_), custom_call_target="tpu_custom_call" | custom-call | tf_op jit(solution)/shard_map/pallas_call | solution.py:727
  7.9 0.0 collective-permute-done.refs_0_
  8.0 3.4 %collective-permute-done.1.refs_1_ = f32[6,16,128]{2,1,0:T(8,128)S(1)} collective-permute-done((f32[6,16,128]{2,1,0:T(8,128)S(1)}, f32[6,16,128]{2,1,0:T(8,128)S(1)}, u32[]{:S(2)}, u32[]{:S(2)}) %collective-permute-start.1) | collective-permute-done | bytes 49184 | tf_op jit(solution)/shard_map/ppermute | solution.py:745
  11.3 0.0 collective-permute-done.2.refs_2_
  11.3 0.3 %shard_map.30 = (f32[11,16,128]{2,1,0:T(8,128)S(1)}, f32[11,16,128]{2,1,0:T(8,128)S(1)}, f32[5,4,16,128]{3,2,1,0:T(8,128)S(1)}, f32[5,16,128]{2,1,0:T(8,128)S(1)}) custom-call(f32[6,16,128]{2,1,0:T(8,128)S(1)} %collective-permute-done.refs_0_, f32[6,16,128]{2,1,0:T(8,128)S(1)} %collective-permute-done.1.refs_1_, ...), custom_call_target="tpu_custom_call" | custom-call | tf_op jit(solution)/shard_map/pallas_call | solution.py:727
  11.7 0.3 %collective-permute-start.3 = (f32[11,16,128]{2,1,0:T(8,128)S(1)}, f32[11,16,128]{2,1,0:T(8,128)S(1)}, u32[]{:S(2)}, u32[]{:S(2)}) collective-permute-start(f32[11,16,128]{2,1,0:T(8,128)S(1)} %get-tuple-element.39), channel_id=1, source_target_pairs={{0,4},{1,2},{2,1},{3,7},{4,0},{5,6},{6,5},{7,3},{8,12},{9,10},{10,... | collective-permute-start | bytes 270344 | tf_op jit(solution)/shard_map/ppermute | solution.py:763
  12.0 1.4 %collective-permute-start.4 = (f32[11,16,128]{2,1,0:T(8,128)S(1)}, f32[11,16,128]{2,1,0:T(8,128)S(1)}, u32[]{:S(2)}, u32[]{:S(2)}) collective-permute-start(f32[11,16,128]{2,1,0:T(8,128)S(1)} %get-tuple-element.40), channel_id=1, source_target_pairs={{0,1},{1,0},{2,3},{3,2},{4,5},{5,4},{6,7},{7,6},{8,9},{9,8},{10,11... | collective-permute-start | bytes 270344 | tf_op jit(solution)/shard_map/ppermute | solution.py:764
  13.4 1.9 %shard_map.31 = (f32[4,9,16,128]{3,2,1,0:T(8,128)S(1)}, f32[9,16,128]{2,1,0:T(8,128)S(1)}, f32[4,5,16,128]{3,2,1,0:T(8,128)S(1)}, f32[5,16,128]{2,1,0:T(8,128)S(...) custom-call(s32[16,128]{1,0:T(8,128)S(1)} %get-tuple-element.26.refs_4_.above, ...), custom_call_target="tpu_custom_call" | custom-call | tf_op jit(solution)/shard_map/pallas_call | solution.py:727
  15.3 1.0 %collective-permute-done.3.near_b = f32[11,16,128]{2,1,0:T(8,128)S(1)} collective-permute-done((f32[11,16,128]{2,1,0:T(8,128)S(1)}, f32[11,16,128]{2,1,0:T(8,128)S(1)}, u32[]{:S(2)}, u32[]{:S(2)}) %collective-permute-start.3) | collective-permute-done | bytes 90144 | tf_op jit(solution)/shard_map/ppermute | solution.py:763
  16.3 0.0 collective-permute-done.4.near_a
  16.3 1.4 %shard_map.32 = (f32[5,16,128]{2,1,0:T(8,128)S(1)}, f32[5,16,128]{2,1,0:T(8,128)S(1)}, f32[5,16,128]{2,1,0:T(8,128)S(1)}, f32[5,16,128]{2,1,0:T(8,128)S(1)}) custom-call(f32[4,9,16,128]{3,2,1,0:T(8,128)S(1)} %get-tuple-element.33.first, f32[9,16,128]{2,1,0:T(8,128)S(1)} %get-tuple-element.34.edge_first, f32[4,5,16,128]{3,2,1,0:T(8,128)S(1)} %get-tuple-element.35.part_first, ...), custom_call_target="tpu_custom_call" | custom-call | tf_op jit(solution)/shard_map/pallas_call | solution.py:727
  17.7 1.6 %collective-permute-start.5 = (f32[5,16,128]{2,1,0:T(8,128)S(1)}, f32[5,16,128]{2,1,0:T(8,128)S(1)}, u32[]{:S(2)}, u32[]{:S(2)}) collective-permute-start(f32[5,16,128]{2,1,0:T(8,128)S(1)} %get-tuple-element.41), channel_id=1, source_target_pairs={{0,8},{4,12},{8,0},{12,4},{1,9},{5,13},{9,1},{13,5},{2,10},{6,14},... | collective-permute-start | bytes 122888 | tf_op jit(solution)/shard_map/ppermute | solution.py:745
  19.3 1.0 %collective-permute-start.6 = (f32[5,16,128]{2,1,0:T(8,128)S(1)}, f32[5,16,128]{2,1,0:T(8,128)S(1)}, u32[]{:S(2)}, u32[]{:S(2)}) collective-permute-start(f32[5,16,128]{2,1,0:T(8,128)S(1)} %get-tuple-element.42), channel_id=1, source_target_pairs={{0,12},{4,8},{8,4},{12,0},{1,13},{5,9},{9,5},{13,1},{2,14},{6,10},... | collective-permute-start | bytes 122888 | tf_op jit(solution)/shard_map/ppermute | solution.py:745
  20.3 0.9 %collective-permute-start.7 = (f32[5,16,128]{2,1,0:T(8,128)S(1)}, f32[5,16,128]{2,1,0:T(8,128)S(1)}, u32[]{:S(2)}, u32[]{:S(2)}) collective-permute-start(f32[5,16,128]{2,1,0:T(8,128)S(1)} %get-tuple-element.43), channel_id=1, source_target_pairs={{0,4},{4,0},{8,12},{12,8},{1,5},{5,1},{9,13},{13,9},{2,6},{6,2},{1... | collective-permute-start | bytes 122888 | tf_op jit(solution)/shard_map/ppermute | solution.py:745
  21.2 2.4 %collective-permute-done.5.refs_0_ = f32[5,16,128]{2,1,0:T(8,128)S(1)} collective-permute-done((f32[5,16,128]{2,1,0:T(8,128)S(1)}, f32[5,16,128]{2,1,0:T(8,128)S(1)}, u32[]{:S(2)}, u32[]{:S(2)}) %collective-permute-start.5) | collective-permute-done | bytes 40992 | tf_op jit(solution)/shard_map/ppermute | solution.py:745
  23.6 1.5 %collective-permute-done.6.refs_1_ = f32[5,16,128]{2,1,0:T(8,128)S(1)} collective-permute-done((f32[5,16,128]{2,1,0:T(8,128)S(1)}, f32[5,16,128]{2,1,0:T(8,128)S(1)}, u32[]{:S(2)}, u32[]{:S(2)}) %collective-permute-start.6) | collective-permute-done | bytes 40992 | tf_op jit(solution)/shard_map/ppermute | solution.py:745
  25.1 0.0 collective-permute-done.7.refs_2_
  25.1 0.9 %shard_map.33 = f32[1,5,4,16,128]{4,3,2,1,0:T(8,128)} custom-call(f32[5,16,128]{2,1,0:T(8,128)S(1)} %collective-permute-done.5.refs_0_, f32[5,16,128]{2,1,0:T(8,128)S(1)} %collective-permute-done.6.refs_1_, f32[5,16,128]{2,1,0:T(8,128)S(1)} %collective-permute-done.7.refs_2_, f32[5,16,128]{2,1,0:T(8,128)S(1)} %get-tuple-element.44.refs_3_), custom_call_target="tpu_custom_call" | custom-call | tf_op jit(solution)/shard_map/pallas_call | solution.py:727
Async XLA Ops:
  0.0 0.9 %copy-start = (f32[1,5,4,16,128]{4,3,2,1,0:T(8,128)S(1)}, f32[1,5,4,16,128]{4,3,2,1,0:T(8,128)}, u32[]{:S(2)}) copy-start(f32[1,5,4,16,128]{4,3,2,1,0:T(8,128)} %flow.1) | copy-start | bytes 491524
  1.3 6.7 %collective-permute-start = (f32[6,16,128]{2,1,0:T(8,128)S(1)}, f32[6,16,128]{2,1,0:T(8,128)S(1)}, u32[]{:S(2)}, u32[]{:S(2)}) collective-permute-start(f32[6,16,128]{2,1,0:T(8,128)S(1)} %get-tuple-element.28), channel_id=1, source_target_pairs={{0,8},{4,12},{8,0},{12,4},{1,9},{5,13},{9,1},{13,5},{2,10},{6,14},... | collective-permute-start | bytes 147464 | tf_op jit(solution)/shard_map/ppermute | solution.py:745
  5.4 6.0 %collective-permute-start.1 = (f32[6,16,128]{2,1,0:T(8,128)S(1)}, f32[6,16,128]{2,1,0:T(8,128)S(1)}, u32[]{:S(2)}, u32[]{:S(2)}) collective-permute-start(f32[6,16,128]{2,1,0:T(8,128)S(1)} %get-tuple-element.29), channel_id=1, source_target_pairs={{0,12},{4,8},{8,4},{12,0},{1,13},{5,9},{9,5},{13,1},{2,14},{6,10},... | collective-permute-start | bytes 147464 | tf_op jit(solution)/shard_map/ppermute | solution.py:745
  6.7 0.7 %copy-start.1 = (s32[16]{0:T(128)S(1)}, s32[16]{0:T(128)}, u32[]{:S(2)}) copy-start(s32[16]{0:T(128)} %match.1) | copy-start | bytes 196
  6.7 4.6 %collective-permute-start.2 = (f32[6,16,128]{2,1,0:T(8,128)S(1)}, f32[6,16,128]{2,1,0:T(8,128)S(1)}, u32[]{:S(2)}, u32[]{:S(2)}) collective-permute-start(f32[6,16,128]{2,1,0:T(8,128)S(1)} %get-tuple-element.30), channel_id=1, source_target_pairs={{0,4},{4,0},{8,12},{12,8},{1,5},{5,1},{9,13},{13,9},{2,6},{6,2},{1... | collective-permute-start | bytes 147464 | tf_op jit(solution)/shard_map/ppermute | solution.py:745
  11.7 4.6 %collective-permute-start.3 = (f32[11,16,128]{2,1,0:T(8,128)S(1)}, f32[11,16,128]{2,1,0:T(8,128)S(1)}, u32[]{:S(2)}, u32[]{:S(2)}) collective-permute-start(f32[11,16,128]{2,1,0:T(8,128)S(1)} %get-tuple-element.39), channel_id=1, source_target_pairs={{0,4},{1,2},{2,1},{3,7},{4,0},{5,6},{6,5},{7,3},{8,12},{9,10},{10,... | collective-permute-start | bytes 270344 | tf_op jit(solution)/shard_map/ppermute | solution.py:763
  12.0 4.3 %collective-permute-start.4 = (f32[11,16,128]{2,1,0:T(8,128)S(1)}, f32[11,16,128]{2,1,0:T(8,128)S(1)}, u32[]{:S(2)}, u32[]{:S(2)}) collective-permute-start(f32[11,16,128]{2,1,0:T(8,128)S(1)} %get-tuple-element.40), channel_id=1, source_target_pairs={{0,1},{1,0},{2,3},{3,2},{4,5},{5,4},{6,7},{7,6},{8,9},{9,8},{10,11... | collective-permute-start | bytes 270344 | tf_op jit(solution)/shard_map/ppermute | solution.py:764
  17.7 5.9 %collective-permute-start.5 = (f32[5,16,128]{2,1,0:T(8,128)S(1)}, f32[5,16,128]{2,1,0:T(8,128)S(1)}, u32[]{:S(2)}, u32[]{:S(2)}) collective-permute-start(f32[5,16,128]{2,1,0:T(8,128)S(1)} %get-tuple-element.41), channel_id=1, source_target_pairs={{0,8},{4,12},{8,0},{12,4},{1,9},{5,13},{9,1},{13,5},{2,10},{6,14},... | collective-permute-start | bytes 122888 | tf_op jit(solution)/shard_map/ppermute | solution.py:745
  19.3 5.8 %collective-permute-start.6 = (f32[5,16,128]{2,1,0:T(8,128)S(1)}, f32[5,16,128]{2,1,0:T(8,128)S(1)}, u32[]{:S(2)}, u32[]{:S(2)}) collective-permute-start(f32[5,16,128]{2,1,0:T(8,128)S(1)} %get-tuple-element.42), channel_id=1, source_target_pairs={{0,12},{4,8},{8,4},{12,0},{1,13},{5,9},{9,5},{13,1},{2,14},{6,10},... | collective-permute-start | bytes 122888 | tf_op jit(solution)/shard_map/ppermute | solution.py:745
  20.3 4.8 %collective-permute-start.7 = (f32[5,16,128]{2,1,0:T(8,128)S(1)}, f32[5,16,128]{2,1,0:T(8,128)S(1)}, u32[]{:S(2)}, u32[]{:S(2)}) collective-permute-start(f32[5,16,128]{2,1,0:T(8,128)S(1)} %get-tuple-element.43), channel_id=1, source_target_pairs={{0,4},{4,0},{8,12},{12,8},{1,5},{5,1},{9,13},{13,9},{2,6},{6,2},{1... | collective-permute-start | bytes 122888 | tf_op jit(solution)/shard_map/ppermute | solution.py:745

commit v5 on v4

--- a/solution.py
+++ b/solution.py
@@ -339,7 +339,7 @@
 
 
 def unpack_kernel(*refs):
-    received, (near_b, near_a, main, halo) = in_order(refs[:4]), refs[5:]
+    received, (near_a, near_b, main, halo) = in_order(refs[:4]), refs[5:]
     me = lax.axis_index("inst")
     even = jnp.bitwise_and(lax.axis_index("space"), 1) == 0
     lane = lane_ids()
@@ -402,11 +402,11 @@
 
 def cells_of_conserved(state):
     dens = state[0]
-    inverse = 1.0 / dens
+    inverse_root = lax.rsqrt(dens)
+    inverse = inverse_root * inverse_root
     vel = [part * inverse for part in state[1:4]]
-    kinetic = vel[0] * vel[0] + vel[1] * vel[1] + vel[2] * vel[2]
-    pres = (gamma_gas - 1.0) * (state[4] - 0.5 * dens * kinetic)
-    return cells_of(dens, vel, pres)
+    kinetic = 0.5 * (vel[0] * vel[0] + vel[1] * vel[1] + vel[2] * vel[2])
+    return Cells([dens * inverse_root] + vel + [(gamma_gas - 1.0) * (state[4] * inverse - kinetic)])
 
 
 def roe_flux(low, high, normal):
@@ -504,9 +504,11 @@
         self.is_first, self.is_last = column == 0, column == chunk - 1
         self.seam = self.slot == jnp.where(me == 0, 1, jnp.where(me == inst_count - 1, 3, -1))
         start = group_ids() * chunk
-        self.to_main = start + jnp.where(self.is_first, 1, 3)
-        self.from_main = start + jnp.where(self.slot == 1, 0, chunk - 1)
-        self.beside = lane + jnp.where(self.slot == 3, -1, 1)
+        ahead = chunk * self.lag
+        low_seam, high_seam = me == 0, me == inst_count - 1
+        self.to_main = start + jnp.where(self.is_first, jnp.where(low_seam, 1 - ahead, 1), 3)
+        self.from_main = mod_lanes(start + jnp.where(self.slot == 1, jnp.where(low_seam, ahead, 0), chunk - 1))
+        self.beside = mod_lanes(lane + jnp.where(self.slot == 3, jnp.where(high_seam, ahead - 1, -1), 1))
 
     def mains(self, ref, places):
         out = [None] * 5
@@ -522,17 +524,20 @@
         upper = []
         for a, b in zip(cells.base, mains):
             value = jnp.where(slot == 1, b, pick_lanes(a, self.beside))
-            other = pick_rows(turn(value, -chunk * self.lag), self.above)
-            upper.append(jnp.where(self.seam, other, value))
+            upper.append(jnp.where(self.seam, pick_rows(value, self.above), value))
         faces = roe_flux(lower, Cells(upper), 1)
-        lower_use = [jnp.where(self.seam, pick_rows(turn(face, chunk * self.lag), self.below), face) for face in faces]
+        moved = [pick_rows(face, self.below) for face in faces]
+        at_low = jnp.logical_and(self.seam, slot == 1)
         for part in range(5):
-            self.edge_faces[part] = jnp.where(slot == 1, lower_use[part], faces[part])
-        return faces, lower_use
+            self.edge_faces[part] = jnp.where(at_low, moved[part], faces[part])
+        return faces, moved
+
+    def as_upper(self, face, moved):
+        return jnp.where(self.seam, turn(moved, chunk * self.lag), face)
 
     def change(self, cells, layer):
         faces = roe_flux(cells, cells.map(lambda part: turn(part, -1)), 1)
-        index = (layer + 1) * 4 + self.to_main
+        index = mod_lanes((layer + 1) * 4 + self.to_main + lanes)
         changes = []
         for part in range(5):
             edge = pick_lanes(self.edge_faces[part], index)
@@ -562,12 +567,13 @@
     cells = cells_of_draws([halo[field] for field in range(5)])
     for number, part in enumerate(cells.parts):
         edge_first[number] = part
-    faces, lower_use = pitch.edges(cells, pitch.mains(first, [(layer, layer) for layer in range(layers)]))
+    faces, moved = pitch.edges(cells, pitch.mains(first, [(layer, layer) for layer in range(layers)]))
     span = span_change(cells)
     axial = roe_flux(cells, cells.map(lambda part: turn(part, -4)), 0)
     state = cells.conserved()
     for part in range(5):
-        along = jnp.where(slot == 1, faces[part] - turn(faces[part], 1), faces[part] - turn(lower_use[part], -1))
+        lower_use = pitch.as_upper(faces[part], moved[part])
+        along = jnp.where(slot == 1, faces[part] - turn(faces[part], 1), faces[part] - turn(lower_use, -1))
         value = over_instances(state[part]) + 0.5 * (along + span[part])
         part_edge[part] = value
         value = value + 0.5 * (axial[part] - turn(axial[part], 4))
@@ -611,47 +617,33 @@
             part_second[place, part] = over_instances(state[part]) + 0.5 * value
         return carry
 
-    lax.fori_loop(0, layers - 2, second_step, 0)
-
-
-def outer_kernel(
-    first, edge_first, part_first, part_edge, second_middle, part_second, above, below, halo, near_b, near_a, *refs
-):
-    messages, (ends, second, change, edge_faces) = in_order(refs[:4]), refs[4:]
-    where_on = lax.axis_index("space")
-    even = jnp.bitwise_and(where_on, 1) == 0
-    at_low = where_on == 0
-    at_high = where_on == lax.axis_size("space") - 1
+    unrolled(layers - 2, second_step)
+
+
+def side_values(high, closed, near, shared, scratch):
+    first, edge_first, part_first, part_edge, second_middle, part_second, above, below, halo = shared
+    ends, second, edge_faces = scratch
     pitch = Pitch(above[...], below[...], edge_faces)
-    band = pitch.band
-
-    for number in range(fields_kept):
-        ends[2, number] = first[0, number]
-        ends[3, number] = first[layers - 1, number]
-        second[2, number] = second_middle[0, number]
-        second[layers - 1, number] = second_middle[layers - 3, number]
-
-    for high in range(2):
-        own = get(first, high * (layers - 1))
-        closed, from_a = (at_high, even) if high else (at_low, jnp.logical_not(even))
-        for place in range(2):
-            draws = [jnp.where(from_a, near_a[2 * field + place], near_b[2 * field + place]) for field in range(5)]
-            cells = cells_of_draws(draws)
-            pairs = zip(own.parts, cells.parts)
-            put(ends, place + 4 * high, Cells([jnp.where(closed, a, b) for a, b in pairs]))
-
-    low_tile = jnp.where(even, near_b[10], near_a[10])
-    high_tile = jnp.where(even, near_a[10], near_b[10])
+    is_high = high == 1
+    own = high * (layers - 1)
+    outer_band = high * (layers + 1)
+
+    own_cells = get(first, own)
+    put(ends, 2 - 2 * high, own_cells)
+    put(second, 2 - 2 * high, get(second_middle, high))
+    for place, part in ((2 * high, high), (1, 1 - high)):
+        cells = cells_of_draws([near[2 * field + part] for field in range(5)])
+        if closed is not None:
+            cells = Cells([jnp.where(closed, a, b) for a, b in zip(own_cells.parts, cells.parts)])
+        put(ends, place, cells)
     outside = []
     for field in range(5):
-        inside = halo[field]
-        low = jnp.where(at_low, inside, turn(low_tile, -4 * field))
-        high = jnp.where(at_high, inside, turn(high_tile, 4 * (layers + 1 - field)))
-        outside.append(jnp.where(band == 0, low, high))
-    within = jnp.logical_and(band > 0, band < layers + 1)
-    edge_cells = cells_of_draws(outside)
-    edge_cells = Cells([jnp.where(within, edge_first[number], edge_cells.parts[number]) for number in range(fields_kept)])
-    pitch.edges(edge_cells, pitch.mains(ends, [(-1, 1), (layers, 4)]))
+        value = turn(near[10], mod_lanes(4 * (outer_band - field) + lanes))
+        outside.append(value if closed is None else jnp.where(closed, halo[field], value))
+    outside = cells_of_draws(outside).parts
+    in_outer = pitch.band == outer_band
+    edge_cells = Cells([jnp.where(in_outer, part, edge_first[number]) for number, part in enumerate(outside)])
+    pitch.edges(edge_cells, pitch.mains(ends, [(0, 1)]))
     axial = roe_flux(edge_cells, edge_cells.map(lambda part: turn(part, -4)), 0)
     state = edge_cells.conserved()
     for part in range(5):
@@ -659,54 +651,54 @@
         state[part] = state[part] - pseudo_step * value
     edge_second = cells_of_conserved(state)
 
-    def end_values(ref, high, layer):
-        base = 3 * high
-        cells = get(ref, base + 1)
-        lower = roe_flux(get(ref, base), cells, 0)
-        upper = roe_flux(cells, get(ref, base + 2), 0)
+    def middle_values(ref, layer):
+        cells = get(ref, 1)
+        lower = roe_flux(get(ref, 0), cells, 0)
+        upper = roe_flux(cells, get(ref, 2), 0)
         span = span_change(cells)
         along = pitch.change(cells, layer)
         state = cells.conserved()
-        values = []
+        values, inward = [], []
         for part in range(5):
             value = (upper[part] - lower[part]) + span[part] + along[part]
             values.append(over_instances(state[part]) + 0.5 * value)
-            change[high, part] = jnp.where(high == 0, -upper[part], lower[part])
-        return state, values
-
-    def first_step(high, carry):
-        state, values = end_values(ends, high, high * (layers + 1) - 1)
-        state = [a - pseudo_step * b for a, b in zip(state, values)]
-        put(second, high * (layers + 1), cells_of_conserved(state))
-        return carry
-
-    unrolled(2, first_step)
-
-    for high in range(2):
-        layer = high * (layers - 1)
-        state = get(first, layer).conserved()
+            inward.append(0.5 * jnp.where(is_high, lower[part], -upper[part]))
+        return state, values, inward
+
+    state, values, inward = middle_values(ends, outer_band - 1)
+    beyond = cells_of_conserved([a - pseudo_step * b for a, b in zip(state, values)])
+    state = own_cells.conserved()
+    state = [a - pseudo_step * (part_first[own, part] + inward[part]) for part, a in enumerate(state)]
+    own_second = cells_of_conserved(state)
+    if closed is not None:
+        beyond = Cells([jnp.where(closed, a, b) for a, b in zip(own_second.parts, beyond.parts)])
+    put(second, 1, own_second)
+    put(second, 2 * high, beyond)
+    pitch.edges(edge_second, pitch.mains(second, [(0, 1)]))
+    _, values, inward = middle_values(second, own)
+    return values, [part_second[high, part] + inward[part] for part in range(5)]
+
+
+def near_side_kernel(near, *refs):
+    shared, out, scratch = refs[:9], refs[9], refs[10:]
+    high = 1 - jnp.bitwise_and(lax.axis_index("space"), 1)
+    for place, values in enumerate(side_values(high, None, near, shared, scratch)):
         for part in range(5):
-            state[part] = state[part] - pseudo_step * (part_first[layer, part] + 0.5 * change[high, part])
-        put(second, layer + 1, cells_of_conserved(state))
-    for number in range(fields_kept):
-        second[0, number] = jnp.where(at_low, second[1, number], second[0, number])
-        second[layers + 1, number] = jnp.where(at_high, second[layers, number], second[layers + 1, number])
-
-    pitch.edges(edge_second, pitch.mains(second, [(0, 1), (layers - 1, layers)]))
-
-    def second_step(high, carry):
-        _, values = end_values(second, high, high * (layers - 1))
-        for part in range(5):
-            ends[high, part] = values[part]
-        return carry
-
-    lax.fori_loop(0, 2, second_step, 0)
-
+            out[place, part] = values[part]
+
+
+def far_side_kernel(near, other, *refs):
+    shared, messages, scratch = refs[:9], in_order(refs[9:13]), refs[13:]
+    where_on = lax.axis_index("space")
+    high = jnp.bitwise_and(where_on, 1)
+    closed = jnp.logical_or(where_on == 0, where_on == lax.axis_size("space") - 1)
+    end, inner = side_values(high, closed, near, shared, scratch)
     me = lax.axis_index("inst")
+    is_high = high == 1
     for field in range(5):
-        tiles = [ends[0, field], part_second[0, field] + 0.5 * change[0, field]]
-        tiles += [part_second[1, field] + 0.5 * change[1, field], ends[1, field]]
-        for distance, values in enumerate(by_distance(turn_groups(tiles), me)):
+        low_side = [jnp.where(is_high, other[place, field], mine[field]) for place, mine in ((0, end), (1, inner))]
+        high_side = [jnp.where(is_high, mine[field], other[place, field]) for place, mine in ((1, inner), (0, end))]
+        for distance, values in enumerate(by_distance(turn_groups(low_side + high_side), me)):
             messages[distance][field] = values
 
 
@@ -751,7 +743,7 @@
     messages = call(pack_kernel, [floats(6)] * inst_count, [flow_state])
     integers = (tile, jnp.int32)
     above, below = call(index_kernel, [integers, integers], [period_match, messages[-1]], scalars=1)
-    near_b, near_a, main, halo = call(
+    near_a, near_b, main, halo = call(
         unpack_kernel, [floats(11), floats(11), floats(5, layers), floats(5)], [*swap_instances(messages), above]
     )
     route_a = [(i, i ^ 1) for i in range(count)]
@@ -760,8 +752,8 @@
         for i in range(count):
             far = (n, ((i - 1) ^ 1) + 1) if 0 < i < count - 1 else (n ^ 1, i)
             route_b.append((n * count + i, far[0] * count + far[1]))
+    near_a = lax.ppermute(near_a, "space", route_a)
     near_b = lax.ppermute(near_b, ("inst", "space"), route_b)
-    near_a = lax.ppermute(near_a, "space", route_a)
     inner = call(
         inner_kernel,
         [
@@ -775,12 +767,10 @@
         [above, below, main, halo],
         [(5,) + tile],
     )
-    results = call(
-        outer_kernel,
-        [floats(5)] * inst_count,
-        [*inner, above, below, halo, near_b, near_a],
-        [(6, fields_kept) + tile, (layers + 2, fields_kept) + tile, (2, 5) + tile, (5,) + tile],
-    )
+    shared = [*inner, above, below, halo]
+    scratch = [(3, fields_kept) + tile, (3, fields_kept) + tile, (5,) + tile]
+    (other,) = call(near_side_kernel, [floats(2, 5)], [near_a, *shared], scratch)
+    results = call(far_side_kernel, [floats(5)] * inst_count, [near_b, other, *shared], scratch)
     return call(return_kernel, [(flow_state.shape, jnp.float32)], swap_instances(results))[0]
 
 

time: 26.1 us -> 25.8 us (0.989)
  starting transfers between devices: 10.9 us -> 9.59 us
  waiting for transfers between devices: 8.29 us -> 9.32 us
    ppermute x1, starting transfers between devices: 1.38 us -> 0.07 us  [on_device_fast(): near_a = lax.ppermute(near_a, 'space', route_a)]
    ppermute x1, waiting for transfers between devices: 1.01 us -> 2.04 us  [on_device_fast(): near_b = lax.ppermute(near_b, ('inst', 'space'), route_b)]
    pallas_call x6 -> x7, Pallas kernels: 5.39 us -> 5.31 us  [call(): pl.pallas_call(kernel, out_shape=shapes, in_specs=[smem] * scalars + [vme...]
  transfers between devices with their start and end apart: 8 -> 8, of which waited for: 4 -> 4; matrix products, arithmetic and copies ran while one was open for 0% -> 0% of each run, Pallas kernels for 9% -> 11%
where the time goes in v5:
time: 25.8 us; the launch traced here: 25.6 us
  starting transfers between devices  9.59 us (37%)
  waiting for transfers between devices  9.32 us (36%)
  Pallas kernels  5.31 us (21%)
  local copies, waits for them, and re-layouts  1.34 us (5%)
    ppermute x6, starting transfers between devices, swap_instances(): got.append(lax.ppermute(message, 'inst', route) if distance else message)  9.23 us
    ppermute x6, waiting for transfers between devices, swap_instances(): got.append(lax.ppermute(message, 'inst', route) if distance else message)  7.28 us
    pallas_call x7, Pallas kernels, call(): pl.pallas_call(kernel, out_shape=shapes, in_specs=[smem] * scalars + [vme...  5.31 us
    ppermute x1, waiting for transfers between devices, on_device_fast(): near_b = lax.ppermute(near_b, ('inst', 'space'), route_b)  2.04 us
    unnamed x4, local copies, waits for them, and re-layouts  1.34 us
  transfers between devices with their start and end apart: 8, of which 4 were waited for; matrix products, arithmetic and copies ran while one was open for 0% of the time, Pallas kernels for 11%

profile of v5, /device:TPU:0, one launch (start us, length us, event | category | flops | bytes accessed | tf_op | source)
XLA Modules:
  0.0 25.6 jit_solution(5196309663076926056)
XLA Ops:
  0.0 0.0 copy-start
  0.0 0.9 %copy-done = f32[1,5,4,16,128]{4,3,2,1,0:T(8,128)S(1)} copy-done((f32[1,5,4,16,128]{4,3,2,1,0:T(8,128)S(1)}, f32[1,5,4,16,128]{4,3,2,1,0:T(8,128)}, u32[]{:S(2)}) %copy-start) | copy-done | bytes 163864
  0.9 0.3 %shard_map.28 = (f32[6,16,128]{2,1,0:T(8,128)S(1)}, f32[6,16,128]{2,1,0:T(8,128)S(1)}, f32[6,16,128]{2,1,0:T(8,128)S(1)}, f32[6,16,128]{2,1,0:T(8,128)S(1)}) custom-call(f32[1,5,4,16,128]{4,3,2,1,0:T(8,128)S(1)} %copy-done), custom_call_target="tpu_custom_call" | custom-call | tf_op jit(solution)/shard_map/pallas_call | solution.py:719
  1.3 4.1 %collective-permute-start = (f32[6,16,128]{2,1,0:T(8,128)S(1)}, f32[6,16,128]{2,1,0:T(8,128)S(1)}, u32[]{:S(2)}, u32[]{:S(2)}) collective-permute-start(f32[6,16,128]{2,1,0:T(8,128)S(1)} %get-tuple-element.25), channel_id=1, source_target_pairs={{0,8},{4,12},{8,0},{12,4},{1,9},{5,13},{9,1},{13,5},{2,10},{6,14},... | collective-permute-start | bytes 147464 | tf_op jit(solution)/shard_map/ppermute | solution.py:737
  5.4 1.3 %collective-permute-start.1 = (f32[6,16,128]{2,1,0:T(8,128)S(1)}, f32[6,16,128]{2,1,0:T(8,128)S(1)}, u32[]{:S(2)}, u32[]{:S(2)}) collective-permute-start(f32[6,16,128]{2,1,0:T(8,128)S(1)} %get-tuple-element.26), channel_id=1, source_target_pairs={{0,12},{4,8},{8,4},{12,0},{1,13},{5,9},{9,5},{13,1},{2,14},{6,10},... | collective-permute-start | bytes 147464 | tf_op jit(solution)/shard_map/ppermute | solution.py:737
  6.7 0.0 copy-start.1
  6.7 0.2 collective-permute-start.2
  7.0 0.4 %copy-done.1 = s32[16]{0:T(128)S(1)} copy-done((s32[16]{0:T(128)S(1)}, s32[16]{0:T(128)}, u32[]{:S(2)}) %copy-start.1) | copy-done | bytes 88
  7.4 0.6 %shard_map.29 = (s32[16,128]{1,0:T(8,128)S(1)}, s32[16,128]{1,0:T(8,128)S(1)}) custom-call(s32[16]{0:T(128)S(1)} %copy-done.1, f32[6,16,128]{2,1,0:T(8,128)S(1)} %get-tuple-element.28.behind.refs_3_), custom_call_target="tpu_custom_call" | custom-call | tf_op jit(solution)/shard_map/pallas_call | solution.py:719
  7.9 0.0 collective-permute-done.refs_0_
  8.0 3.4 %collective-permute-done.1.refs_1_ = f32[6,16,128]{2,1,0:T(8,128)S(1)} collective-permute-done((f32[6,16,128]{2,1,0:T(8,128)S(1)}, f32[6,16,128]{2,1,0:T(8,128)S(1)}, u32[]{:S(2)}, u32[]{:S(2)}) %collective-permute-start.1) | collective-permute-done | bytes 49184 | tf_op jit(solution)/shard_map/ppermute | solution.py:737
  11.3 0.0 collective-permute-done.2.refs_2_
  11.3 0.3 %shard_map.30 = (f32[11,16,128]{2,1,0:T(8,128)S(1)}, f32[11,16,128]{2,1,0:T(8,128)S(1)}, f32[5,4,16,128]{3,2,1,0:T(8,128)S(1)}, f32[5,16,128]{2,1,0:T(8,128)S(1)}) custom-call(f32[6,16,128]{2,1,0:T(8,128)S(1)} %collective-permute-done.refs_0_, f32[6,16,128]{2,1,0:T(8,128)S(1)} %collective-permute-done.1.refs_1_, ...), custom_call_target="tpu_custom_call" | custom-call | tf_op jit(solution)/shard_map/pallas_call | solution.py:719
  11.7 0.1 collective-permute-start.4
  11.8 0.3 %collective-permute-start.3 = (f32[11,16,128]{2,1,0:T(8,128)S(1)}, f32[11,16,128]{2,1,0:T(8,128)S(1)}, u32[]{:S(2)}, u32[]{:S(2)}) collective-permute-start(f32[11,16,128]{2,1,0:T(8,128)S(1)} %get-tuple-element.30), channel_id=1, source_target_pairs={{0,4},{1,2},{2,1},{3,7},{4,0},{5,6},{6,5},{7,3},{8,12},{9,10},{10,... | collective-permute-start | bytes 270344 | tf_op jit(solution)/shard_map/ppermute | solution.py:756
  12.1 1.5 %shard_map.31 = (f32[4,9,16,128]{3,2,1,0:T(8,128)S(1)}, f32[9,16,128]{2,1,0:T(8,128)S(1)}, f32[4,5,16,128]{3,2,1,0:T(8,128)S(1)}, f32[5,16,128]{2,1,0:T(8,128)S(...) custom-call(s32[16,128]{1,0:T(8,128)S(1)} %get-tuple-element.29.refs_4_.above.refs_6_, ...), custom_call_target="tpu_custom_call" | custom-call | tf_op jit(solution)/shard_map/pallas_call | solution.py:719
  13.6 0.0 collective-permute-done.4.near
  13.6 0.7 %shard_map.32.other = f32[2,5,16,128]{3,2,1,0:T(8,128)S(1)} custom-call(f32[11,16,128]{2,1,0:T(8,128)S(1)} %collective-permute-done.4.near, f32[4,9,16,128]{3,2,1,0:T(8,128)S(1)} %get-tuple-element.35.refs_0_, f32[9,16,128]{2,1,0:T(8,128)S(1)} %get-tuple-element.36.refs_1_, f32[4,5,16,128]{3,2,1,0:T(8,128)S(1)} %get-tuple-element.37.refs_2_, ...), custom_call_target="tpu_custom_call" | custom-call | tf_op jit(solution)/shard_map/pallas_call | solution.py:719
  14.3 2.0 %collective-permute-done.3.near = f32[11,16,128]{2,1,0:T(8,128)S(1)} collective-permute-done((f32[11,16,128]{2,1,0:T(8,128)S(1)}, f32[11,16,128]{2,1,0:T(8,128)S(1)}, u32[]{:S(2)}, u32[]{:S(2)}) %collective-permute-start.3) | collective-permute-done | bytes 90144 | tf_op jit(solution)/shard_map/ppermute | solution.py:756
  16.4 1.0 %shard_map.33 = (f32[5,16,128]{2,1,0:T(8,128)S(1)}, f32[5,16,128]{2,1,0:T(8,128)S(1)}, f32[5,16,128]{2,1,0:T(8,128)S(1)}, f32[5,16,128]{2,1,0:T(8,128)S(1)}) custom-call(f32[11,16,128]{2,1,0:T(8,128)S(1)} %collective-permute-done.3.near, f32[2,5,16,128]{3,2,1,0:T(8,128)S(1)} %shard_map.32.other, f32[4,9,16,128]{3,2,1,0:T(8,128)S(1)} %get-tuple-element.35.refs_0_, ...), custom_call_target="tpu_custom_call" | custom-call | tf_op jit(solution)/shard_map/pallas_call | solution.py:719
  17.3 1.6 %collective-permute-start.5 = (f32[5,16,128]{2,1,0:T(8,128)S(1)}, f32[5,16,128]{2,1,0:T(8,128)S(1)}, u32[]{:S(2)}, u32[]{:S(2)}) collective-permute-start(f32[5,16,128]{2,1,0:T(8,128)S(1)} %get-tuple-element.41), channel_id=1, source_target_pairs={{0,8},{4,12},{8,0},{12,4},{1,9},{5,13},{9,1},{13,5},{2,10},{6,14},... | collective-permute-start | bytes 122888 | tf_op jit(solution)/shard_map/ppermute | solution.py:737
  19.0 1.0 %collective-permute-start.6 = (f32[5,16,128]{2,1,0:T(8,128)S(1)}, f32[5,16,128]{2,1,0:T(8,128)S(1)}, u32[]{:S(2)}, u32[]{:S(2)}) collective-permute-start(f32[5,16,128]{2,1,0:T(8,128)S(1)} %get-tuple-element.42), channel_id=1, source_target_pairs={{0,12},{4,8},{8,4},{12,0},{1,13},{5,9},{9,5},{13,1},{2,14},{6,10},... | collective-permute-start | bytes 122888 | tf_op jit(solution)/shard_map/ppermute | solution.py:737
  20.0 0.9 %collective-permute-start.7 = (f32[5,16,128]{2,1,0:T(8,128)S(1)}, f32[5,16,128]{2,1,0:T(8,128)S(1)}, u32[]{:S(2)}, u32[]{:S(2)}) collective-permute-start(f32[5,16,128]{2,1,0:T(8,128)S(1)} %get-tuple-element.43), channel_id=1, source_target_pairs={{0,4},{4,0},{8,12},{12,8},{1,5},{5,1},{9,13},{13,9},{2,6},{6,2},{1... | collective-permute-start | bytes 122888 | tf_op jit(solution)/shard_map/ppermute | solution.py:737
  20.9 1.8 %collective-permute-done.5.refs_0_ = f32[5,16,128]{2,1,0:T(8,128)S(1)} collective-permute-done((f32[5,16,128]{2,1,0:T(8,128)S(1)}, f32[5,16,128]{2,1,0:T(8,128)S(1)}, u32[]{:S(2)}, u32[]{:S(2)}) %collective-permute-start.5) | collective-permute-done | bytes 40992 | tf_op jit(solution)/shard_map/ppermute | solution.py:737
  22.7 2.0 %collective-permute-done.6.refs_1_ = f32[5,16,128]{2,1,0:T(8,128)S(1)} collective-permute-done((f32[5,16,128]{2,1,0:T(8,128)S(1)}, f32[5,16,128]{2,1,0:T(8,128)S(1)}, u32[]{:S(2)}, u32[]{:S(2)}) %collective-permute-start.6) | collective-permute-done | bytes 40992 | tf_op jit(solution)/shard_map/ppermute | solution.py:737
  24.8 0.0 collective-permute-done.7.refs_2_
  24.8 0.9 %shard_map.34 = f32[1,5,4,16,128]{4,3,2,1,0:T(8,128)} custom-call(f32[5,16,128]{2,1,0:T(8,128)S(1)} %collective-permute-done.5.refs_0_, f32[5,16,128]{2,1,0:T(8,128)S(1)} %collective-permute-done.6.refs_1_, f32[5,16,128]{2,1,0:T(8,128)S(1)} %collective-permute-done.7.refs_2_, f32[5,16,128]{2,1,0:T(8,128)S(1)} %get-tuple-element.44.refs_3_), custom_call_target="tpu_custom_call" | custom-call | tf_op jit(solution)/shard_map/pallas_call | solution.py:719
Async XLA Ops:
  0.0 0.9 %copy-start = (f32[1,5,4,16,128]{4,3,2,1,0:T(8,128)S(1)}, f32[1,5,4,16,128]{4,3,2,1,0:T(8,128)}, u32[]{:S(2)}) copy-start(f32[1,5,4,16,128]{4,3,2,1,0:T(8,128)} %flow.1) | copy-start | bytes 491524
  1.3 6.7 %collective-permute-start = (f32[6,16,128]{2,1,0:T(8,128)S(1)}, f32[6,16,128]{2,1,0:T(8,128)S(1)}, u32[]{:S(2)}, u32[]{:S(2)}) collective-permute-start(f32[6,16,128]{2,1,0:T(8,128)S(1)} %get-tuple-element.25), channel_id=1, source_target_pairs={{0,8},{4,12},{8,0},{12,4},{1,9},{5,13},{9,1},{13,5},{2,10},{6,14},... | collective-permute-start | bytes 147464 | tf_op jit(solution)/shard_map/ppermute | solution.py:737
  5.4 6.0 %collective-permute-start.1 = (f32[6,16,128]{2,1,0:T(8,128)S(1)}, f32[6,16,128]{2,1,0:T(8,128)S(1)}, u32[]{:S(2)}, u32[]{:S(2)}) collective-permute-start(f32[6,16,128]{2,1,0:T(8,128)S(1)} %get-tuple-element.26), channel_id=1, source_target_pairs={{0,12},{4,8},{8,4},{12,0},{1,13},{5,9},{9,5},{13,1},{2,14},{6,10},... | collective-permute-start | bytes 147464 | tf_op jit(solution)/shard_map/ppermute | solution.py:737
  6.7 0.7 %copy-start.1 = (s32[16]{0:T(128)S(1)}, s32[16]{0:T(128)}, u32[]{:S(2)}) copy-start(s32[16]{0:T(128)} %match.1) | copy-start | bytes 196
  6.7 4.6 %collective-permute-start.2 = (f32[6,16,128]{2,1,0:T(8,128)S(1)}, f32[6,16,128]{2,1,0:T(8,128)S(1)}, u32[]{:S(2)}, u32[]{:S(2)}) collective-permute-start(f32[6,16,128]{2,1,0:T(8,128)S(1)} %get-tuple-element.27), channel_id=1, source_target_pairs={{0,4},{4,0},{8,12},{12,8},{1,5},{5,1},{9,13},{13,9},{2,6},{6,2},{1... | collective-permute-start | bytes 147464 | tf_op jit(solution)/shard_map/ppermute | solution.py:737
  11.7 1.9 %collective-permute-start.4 = (f32[11,16,128]{2,1,0:T(8,128)S(1)}, f32[11,16,128]{2,1,0:T(8,128)S(1)}, u32[]{:S(2)}, u32[]{:S(2)}) collective-permute-start(f32[11,16,128]{2,1,0:T(8,128)S(1)} %get-tuple-element.31), channel_id=1, source_target_pairs={{0,1},{1,0},{2,3},{3,2},{4,5},{5,4},{6,7},{7,6},{8,9},{9,8},{10,11... | collective-permute-start | bytes 270344 | tf_op jit(solution)/shard_map/ppermute | solution.py:755
  11.8 4.6 %collective-permute-start.3 = (f32[11,16,128]{2,1,0:T(8,128)S(1)}, f32[11,16,128]{2,1,0:T(8,128)S(1)}, u32[]{:S(2)}, u32[]{:S(2)}) collective-permute-start(f32[11,16,128]{2,1,0:T(8,128)S(1)} %get-tuple-element.30), channel_id=1, source_target_pairs={{0,4},{1,2},{2,1},{3,7},{4,0},{5,6},{6,5},{7,3},{8,12},{9,10},{10,... | collective-permute-start | bytes 270344 | tf_op jit(solution)/shard_map/ppermute | solution.py:756
  17.3 5.4 %collective-permute-start.5 = (f32[5,16,128]{2,1,0:T(8,128)S(1)}, f32[5,16,128]{2,1,0:T(8,128)S(1)}, u32[]{:S(2)}, u32[]{:S(2)}) collective-permute-start(f32[5,16,128]{2,1,0:T(8,128)S(1)} %get-tuple-element.41), channel_id=1, source_target_pairs={{0,8},{4,12},{8,0},{12,4},{1,9},{5,13},{9,1},{13,5},{2,10},{6,14},... | collective-permute-start | bytes 122888 | tf_op jit(solution)/shard_map/ppermute | solution.py:737
  19.0 5.8 %collective-permute-start.6 = (f32[5,16,128]{2,1,0:T(8,128)S(1)}, f32[5,16,128]{2,1,0:T(8,128)S(1)}, u32[]{:S(2)}, u32[]{:S(2)}) collective-permute-start(f32[5,16,128]{2,1,0:T(8,128)S(1)} %get-tuple-element.42), channel_id=1, source_target_pairs={{0,12},{4,8},{8,4},{12,0},{1,13},{5,9},{9,5},{13,1},{2,14},{6,10},... | collective-permute-start | bytes 122888 | tf_op jit(solution)/shard_map/ppermute | solution.py:737
  20.0 4.8 %collective-permute-start.7 = (f32[5,16,128]{2,1,0:T(8,128)S(1)}, f32[5,16,128]{2,1,0:T(8,128)S(1)}, u32[]{:S(2)}, u32[]{:S(2)}) collective-permute-start(f32[5,16,128]{2,1,0:T(8,128)S(1)} %get-tuple-element.43), channel_id=1, source_target_pairs={{0,4},{4,0},{8,12},{12,8},{1,5},{5,1},{9,13},{13,9},{2,6},{6,2},{1... | collective-permute-start | bytes 122888 | tf_op jit(solution)/shard_map/ppermute | solution.py:737

commit v6 on v5

--- a/solution.py
+++ b/solution.py
@@ -291,24 +291,33 @@
     return lane_ids() // chunk
 
 
-def turn_groups(tiles):
-    low_half = lane_ids() < lanes // 2
-    even_group = jnp.bitwise_and(group_ids(), 1) == 0
-    out = list(tiles)
-    for a, b, mask, width in ((0, 2, low_half, 2), (1, 3, low_half, 2), (0, 1, even_group, 1), (2, 3, even_group, 1)):
-        first, second = out[a], out[b]
-        out[a] = jnp.where(mask, first, turn(second, chunk * width))
-        out[b] = jnp.where(mask, turn(first, -chunk * width), second)
-    return out
-
-
-def by_distance(items, me):
-    out = list(items)
-    for bit, pairs in ((1, ((0, 1), (2, 3))), (2, ((0, 2), (1, 3)))):
-        is_set = jnp.bitwise_and(me, bit) != 0
-        for a, b in pairs:
-            out[a], out[b] = jnp.where(is_set, out[b], out[a]), jnp.where(is_set, out[a], out[b])
-    return out
+class Groups:
+    def __init__(self, me):
+        group = group_ids()
+        self.amounts = [chunk * (me + layer) for layer in range(layers)]
+        self.masks = []
+        for distance in range(inst_count):
+            total = jnp.bitwise_xor(me, distance) + me
+            self.masks.append([group == jnp.bitwise_and(total + layer, 3) for layer in range(layers)])
+
+    def send(self, tiles):
+        turned = [turn(values, mod_lanes(amount)) for values, amount in zip(tiles, self.amounts)]
+        messages = []
+        for masks in self.masks:
+            out = turned[0]
+            for layer in range(1, layers):
+                out = jnp.where(masks[layer], turned[layer], out)
+            messages.append(out)
+        return messages
+
+    def receive(self, messages):
+        tiles = []
+        for layer, amount in enumerate(self.amounts):
+            out = messages[0]
+            for distance in range(1, inst_count):
+                out = jnp.where(self.masks[distance][layer], messages[distance], out)
+            tiles.append(turn(out, mod_lanes(4 * lanes - amount)))
+        return tiles
 
 
 def pack_kernel(flow, *refs):
@@ -321,9 +330,10 @@
     part_at = jnp.bitwise_and(place, 3)
     index = [mod_lanes(step + (chunk * jnp.bitwise_xor(part_at, layer) + lanes)) for layer in range(layers)]
     edges = [jnp.zeros(tile, jnp.float32)] * inst_count
+    groups = Groups(me)
     for field in range(5):
         tiles = [flow[0, field, layer] for layer in range(layers)]
-        for distance, values in enumerate(by_distance(turn_groups(tiles), me)):
+        for distance, values in enumerate(groups.send(tiles)):
             messages[distance][field] = values
         for layer in range(layers):
             got = pick_lanes(tiles[layer], index[layer])
@@ -332,10 +342,6 @@
                 edges[distance] = jnp.where(here, got, edges[distance])
     for distance in range(inst_count):
         messages[distance][5] = edges[distance]
-
-
-def spread_tiles(received, field, me):
-    return turn_groups(by_distance([message[field] for message in received], me))
 
 
 def unpack_kernel(*refs):
@@ -348,8 +354,9 @@
     level = jnp.clip(band - 1, 0, layers - 1)
     inner = jnp.bitwise_xor(level, me) * 4 + jnp.bitwise_and(lane, 3)
     up_edge = down_edge = jnp.zeros(tile, jnp.float32)
+    groups = Groups(me)
     for field in range(5):
-        tiles = spread_tiles(received, field, me)
+        tiles = groups.receive([message[field] for message in received])
         for layer in range(layers):
             main[field, layer] = tiles[layer]
         for place in range(2):
@@ -693,25 +700,21 @@
     high = jnp.bitwise_and(where_on, 1)
     closed = jnp.logical_or(where_on == 0, where_on == lax.axis_size("space") - 1)
     end, inner = side_values(high, closed, near, shared, scratch)
-    me = lax.axis_index("inst")
+    groups = Groups(lax.axis_index("inst"))
     is_high = high == 1
     for field in range(5):
         low_side = [jnp.where(is_high, other[place, field], mine[field]) for place, mine in ((0, end), (1, inner))]
         high_side = [jnp.where(is_high, mine[field], other[place, field]) for place, mine in ((1, inner), (0, end))]
-        for distance, values in enumerate(by_distance(turn_groups(low_side + high_side), me)):
+        for distance, values in enumerate(groups.send(low_side + high_side)):
             messages[distance][field] = values
 
 
 def return_kernel(*refs):
     received, out = in_order(refs[:4]), refs[4]
-    me = lax.axis_index("inst")
-
-    def one_field(field, carry):
-        for layer, values in enumerate(spread_tiles(received, field, me)):
+    groups = Groups(lax.axis_index("inst"))
+    for field in range(5):
+        for layer, values in enumerate(groups.receive([message[field] for message in received])):
             out[0, field, layer] = values
-        return carry
-
-    unrolled(5, one_field)
 
 
 def call(kernel, outs, operands, scratch=(), scalars=0):

time: 25.8 us -> 25.4 us (0.984)
  Pallas kernels: 5.31 us -> 4.89 us
    pallas_call x7, Pallas kernels: 5.31 us -> 4.89 us  [call(): pl.pallas_call(kernel, out_shape=shapes, in_specs=[smem] * scalars + [vme...]
where the time goes in v6:
time: 25.4 us; the launch traced here: 25.2 us
  starting transfers between devices  9.59 us (38%)
  waiting for transfers between devices  9.32 us (37%)
  Pallas kernels  4.89 us (19%)
  local copies, waits for them, and re-layouts  1.34 us (5%)
    ppermute x6, starting transfers between devices, swap_instances(): got.append(lax.ppermute(message, 'inst', route) if distance else message)  9.23 us
    ppermute x6, waiting for transfers between devices, swap_instances(): got.append(lax.ppermute(message, 'inst', route) if distance else message)  7.28 us
    pallas_call x7, Pallas kernels, call(): pl.pallas_call(kernel, out_shape=shapes, in_specs=[smem] * scalars + [vme...  4.89 us
    ppermute x1, waiting for transfers between devices, on_device_fast(): near_b = lax.ppermute(near_b, ('inst', 'space'), route_b)  2.04 us
    unnamed x4, local copies, waits for them, and re-layouts  1.34 us
  transfers between devices with their start and end apart: 8, of which 4 were waited for; matrix products, arithmetic and copies ran while one was open for 0% of the time, Pallas kernels for 11%

profile of v6, /device:TPU:0, one launch (start us, length us, event | category | flops | bytes accessed | tf_op | source)
XLA Modules:
  0.0 25.2 jit_solution(12016016263864932880)
XLA Ops:
  0.0 0.0 copy-start
  0.0 0.9 %copy-done = f32[1,5,4,16,128]{4,3,2,1,0:T(8,128)S(1)} copy-done((f32[1,5,4,16,128]{4,3,2,1,0:T(8,128)S(1)}, f32[1,5,4,16,128]{4,3,2,1,0:T(8,128)}, u32[]{:S(2)}) %copy-start) | copy-done | bytes 163864
  0.9 0.2 shard_map.28
  1.1 4.1 %collective-permute-start = (f32[6,16,128]{2,1,0:T(8,128)S(1)}, f32[6,16,128]{2,1,0:T(8,128)S(1)}, u32[]{:S(2)}, u32[]{:S(2)}) collective-permute-start(f32[6,16,128]{2,1,0:T(8,128)S(1)} %get-tuple-element.25), channel_id=1, source_target_pairs={{0,8},{4,12},{8,0},{12,4},{1,9},{5,13},{9,1},{13,5},{2,10},{6,14},... | collective-permute-start | bytes 147464 | tf_op jit(solution)/shard_map/ppermute | solution.py:740
  5.2 1.3 %collective-permute-start.1 = (f32[6,16,128]{2,1,0:T(8,128)S(1)}, f32[6,16,128]{2,1,0:T(8,128)S(1)}, u32[]{:S(2)}, u32[]{:S(2)}) collective-permute-start(f32[6,16,128]{2,1,0:T(8,128)S(1)} %get-tuple-element.26), channel_id=1, source_target_pairs={{0,12},{4,8},{8,4},{12,0},{1,13},{5,9},{9,5},{13,1},{2,14},{6,10},... | collective-permute-start | bytes 147464 | tf_op jit(solution)/shard_map/ppermute | solution.py:740
  6.6 0.0 copy-start.1
  6.6 0.2 collective-permute-start.2
  6.8 0.4 %copy-done.1 = s32[16]{0:T(128)S(1)} copy-done((s32[16]{0:T(128)S(1)}, s32[16]{0:T(128)}, u32[]{:S(2)}) %copy-start.1) | copy-done | bytes 88
  7.2 0.6 %shard_map.29 = (s32[16,128]{1,0:T(8,128)S(1)}, s32[16,128]{1,0:T(8,128)S(1)}) custom-call(s32[16]{0:T(128)S(1)} %copy-done.1, f32[6,16,128]{2,1,0:T(8,128)S(1)} %get-tuple-element.28.behind.refs_3_), custom_call_target="tpu_custom_call" | custom-call | tf_op jit(solution)/shard_map/pallas_call | solution.py:722
  7.8 0.0 collective-permute-done.refs_0_
  7.8 3.4 %collective-permute-done.1.refs_1_ = f32[6,16,128]{2,1,0:T(8,128)S(1)} collective-permute-done((f32[6,16,128]{2,1,0:T(8,128)S(1)}, f32[6,16,128]{2,1,0:T(8,128)S(1)}, u32[]{:S(2)}, u32[]{:S(2)}) %collective-permute-start.1) | collective-permute-done | bytes 49184 | tf_op jit(solution)/shard_map/ppermute | solution.py:740
  11.2 0.0 collective-permute-done.2.refs_2_
  11.2 0.3 %shard_map.30 = (f32[11,16,128]{2,1,0:T(8,128)S(1)}, f32[11,16,128]{2,1,0:T(8,128)S(1)}, f32[5,4,16,128]{3,2,1,0:T(8,128)S(1)}, f32[5,16,128]{2,1,0:T(8,128)S(1)}) custom-call(f32[6,16,128]{2,1,0:T(8,128)S(1)} %collective-permute-done.refs_0_, f32[6,16,128]{2,1,0:T(8,128)S(1)} %collective-permute-done.1.refs_1_, ...), custom_call_target="tpu_custom_call" | custom-call | tf_op jit(solution)/shard_map/pallas_call | solution.py:722
  11.5 0.1 collective-permute-start.4
  11.6 0.3 %collective-permute-start.3 = (f32[11,16,128]{2,1,0:T(8,128)S(1)}, f32[11,16,128]{2,1,0:T(8,128)S(1)}, u32[]{:S(2)}, u32[]{:S(2)}) collective-permute-start(f32[11,16,128]{2,1,0:T(8,128)S(1)} %get-tuple-element.30), channel_id=1, source_target_pairs={{0,4},{1,2},{2,1},{3,7},{4,0},{5,6},{6,5},{7,3},{8,12},{9,10},{10,... | collective-permute-start | bytes 270344 | tf_op jit(solution)/shard_map/ppermute | solution.py:759
  11.8 1.5 %shard_map.31 = (f32[4,9,16,128]{3,2,1,0:T(8,128)S(1)}, f32[9,16,128]{2,1,0:T(8,128)S(1)}, f32[4,5,16,128]{3,2,1,0:T(8,128)S(1)}, f32[5,16,128]{2,1,0:T(8,128)S(...) custom-call(s32[16,128]{1,0:T(8,128)S(1)} %get-tuple-element.29.refs_4_.above.refs_6_, ...), custom_call_target="tpu_custom_call" | custom-call | tf_op jit(solution)/shard_map/pallas_call | solution.py:722
  13.4 0.0 collective-permute-done.4.near
  13.4 0.7 %shard_map.32.other = f32[2,5,16,128]{3,2,1,0:T(8,128)S(1)} custom-call(f32[11,16,128]{2,1,0:T(8,128)S(1)} %collective-permute-done.4.near, f32[4,9,16,128]{3,2,1,0:T(8,128)S(1)} %get-tuple-element.35.refs_0_, f32[9,16,128]{2,1,0:T(8,128)S(1)} %get-tuple-element.36.refs_1_, f32[4,5,16,128]{3,2,1,0:T(8,128)S(1)} %get-tuple-element.37.refs_2_, ...), custom_call_target="tpu_custom_call" | custom-call | tf_op jit(solution)/shard_map/pallas_call | solution.py:722
  14.1 2.0 %collective-permute-done.3.near = f32[11,16,128]{2,1,0:T(8,128)S(1)} collective-permute-done((f32[11,16,128]{2,1,0:T(8,128)S(1)}, f32[11,16,128]{2,1,0:T(8,128)S(1)}, u32[]{:S(2)}, u32[]{:S(2)}) %collective-permute-start.3) | collective-permute-done | bytes 90144 | tf_op jit(solution)/shard_map/ppermute | solution.py:759
  16.1 0.8 %shard_map.33 = (f32[5,16,128]{2,1,0:T(8,128)S(1)}, f32[5,16,128]{2,1,0:T(8,128)S(1)}, f32[5,16,128]{2,1,0:T(8,128)S(1)}, f32[5,16,128]{2,1,0:T(8,128)S(1)}) custom-call(f32[11,16,128]{2,1,0:T(8,128)S(1)} %collective-permute-done.3.near, f32[2,5,16,128]{3,2,1,0:T(8,128)S(1)} %shard_map.32.other, f32[4,9,16,128]{3,2,1,0:T(8,128)S(1)} %get-tuple-element.35.refs_0_, ...), custom_call_target="tpu_custom_call" | custom-call | tf_op jit(solution)/shard_map/pallas_call | solution.py:722
  17.0 1.6 %collective-permute-start.5 = (f32[5,16,128]{2,1,0:T(8,128)S(1)}, f32[5,16,128]{2,1,0:T(8,128)S(1)}, u32[]{:S(2)}, u32[]{:S(2)}) collective-permute-start(f32[5,16,128]{2,1,0:T(8,128)S(1)} %get-tuple-element.41), channel_id=1, source_target_pairs={{0,8},{4,12},{8,0},{12,4},{1,9},{5,13},{9,1},{13,5},{2,10},{6,14},... | collective-permute-start | bytes 122888 | tf_op jit(solution)/shard_map/ppermute | solution.py:740
  18.6 1.0 %collective-permute-start.6 = (f32[5,16,128]{2,1,0:T(8,128)S(1)}, f32[5,16,128]{2,1,0:T(8,128)S(1)}, u32[]{:S(2)}, u32[]{:S(2)}) collective-permute-start(f32[5,16,128]{2,1,0:T(8,128)S(1)} %get-tuple-element.42), channel_id=1, source_target_pairs={{0,12},{4,8},{8,4},{12,0},{1,13},{5,9},{9,5},{13,1},{2,14},{6,10},... | collective-permute-start | bytes 122888 | tf_op jit(solution)/shard_map/ppermute | solution.py:740
  19.6 0.9 %collective-permute-start.7 = (f32[5,16,128]{2,1,0:T(8,128)S(1)}, f32[5,16,128]{2,1,0:T(8,128)S(1)}, u32[]{:S(2)}, u32[]{:S(2)}) collective-permute-start(f32[5,16,128]{2,1,0:T(8,128)S(1)} %get-tuple-element.43), channel_id=1, source_target_pairs={{0,4},{4,0},{8,12},{12,8},{1,5},{5,1},{9,13},{13,9},{2,6},{6,2},{1... | collective-permute-start | bytes 122888 | tf_op jit(solution)/shard_map/ppermute | solution.py:740
  20.5 1.8 %collective-permute-done.5.refs_0_ = f32[5,16,128]{2,1,0:T(8,128)S(1)} collective-permute-done((f32[5,16,128]{2,1,0:T(8,128)S(1)}, f32[5,16,128]{2,1,0:T(8,128)S(1)}, u32[]{:S(2)}, u32[]{:S(2)}) %collective-permute-start.5) | collective-permute-done | bytes 40992 | tf_op jit(solution)/shard_map/ppermute | solution.py:740
  22.4 2.0 %collective-permute-done.6.refs_1_ = f32[5,16,128]{2,1,0:T(8,128)S(1)} collective-permute-done((f32[5,16,128]{2,1,0:T(8,128)S(1)}, f32[5,16,128]{2,1,0:T(8,128)S(1)}, u32[]{:S(2)}, u32[]{:S(2)}) %collective-permute-start.6) | collective-permute-done | bytes 40992 | tf_op jit(solution)/shard_map/ppermute | solution.py:740
  24.4 0.0 collective-permute-done.7.refs_2_
  24.4 0.8 %shard_map.34 = f32[1,5,4,16,128]{4,3,2,1,0:T(8,128)} custom-call(f32[5,16,128]{2,1,0:T(8,128)S(1)} %collective-permute-done.5.refs_0_, f32[5,16,128]{2,1,0:T(8,128)S(1)} %collective-permute-done.6.refs_1_, f32[5,16,128]{2,1,0:T(8,128)S(1)} %collective-permute-done.7.refs_2_, f32[5,16,128]{2,1,0:T(8,128)S(1)} %get-tuple-element.44.refs_3_), custom_call_target="tpu_custom_call" | custom-call | tf_op jit(solution)/shard_map/pallas_call | solution.py:722
Async XLA Ops:
  0.0 0.9 %copy-start = (f32[1,5,4,16,128]{4,3,2,1,0:T(8,128)S(1)}, f32[1,5,4,16,128]{4,3,2,1,0:T(8,128)}, u32[]{:S(2)}) copy-start(f32[1,5,4,16,128]{4,3,2,1,0:T(8,128)} %flow.1) | copy-start | bytes 491524
  1.1 6.7 %collective-permute-start = (f32[6,16,128]{2,1,0:T(8,128)S(1)}, f32[6,16,128]{2,1,0:T(8,128)S(1)}, u32[]{:S(2)}, u32[]{:S(2)}) collective-permute-start(f32[6,16,128]{2,1,0:T(8,128)S(1)} %get-tuple-element.25), channel_id=1, source_target_pairs={{0,8},{4,12},{8,0},{12,4},{1,9},{5,13},{9,1},{13,5},{2,10},{6,14},... | collective-permute-start | bytes 147464 | tf_op jit(solution)/shard_map/ppermute | solution.py:740
  5.2 6.0 %collective-permute-start.1 = (f32[6,16,128]{2,1,0:T(8,128)S(1)}, f32[6,16,128]{2,1,0:T(8,128)S(1)}, u32[]{:S(2)}, u32[]{:S(2)}) collective-permute-start(f32[6,16,128]{2,1,0:T(8,128)S(1)} %get-tuple-element.26), channel_id=1, source_target_pairs={{0,12},{4,8},{8,4},{12,0},{1,13},{5,9},{9,5},{13,1},{2,14},{6,10},... | collective-permute-start | bytes 147464 | tf_op jit(solution)/shard_map/ppermute | solution.py:740
  6.6 0.7 %copy-start.1 = (s32[16]{0:T(128)S(1)}, s32[16]{0:T(128)}, u32[]{:S(2)}) copy-start(s32[16]{0:T(128)} %match.1) | copy-start | bytes 196
  6.6 4.6 %collective-permute-start.2 = (f32[6,16,128]{2,1,0:T(8,128)S(1)}, f32[6,16,128]{2,1,0:T(8,128)S(1)}, u32[]{:S(2)}, u32[]{:S(2)}) collective-permute-start(f32[6,16,128]{2,1,0:T(8,128)S(1)} %get-tuple-element.27), channel_id=1, source_target_pairs={{0,4},{4,0},{8,12},{12,8},{1,5},{5,1},{9,13},{13,9},{2,6},{6,2},{1... | collective-permute-start | bytes 147464 | tf_op jit(solution)/shard_map/ppermute | solution.py:740
  11.5 1.9 %collective-permute-start.4 = (f32[11,16,128]{2,1,0:T(8,128)S(1)}, f32[11,16,128]{2,1,0:T(8,128)S(1)}, u32[]{:S(2)}, u32[]{:S(2)}) collective-permute-start(f32[11,16,128]{2,1,0:T(8,128)S(1)} %get-tuple-element.31), channel_id=1, source_target_pairs={{0,1},{1,0},{2,3},{3,2},{4,5},{5,4},{6,7},{7,6},{8,9},{9,8},{10,11... | collective-permute-start | bytes 270344 | tf_op jit(solution)/shard_map/ppermute | solution.py:758
  11.6 4.6 %collective-permute-start.3 = (f32[11,16,128]{2,1,0:T(8,128)S(1)}, f32[11,16,128]{2,1,0:T(8,128)S(1)}, u32[]{:S(2)}, u32[]{:S(2)}) collective-permute-start(f32[11,16,128]{2,1,0:T(8,128)S(1)} %get-tuple-element.30), channel_id=1, source_target_pairs={{0,4},{1,2},{2,1},{3,7},{4,0},{5,6},{6,5},{7,3},{8,12},{9,10},{10,... | collective-permute-start | bytes 270344 | tf_op jit(solution)/shard_map/ppermute | solution.py:759
  17.0 5.4 %collective-permute-start.5 = (f32[5,16,128]{2,1,0:T(8,128)S(1)}, f32[5,16,128]{2,1,0:T(8,128)S(1)}, u32[]{:S(2)}, u32[]{:S(2)}) collective-permute-start(f32[5,16,128]{2,1,0:T(8,128)S(1)} %get-tuple-element.41), channel_id=1, source_target_pairs={{0,8},{4,12},{8,0},{12,4},{1,9},{5,13},{9,1},{13,5},{2,10},{6,14},... | collective-permute-start | bytes 122888 | tf_op jit(solution)/shard_map/ppermute | solution.py:740
  18.6 5.8 %collective-permute-start.6 = (f32[5,16,128]{2,1,0:T(8,128)S(1)}, f32[5,16,128]{2,1,0:T(8,128)S(1)}, u32[]{:S(2)}, u32[]{:S(2)}) collective-permute-start(f32[5,16,128]{2,1,0:T(8,128)S(1)} %get-tuple-element.42), channel_id=1, source_target_pairs={{0,12},{4,8},{8,4},{12,0},{1,13},{5,9},{9,5},{13,1},{2,14},{6,10},... | collective-permute-start | bytes 122888 | tf_op jit(solution)/shard_map/ppermute | solution.py:740
  19.6 4.8 %collective-permute-start.7 = (f32[5,16,128]{2,1,0:T(8,128)S(1)}, f32[5,16,128]{2,1,0:T(8,128)S(1)}, u32[]{:S(2)}, u32[]{:S(2)}) collective-permute-start(f32[5,16,128]{2,1,0:T(8,128)S(1)} %get-tuple-element.43), channel_id=1, source_target_pairs={{0,4},{4,0},{8,12},{12,8},{1,5},{5,1},{9,13},{13,9},{2,6},{6,2},{1... | collective-permute-start | bytes 122888 | tf_op jit(solution)/shard_map/ppermute | solution.py:740

commit v7 on v6

--- a/solution.py
+++ b/solution.py
@@ -239,9 +239,10 @@
 
 
 order = (2, 3, 1, 0)
-
-
-def in_order(items):
+back = (3, 2, 1, 0)
+
+
+def in_order(items, order=order):
     return [items[order.index(distance)] for distance in range(inst_count)]
 
 
@@ -294,6 +295,7 @@
 class Groups:
     def __init__(self, me):
         group = group_ids()
+        self.me = me
         self.amounts = [chunk * (me + layer) for layer in range(layers)]
         self.masks = []
         for distance in range(inst_count):
@@ -301,7 +303,12 @@
             self.masks.append([group == jnp.bitwise_and(total + layer, 3) for layer in range(layers)])
 
     def send(self, tiles):
-        turned = [turn(values, mod_lanes(amount)) for values, amount in zip(tiles, self.amounts)]
+        return self.share([self.turned(values, layer) for layer, values in enumerate(tiles)])
+
+    def turned(self, values, layer):
+        return turn(values, mod_lanes(chunk * (self.me + layer)))
+
+    def share(self, turned):
         messages = []
         for masks in self.masks:
             out = turned[0]
@@ -515,6 +522,7 @@
         low_seam, high_seam = me == 0, me == inst_count - 1
         self.to_main = start + jnp.where(self.is_first, jnp.where(low_seam, 1 - ahead, 1), 3)
         self.from_main = mod_lanes(start + jnp.where(self.slot == 1, jnp.where(low_seam, ahead, 0), chunk - 1))
+        self.beside_end = start + jnp.where(self.slot == 3, jnp.where(high_seam, ahead + 2, 2), 1)
         self.beside = mod_lanes(lane + jnp.where(self.slot == 3, jnp.where(high_seam, ahead - 1, -1), 1))
 
     def mains(self, ref, places):
@@ -542,12 +550,26 @@
     def as_upper(self, face, moved):
         return jnp.where(self.seam, turn(moved, chunk * self.lag), face)
 
-    def change(self, cells, layer):
+    def end_faces(self, cells, band, mains):
+        slot = self.slot
+        index = mod_lanes(self.beside_end + band * 4)
+        halo = [pick_lanes(part, index) for part in cells.base]
+        lower = Cells([jnp.where(slot == 3, b, a) for a, b in zip(halo, mains)])
+        upper = [jnp.where(slot == 1, b, a) for a, b in zip(halo, mains)]
+        upper = Cells([jnp.where(self.seam, pick_rows(part, self.above), part) for part in upper])
+        faces = roe_flux(lower, upper, 1)
+        packed = faces[0]
+        for part in range(1, 5):
+            packed = jnp.where(self.band == part, faces[part], packed)
+        at_low = jnp.logical_and(self.seam, slot == 1)
+        return jnp.where(at_low, pick_rows(packed, self.below), packed)
+
+    def change(self, cells, layer, packed=None):
         faces = roe_flux(cells, cells.map(lambda part: turn(part, -1)), 1)
-        index = mod_lanes((layer + 1) * 4 + self.to_main + lanes)
         changes = []
         for part in range(5):
-            edge = pick_lanes(self.edge_faces[part], index)
+            tile_of, band = (self.edge_faces[part], layer + 1) if packed is None else (packed, part)
+            edge = pick_lanes(tile_of, mod_lanes(band * 4 + self.to_main + lanes))
             upper = jnp.where(self.is_last, edge, faces[part])
             lower = jnp.where(self.is_first, edge, turn(faces[part], 1))
             changes.append(upper - lower)
@@ -581,9 +603,9 @@
     for part in range(5):
         lower_use = pitch.as_upper(faces[part], moved[part])
         along = jnp.where(slot == 1, faces[part] - turn(faces[part], 1), faces[part] - turn(lower_use, -1))
-        value = over_instances(state[part]) + 0.5 * (along + span[part])
+        between = jnp.where(jnp.logical_and(pitch.band > 0, pitch.band < layers), axial[part], 0.0)
+        value = over_instances(state[part]) + 0.5 * (along + span[part] + (between - turn(between, 4)))
         part_edge[part] = value
-        value = value + 0.5 * (axial[part] - turn(axial[part], 4))
         state[part] = state[part] - pseudo_step * value
     edge_second = cells_of_conserved(state)
 
@@ -629,11 +651,10 @@
 
 def side_values(high, closed, near, shared, scratch):
     first, edge_first, part_first, part_edge, second_middle, part_second, above, below, halo = shared
-    ends, second, edge_faces = scratch
-    pitch = Pitch(above[...], below[...], edge_faces)
+    ends, second = scratch
+    pitch = Pitch(above[...], below[...], None)
     is_high = high == 1
     own = high * (layers - 1)
-    outer_band = high * (layers + 1)
 
     own_cells = get(first, own)
     put(ends, 2 - 2 * high, own_cells)
@@ -643,27 +664,29 @@
         if closed is not None:
             cells = Cells([jnp.where(closed, a, b) for a, b in zip(own_cells.parts, cells.parts)])
         put(ends, place, cells)
-    outside = []
+    draws = []
     for field in range(5):
-        value = turn(near[10], mod_lanes(4 * (outer_band - field) + lanes))
-        outside.append(value if closed is None else jnp.where(closed, halo[field], value))
-    outside = cells_of_draws(outside).parts
-    in_outer = pitch.band == outer_band
-    edge_cells = Cells([jnp.where(in_outer, part, edge_first[number]) for number, part in enumerate(outside)])
-    pitch.edges(edge_cells, pitch.mains(ends, [(0, 1)]))
-    axial = roe_flux(edge_cells, edge_cells.map(lambda part: turn(part, -4)), 0)
-    state = edge_cells.conserved()
+        value = turn(near[10], mod_lanes(4 * (own + 1 - field) + lanes))
+        draws.append(value if closed is None else jnp.where(closed, halo[field], value))
+    outside = cells_of_draws(draws)
+    inside = Cells([edge_first[number] for number in range(fields_kept)])
+    pairs = list(zip(inside.base, outside.base))
+    lower = Cells([jnp.where(is_high, a, b) for a, b in pairs])
+    upper = Cells([jnp.where(is_high, b, a) for a, b in pairs])
+    axial = roe_flux(lower, upper, 0)
+    state = inside.conserved()
     for part in range(5):
-        value = part_edge[part] + 0.5 * (axial[part] - turn(axial[part], 4))
+        value = part_edge[part] + 0.5 * jnp.where(is_high, axial[part], -axial[part])
         state[part] = state[part] - pseudo_step * value
     edge_second = cells_of_conserved(state)
 
-    def middle_values(ref, layer):
+    def middle_values(ref, edge_cells):
         cells = get(ref, 1)
+        packed = pitch.end_faces(edge_cells, own + 1, pitch.mains(ref, [(0, 1)]))
         lower = roe_flux(get(ref, 0), cells, 0)
         upper = roe_flux(cells, get(ref, 2), 0)
         span = span_change(cells)
-        along = pitch.change(cells, layer)
+        along = pitch.change(cells, None, packed)
         state = cells.conserved()
         values, inward = [], []
         for part in range(5):
@@ -672,7 +695,7 @@
             inward.append(0.5 * jnp.where(is_high, lower[part], -upper[part]))
         return state, values, inward
 
-    state, values, inward = middle_values(ends, outer_band - 1)
+    state, values, inward = middle_values(ends, outside)
     beyond = cells_of_conserved([a - pseudo_step * b for a, b in zip(state, values)])
     state = own_cells.conserved()
     state = [a - pseudo_step * (part_first[own, part] + inward[part]) for part, a in enumerate(state)]
@@ -681,9 +704,10 @@
         beyond = Cells([jnp.where(closed, a, b) for a, b in zip(own_second.parts, beyond.parts)])
     put(second, 1, own_second)
     put(second, 2 * high, beyond)
-    pitch.edges(edge_second, pitch.mains(second, [(0, 1)]))
-    _, values, inward = middle_values(second, own)
-    return values, [part_second[high, part] + inward[part] for part in range(5)]
+    _, values, inward = middle_values(second, edge_second)
+    groups = Groups(lax.axis_index("inst"))
+    inner = [part_second[high, part] + inward[part] for part in range(5)]
+    return [groups.turned(part, own) for part in values], [groups.turned(part, 1 + high) for part in inner]
 
 
 def near_side_kernel(near, *refs):
@@ -695,7 +719,7 @@
 
 
 def far_side_kernel(near, other, *refs):
-    shared, messages, scratch = refs[:9], in_order(refs[9:13]), refs[13:]
+    shared, messages, scratch = refs[:9], in_order(refs[9:13], back), refs[13:]
     where_on = lax.axis_index("space")
     high = jnp.bitwise_and(where_on, 1)
     closed = jnp.logical_or(where_on == 0, where_on == lax.axis_size("space") - 1)
@@ -705,12 +729,12 @@
     for field in range(5):
         low_side = [jnp.where(is_high, other[place, field], mine[field]) for place, mine in ((0, end), (1, inner))]
         high_side = [jnp.where(is_high, mine[field], other[place, field]) for place, mine in ((1, inner), (0, end))]
-        for distance, values in enumerate(groups.send(low_side + high_side)):
+        for distance, values in enumerate(groups.share(low_side + high_side)):
             messages[distance][field] = values
 
 
 def return_kernel(*refs):
-    received, out = in_order(refs[:4]), refs[4]
+    received, out = in_order(refs[:4], back), refs[4]
     groups = Groups(lax.axis_index("inst"))
     for field in range(5):
         for layer, values in enumerate(groups.receive([message[field] for message in received])):
@@ -733,7 +757,7 @@
     return shape + tile, jnp.float32
 
 
-def swap_instances(messages):
+def swap_instances(messages, order=order):
     got = []
     for distance, message in zip(order, messages):
         route = [(i, i ^ distance) for i in range(inst_count)]
@@ -771,10 +795,10 @@
         [(5,) + tile],
     )
     shared = [*inner, above, below, halo]
-    scratch = [(3, fields_kept) + tile, (3, fields_kept) + tile, (5,) + tile]
+    scratch = [(3, fields_kept) + tile, (3, fields_kept) + tile]
     (other,) = call(near_side_kernel, [floats(2, 5)], [near_a, *shared], scratch)
     results = call(far_side_kernel, [floats(5)] * inst_count, [near_b, other, *shared], scratch)
-    return call(return_kernel, [(flow_state.shape, jnp.float32)], swap_instances(results))[0]
+    return call(return_kernel, [(flow_state.shape, jnp.float32)], swap_instances(results, back))[0]
 
 
 def solution(mesh):

time: 25.4 us -> 25.1 us (0.988)
  waiting for transfers between devices: 9.32 us -> 8.32 us
  starting transfers between devices: 9.59 us -> 10.5 us
    ppermute x6, waiting for transfers between devices: 7.28 us -> 6.23 us  [swap_instances(): got.append(lax.ppermute(message, 'inst', route) if distance else message)]
    ppermute x6, starting transfers between devices: 9.23 us -> 10.1 us  [swap_instances(): got.append(lax.ppermute(message, 'inst', route) if distance else message)]
where the time goes in v7:
time: 25.1 us; the launch traced here: 24.9 us
  starting transfers between devices  10.5 us (42%)
  waiting for transfers between devices  8.32 us (33%)
  Pallas kernels  4.73 us (19%)
  local copies, waits for them, and re-layouts  1.34 us (5%)
    ppermute x6, starting transfers between devices, swap_instances(): got.append(lax.ppermute(message, 'inst', route) if distance else message)  10.1 us
    ppermute x6, waiting for transfers between devices, swap_instances(): got.append(lax.ppermute(message, 'inst', route) if distance else message)  6.23 us
    pallas_call x7, Pallas kernels, call(): pl.pallas_call(kernel, out_shape=shapes, in_specs=[smem] * scalars + [vme...  4.73 us
    ppermute x1, waiting for transfers between devices, on_device_fast(): near_b = lax.ppermute(near_b, ('inst', 'space'), route_b)  2.08 us
    unnamed x4, local copies, waits for them, and re-layouts  1.34 us
  transfers between devices with their start and end apart: 8, of which 4 were waited for; matrix products, arithmetic and copies ran while one was open for 0% of the time, Pallas kernels for 11%

profile of v7, /device:TPU:0, one launch (start us, length us, event | category | flops | bytes accessed | tf_op | source)
XLA Modules:
  0.0 24.9 jit_solution(14296100216340589722)
XLA Ops:
  0.0 0.0 copy-start
  0.0 0.9 %copy-done = f32[1,5,4,16,128]{4,3,2,1,0:T(8,128)S(1)} copy-done((f32[1,5,4,16,128]{4,3,2,1,0:T(8,128)S(1)}, f32[1,5,4,16,128]{4,3,2,1,0:T(8,128)}, u32[]{:S(2)}) %copy-start) | copy-done | bytes 163864
  0.9 0.2 shard_map.28
  1.1 4.1 %collective-permute-start = (f32[6,16,128]{2,1,0:T(8,128)S(1)}, f32[6,16,128]{2,1,0:T(8,128)S(1)}, u32[]{:S(2)}, u32[]{:S(2)}) collective-permute-start(f32[6,16,128]{2,1,0:T(8,128)S(1)} %get-tuple-element.25), channel_id=1, source_target_pairs={{0,8},{4,12},{8,0},{12,4},{1,9},{5,13},{9,1},{13,5},{2,10},{6,14},... | collective-permute-start | bytes 147464 | tf_op jit(solution)/shard_map/ppermute | solution.py:764
  5.2 1.3 %collective-permute-start.1 = (f32[6,16,128]{2,1,0:T(8,128)S(1)}, f32[6,16,128]{2,1,0:T(8,128)S(1)}, u32[]{:S(2)}, u32[]{:S(2)}) collective-permute-start(f32[6,16,128]{2,1,0:T(8,128)S(1)} %get-tuple-element.26), channel_id=1, source_target_pairs={{0,12},{4,8},{8,4},{12,0},{1,13},{5,9},{9,5},{13,1},{2,14},{6,10},... | collective-permute-start | bytes 147464 | tf_op jit(solution)/shard_map/ppermute | solution.py:764
  6.6 0.0 copy-start.1
  6.6 0.2 collective-permute-start.2
  6.8 0.4 %copy-done.1 = s32[16]{0:T(128)S(1)} copy-done((s32[16]{0:T(128)S(1)}, s32[16]{0:T(128)}, u32[]{:S(2)}) %copy-start.1) | copy-done | bytes 88
  7.2 0.6 %shard_map.29 = (s32[16,128]{1,0:T(8,128)S(1)}, s32[16,128]{1,0:T(8,128)S(1)}) custom-call(s32[16]{0:T(128)S(1)} %copy-done.1, f32[6,16,128]{2,1,0:T(8,128)S(1)} %get-tuple-element.28.behind.refs_3_), custom_call_target="tpu_custom_call" | custom-call | tf_op jit(solution)/shard_map/pallas_call | solution.py:746
  7.8 0.0 collective-permute-done.refs_0_
  7.8 3.4 %collective-permute-done.1.refs_1_ = f32[6,16,128]{2,1,0:T(8,128)S(1)} collective-permute-done((f32[6,16,128]{2,1,0:T(8,128)S(1)}, f32[6,16,128]{2,1,0:T(8,128)S(1)}, u32[]{:S(2)}, u32[]{:S(2)}) %collective-permute-start.1) | collective-permute-done | bytes 49184 | tf_op jit(solution)/shard_map/ppermute | solution.py:764
  11.2 0.0 collective-permute-done.2.refs_2_
  11.2 0.3 %shard_map.30 = (f32[11,16,128]{2,1,0:T(8,128)S(1)}, f32[11,16,128]{2,1,0:T(8,128)S(1)}, f32[5,4,16,128]{3,2,1,0:T(8,128)S(1)}, f32[5,16,128]{2,1,0:T(8,128)S(1)}) custom-call(f32[6,16,128]{2,1,0:T(8,128)S(1)} %collective-permute-done.refs_0_, f32[6,16,128]{2,1,0:T(8,128)S(1)} %collective-permute-done.1.refs_1_, ...), custom_call_target="tpu_custom_call" | custom-call | tf_op jit(solution)/shard_map/pallas_call | solution.py:746
  11.5 0.1 collective-permute-start.4
  11.6 0.3 %collective-permute-start.3 = (f32[11,16,128]{2,1,0:T(8,128)S(1)}, f32[11,16,128]{2,1,0:T(8,128)S(1)}, u32[]{:S(2)}, u32[]{:S(2)}) collective-permute-start(f32[11,16,128]{2,1,0:T(8,128)S(1)} %get-tuple-element.30), channel_id=1, source_target_pairs={{0,4},{1,2},{2,1},{3,7},{4,0},{5,6},{6,5},{7,3},{8,12},{9,10},{10,... | collective-permute-start | bytes 270344 | tf_op jit(solution)/shard_map/ppermute | solution.py:783
  11.8 1.5 %shard_map.31 = (f32[4,9,16,128]{3,2,1,0:T(8,128)S(1)}, f32[9,16,128]{2,1,0:T(8,128)S(1)}, f32[4,5,16,128]{3,2,1,0:T(8,128)S(1)}, f32[5,16,128]{2,1,0:T(8,128)S(...) custom-call(s32[16,128]{1,0:T(8,128)S(1)} %get-tuple-element.29.refs_4_.above.refs_6_, ...), custom_call_target="tpu_custom_call" | custom-call | tf_op jit(solution)/shard_map/pallas_call | solution.py:746
  13.4 0.0 collective-permute-done.4.near
  13.4 0.7 %shard_map.32.other = f32[2,5,16,128]{3,2,1,0:T(8,128)S(1)} custom-call(f32[11,16,128]{2,1,0:T(8,128)S(1)} %collective-permute-done.4.near, f32[4,9,16,128]{3,2,1,0:T(8,128)S(1)} %get-tuple-element.35.refs_0_, f32[9,16,128]{2,1,0:T(8,128)S(1)} %get-tuple-element.36.refs_1_, f32[4,5,16,128]{3,2,1,0:T(8,128)S(1)} %get-tuple-element.37.refs_2_, ...), custom_call_target="tpu_custom_call" | custom-call | tf_op jit(solution)/shard_map/pallas_call | solution.py:746
  14.1 2.1 %collective-permute-done.3.near = f32[11,16,128]{2,1,0:T(8,128)S(1)} collective-permute-done((f32[11,16,128]{2,1,0:T(8,128)S(1)}, f32[11,16,128]{2,1,0:T(8,128)S(1)}, u32[]{:S(2)}, u32[]{:S(2)}) %collective-permute-start.3) | collective-permute-done | bytes 90144 | tf_op jit(solution)/shard_map/ppermute | solution.py:783
  16.1 0.7 %shard_map.33 = (f32[5,16,128]{2,1,0:T(8,128)S(1)}, f32[5,16,128]{2,1,0:T(8,128)S(1)}, f32[5,16,128]{2,1,0:T(8,128)S(1)}, f32[5,16,128]{2,1,0:T(8,128)S(1)}) custom-call(f32[11,16,128]{2,1,0:T(8,128)S(1)} %collective-permute-done.3.near, f32[2,5,16,128]{3,2,1,0:T(8,128)S(1)} %shard_map.32.other, f32[4,9,16,128]{3,2,1,0:T(8,128)S(1)} %get-tuple-element.35.refs_0_, ...), custom_call_target="tpu_custom_call" | custom-call | tf_op jit(solution)/shard_map/pallas_call | solution.py:746
  16.9 2.4 %collective-permute-start.5 = (f32[5,16,128]{2,1,0:T(8,128)S(1)}, f32[5,16,128]{2,1,0:T(8,128)S(1)}, u32[]{:S(2)}, u32[]{:S(2)}) collective-permute-start(f32[5,16,128]{2,1,0:T(8,128)S(1)} %get-tuple-element.41), channel_id=1, source_target_pairs={{0,12},{4,8},{8,4},{12,0},{1,13},{5,9},{9,5},{13,1},{2,14},{6,10},... | collective-permute-start | bytes 122888 | tf_op jit(solution)/shard_map/ppermute | solution.py:764
  19.2 0.0 collective-permute-start.6
  19.2 2.1 %collective-permute-start.7 = (f32[5,16,128]{2,1,0:T(8,128)S(1)}, f32[5,16,128]{2,1,0:T(8,128)S(1)}, u32[]{:S(2)}, u32[]{:S(2)}) collective-permute-start(f32[5,16,128]{2,1,0:T(8,128)S(1)} %get-tuple-element.43), channel_id=1, source_target_pairs={{0,4},{4,0},{8,12},{12,8},{1,5},{5,1},{9,13},{13,9},{2,6},{6,2},{1... | collective-permute-start | bytes 122888 | tf_op jit(solution)/shard_map/ppermute | solution.py:764
  21.3 1.5 %collective-permute-done.5.refs_0_ = f32[5,16,128]{2,1,0:T(8,128)S(1)} collective-permute-done((f32[5,16,128]{2,1,0:T(8,128)S(1)}, f32[5,16,128]{2,1,0:T(8,128)S(1)}, u32[]{:S(2)}, u32[]{:S(2)}) %collective-permute-start.5) | collective-permute-done | bytes 40992 | tf_op jit(solution)/shard_map/ppermute | solution.py:764
  22.8 1.4 %collective-permute-done.6.refs_1_ = f32[5,16,128]{2,1,0:T(8,128)S(1)} collective-permute-done((f32[5,16,128]{2,1,0:T(8,128)S(1)}, f32[5,16,128]{2,1,0:T(8,128)S(1)}, u32[]{:S(2)}, u32[]{:S(2)}) %collective-permute-start.6) | collective-permute-done | bytes 40992 | tf_op jit(solution)/shard_map/ppermute | solution.py:764
  24.1 0.0 collective-permute-done.7.refs_2_
  24.2 0.8 %shard_map.34 = f32[1,5,4,16,128]{4,3,2,1,0:T(8,128)} custom-call(f32[5,16,128]{2,1,0:T(8,128)S(1)} %collective-permute-done.5.refs_0_, f32[5,16,128]{2,1,0:T(8,128)S(1)} %collective-permute-done.6.refs_1_, f32[5,16,128]{2,1,0:T(8,128)S(1)} %collective-permute-done.7.refs_2_, f32[5,16,128]{2,1,0:T(8,128)S(1)} %get-tuple-element.44.refs_3_), custom_call_target="tpu_custom_call" | custom-call | tf_op jit(solution)/shard_map/pallas_call | solution.py:746
Async XLA Ops:
  0.0 0.9 %copy-start = (f32[1,5,4,16,128]{4,3,2,1,0:T(8,128)S(1)}, f32[1,5,4,16,128]{4,3,2,1,0:T(8,128)}, u32[]{:S(2)}) copy-start(f32[1,5,4,16,128]{4,3,2,1,0:T(8,128)} %flow.1) | copy-start | bytes 491524
  1.1 6.7 %collective-permute-start = (f32[6,16,128]{2,1,0:T(8,128)S(1)}, f32[6,16,128]{2,1,0:T(8,128)S(1)}, u32[]{:S(2)}, u32[]{:S(2)}) collective-permute-start(f32[6,16,128]{2,1,0:T(8,128)S(1)} %get-tuple-element.25), channel_id=1, source_target_pairs={{0,8},{4,12},{8,0},{12,4},{1,9},{5,13},{9,1},{13,5},{2,10},{6,14},... | collective-permute-start | bytes 147464 | tf_op jit(solution)/shard_map/ppermute | solution.py:764
  5.2 6.0 %collective-permute-start.1 = (f32[6,16,128]{2,1,0:T(8,128)S(1)}, f32[6,16,128]{2,1,0:T(8,128)S(1)}, u32[]{:S(2)}, u32[]{:S(2)}) collective-permute-start(f32[6,16,128]{2,1,0:T(8,128)S(1)} %get-tuple-element.26), channel_id=1, source_target_pairs={{0,12},{4,8},{8,4},{12,0},{1,13},{5,9},{9,5},{13,1},{2,14},{6,10},... | collective-permute-start | bytes 147464 | tf_op jit(solution)/shard_map/ppermute | solution.py:764
  6.6 0.7 %copy-start.1 = (s32[16]{0:T(128)S(1)}, s32[16]{0:T(128)}, u32[]{:S(2)}) copy-start(s32[16]{0:T(128)} %match.1) | copy-start | bytes 196
  6.6 4.6 %collective-permute-start.2 = (f32[6,16,128]{2,1,0:T(8,128)S(1)}, f32[6,16,128]{2,1,0:T(8,128)S(1)}, u32[]{:S(2)}, u32[]{:S(2)}) collective-permute-start(f32[6,16,128]{2,1,0:T(8,128)S(1)} %get-tuple-element.27), channel_id=1, source_target_pairs={{0,4},{4,0},{8,12},{12,8},{1,5},{5,1},{9,13},{13,9},{2,6},{6,2},{1... | collective-permute-start | bytes 147464 | tf_op jit(solution)/shard_map/ppermute | solution.py:764
  11.5 1.9 %collective-permute-start.4 = (f32[11,16,128]{2,1,0:T(8,128)S(1)}, f32[11,16,128]{2,1,0:T(8,128)S(1)}, u32[]{:S(2)}, u32[]{:S(2)}) collective-permute-start(f32[11,16,128]{2,1,0:T(8,128)S(1)} %get-tuple-element.31), channel_id=1, source_target_pairs={{0,1},{1,0},{2,3},{3,2},{4,5},{5,4},{6,7},{7,6},{8,9},{9,8},{10,11... | collective-permute-start | bytes 270344 | tf_op jit(solution)/shard_map/ppermute | solution.py:782
  11.6 4.6 %collective-permute-start.3 = (f32[11,16,128]{2,1,0:T(8,128)S(1)}, f32[11,16,128]{2,1,0:T(8,128)S(1)}, u32[]{:S(2)}, u32[]{:S(2)}) collective-permute-start(f32[11,16,128]{2,1,0:T(8,128)S(1)} %get-tuple-element.30), channel_id=1, source_target_pairs={{0,4},{1,2},{2,1},{3,7},{4,0},{5,6},{6,5},{7,3},{8,12},{9,10},{10,... | collective-permute-start | bytes 270344 | tf_op jit(solution)/shard_map/ppermute | solution.py:783
  16.9 5.9 %collective-permute-start.5 = (f32[5,16,128]{2,1,0:T(8,128)S(1)}, f32[5,16,128]{2,1,0:T(8,128)S(1)}, u32[]{:S(2)}, u32[]{:S(2)}) collective-permute-start(f32[5,16,128]{2,1,0:T(8,128)S(1)} %get-tuple-element.41), channel_id=1, source_target_pairs={{0,12},{4,8},{8,4},{12,0},{1,13},{5,9},{9,5},{13,1},{2,14},{6,10},... | collective-permute-start | bytes 122888 | tf_op jit(solution)/shard_map/ppermute | solution.py:764
  19.2 4.9 %collective-permute-start.6 = (f32[5,16,128]{2,1,0:T(8,128)S(1)}, f32[5,16,128]{2,1,0:T(8,128)S(1)}, u32[]{:S(2)}, u32[]{:S(2)}) collective-permute-start(f32[5,16,128]{2,1,0:T(8,128)S(1)} %get-tuple-element.42), channel_id=1, source_target_pairs={{0,8},{4,12},{8,0},{12,4},{1,9},{5,13},{9,1},{13,5},{2,10},{6,14},... | collective-permute-start | bytes 122888 | tf_op jit(solution)/shard_map/ppermute | solution.py:764
  19.2 4.9 %collective-permute-start.7 = (f32[5,16,128]{2,1,0:T(8,128)S(1)}, f32[5,16,128]{2,1,0:T(8,128)S(1)}, u32[]{:S(2)}, u32[]{:S(2)}) collective-permute-start(f32[5,16,128]{2,1,0:T(8,128)S(1)} %get-tuple-element.43), channel_id=1, source_target_pairs={{0,4},{4,0},{8,12},{12,8},{1,5},{5,1},{9,13},{13,9},{2,6},{6,2},{1... | collective-permute-start | bytes 122888 | tf_op jit(solution)/shard_map/ppermute | solution.py:764

commit v8 on v7

--- a/solution.py
+++ b/solution.py
@@ -285,6 +285,8 @@
 
 
 def mod_lanes(amount):
+    if isinstance(amount, int):
+        return amount % lanes
     return jnp.bitwise_and(amount, lanes - 1)
 
 
@@ -653,7 +655,6 @@
     first, edge_first, part_first, part_edge, second_middle, part_second, above, below, halo = shared
     ends, second = scratch
     pitch = Pitch(above[...], below[...], None)
-    is_high = high == 1
     own = high * (layers - 1)
 
     own_cells = get(first, own)
@@ -670,13 +671,10 @@
         draws.append(value if closed is None else jnp.where(closed, halo[field], value))
     outside = cells_of_draws(draws)
     inside = Cells([edge_first[number] for number in range(fields_kept)])
-    pairs = list(zip(inside.base, outside.base))
-    lower = Cells([jnp.where(is_high, a, b) for a, b in pairs])
-    upper = Cells([jnp.where(is_high, b, a) for a, b in pairs])
-    axial = roe_flux(lower, upper, 0)
+    axial = roe_flux(inside, outside, 0) if high else roe_flux(outside, inside, 0)
     state = inside.conserved()
     for part in range(5):
-        value = part_edge[part] + 0.5 * jnp.where(is_high, axial[part], -axial[part])
+        value = part_edge[part] + 0.5 * (axial[part] if high else -axial[part])
         state[part] = state[part] - pseudo_step * value
     edge_second = cells_of_conserved(state)
 
@@ -692,7 +690,7 @@
         for part in range(5):
             value = (upper[part] - lower[part]) + span[part] + along[part]
             values.append(over_instances(state[part]) + 0.5 * value)
-            inward.append(0.5 * jnp.where(is_high, lower[part], -upper[part]))
+            inward.append(0.5 * (lower[part] if high else -upper[part]))
         return state, values, inward
 
     state, values, inward = middle_values(ends, outside)
@@ -712,25 +710,35 @@
 
 def near_side_kernel(near, *refs):
     shared, out, scratch = refs[:9], refs[9], refs[10:]
-    high = 1 - jnp.bitwise_and(lax.axis_index("space"), 1)
-    for place, values in enumerate(side_values(high, None, near, shared, scratch)):
-        for part in range(5):
-            out[place, part] = values[part]
+    odd = jnp.bitwise_and(lax.axis_index("space"), 1)
+
+    for side in range(2):
+
+        @pl.when(odd == 1 - side)
+        def _(high=side):
+            for place, values in enumerate(side_values(high, None, near, shared, scratch)):
+                for part in range(5):
+                    out[place, part] = values[part]
 
 
 def far_side_kernel(near, other, *refs):
     shared, messages, scratch = refs[:9], in_order(refs[9:13], back), refs[13:]
     where_on = lax.axis_index("space")
-    high = jnp.bitwise_and(where_on, 1)
+    odd = jnp.bitwise_and(where_on, 1)
     closed = jnp.logical_or(where_on == 0, where_on == lax.axis_size("space") - 1)
-    end, inner = side_values(high, closed, near, shared, scratch)
-    groups = Groups(lax.axis_index("inst"))
-    is_high = high == 1
-    for field in range(5):
-        low_side = [jnp.where(is_high, other[place, field], mine[field]) for place, mine in ((0, end), (1, inner))]
-        high_side = [jnp.where(is_high, mine[field], other[place, field]) for place, mine in ((1, inner), (0, end))]
-        for distance, values in enumerate(groups.share(low_side + high_side)):
-            messages[distance][field] = values
+
+    for side in range(2):
+
+        @pl.when(odd == side)
+        def _(high=side):
+            end, inner = side_values(high, closed, near, shared, scratch)
+            groups = Groups(lax.axis_index("inst"))
+            for field in range(5):
+                others = [other[place, field] for place in range(2)]
+                tiles = [others[0], others[1], inner[field], end[field]]
+                tiles = tiles if high else [end[field], inner[field], others[1], others[0]]
+                for distance, values in enumerate(groups.share(tiles)):
+                    messages[distance][field] = values
 
 
 def return_kernel(*refs):

time: 25.1 us -> 25 us (level)
  no operation moved by 1% of the time
where the time goes in v8:
time: 25 us; the launch traced here: 24.9 us
  starting transfers between devices  10.5 us (42%)
  waiting for transfers between devices  8.34 us (33%)
  Pallas kernels  4.66 us (19%)
  local copies, waits for them, and re-layouts  1.34 us (5%)
    ppermute x6, starting transfers between devices, swap_instances(): got.append(lax.ppermute(message, 'inst', route) if distance else message)  10.1 us
    ppermute x6, waiting for transfers between devices, swap_instances(): got.append(lax.ppermute(message, 'inst', route) if distance else message)  6.23 us
    pallas_call x7, Pallas kernels, call(): pl.pallas_call(kernel, out_shape=shapes, in_specs=[smem] * scalars + [vme...  4.66 us
    ppermute x1, waiting for transfers between devices, on_device_fast(): near_b = lax.ppermute(near_b, ('inst', 'space'), route_b)  2.11 us
    unnamed x4, local copies, waits for them, and re-layouts  1.34 us
  transfers between devices with their start and end apart: 8, of which 4 were waited for; matrix products, arithmetic and copies ran while one was open for 0% of the time, Pallas kernels for 11%

profile of v8, /device:TPU:0, one launch (start us, length us, event | category | flops | bytes accessed | tf_op | source)
XLA Modules:
  0.0 24.9 jit_solution(3343124290053199508)
XLA Ops:
  0.0 0.0 copy-start
  0.0 0.9 %copy-done = f32[1,5,4,16,128]{4,3,2,1,0:T(8,128)S(1)} copy-done((f32[1,5,4,16,128]{4,3,2,1,0:T(8,128)S(1)}, f32[1,5,4,16,128]{4,3,2,1,0:T(8,128)}, u32[]{:S(2)}) %copy-start) | copy-done | bytes 163864
  0.9 0.2 shard_map.28
  1.1 4.1 %collective-permute-start = (f32[6,16,128]{2,1,0:T(8,128)S(1)}, f32[6,16,128]{2,1,0:T(8,128)S(1)}, u32[]{:S(2)}, u32[]{:S(2)}) collective-permute-start(f32[6,16,128]{2,1,0:T(8,128)S(1)} %get-tuple-element.25), channel_id=1, source_target_pairs={{0,8},{4,12},{8,0},{12,4},{1,9},{5,13},{9,1},{13,5},{2,10},{6,14},... | collective-permute-start | bytes 147464 | tf_op jit(solution)/shard_map/ppermute | solution.py:772
  5.2 1.3 %collective-permute-start.1 = (f32[6,16,128]{2,1,0:T(8,128)S(1)}, f32[6,16,128]{2,1,0:T(8,128)S(1)}, u32[]{:S(2)}, u32[]{:S(2)}) collective-permute-start(f32[6,16,128]{2,1,0:T(8,128)S(1)} %get-tuple-element.26), channel_id=1, source_target_pairs={{0,12},{4,8},{8,4},{12,0},{1,13},{5,9},{9,5},{13,1},{2,14},{6,10},... | collective-permute-start | bytes 147464 | tf_op jit(solution)/shard_map/ppermute | solution.py:772
  6.6 0.0 copy-start.1
  6.6 0.2 collective-permute-start.2
  6.8 0.4 %copy-done.1 = s32[16]{0:T(128)S(1)} copy-done((s32[16]{0:T(128)S(1)}, s32[16]{0:T(128)}, u32[]{:S(2)}) %copy-start.1) | copy-done | bytes 88
  7.2 0.6 %shard_map.29 = (s32[16,128]{1,0:T(8,128)S(1)}, s32[16,128]{1,0:T(8,128)S(1)}) custom-call(s32[16]{0:T(128)S(1)} %copy-done.1, f32[6,16,128]{2,1,0:T(8,128)S(1)} %get-tuple-element.28.behind.refs_3_), custom_call_target="tpu_custom_call" | custom-call | tf_op jit(solution)/shard_map/pallas_call | solution.py:754
  7.8 0.0 collective-permute-done.refs_0_
  7.8 3.4 %collective-permute-done.1.refs_1_ = f32[6,16,128]{2,1,0:T(8,128)S(1)} collective-permute-done((f32[6,16,128]{2,1,0:T(8,128)S(1)}, f32[6,16,128]{2,1,0:T(8,128)S(1)}, u32[]{:S(2)}, u32[]{:S(2)}) %collective-permute-start.1) | collective-permute-done | bytes 49184 | tf_op jit(solution)/shard_map/ppermute | solution.py:772
  11.2 0.0 collective-permute-done.2.refs_2_
  11.2 0.3 %shard_map.30 = (f32[11,16,128]{2,1,0:T(8,128)S(1)}, f32[11,16,128]{2,1,0:T(8,128)S(1)}, f32[5,4,16,128]{3,2,1,0:T(8,128)S(1)}, f32[5,16,128]{2,1,0:T(8,128)S(1)}) custom-call(f32[6,16,128]{2,1,0:T(8,128)S(1)} %collective-permute-done.refs_0_, f32[6,16,128]{2,1,0:T(8,128)S(1)} %collective-permute-done.1.refs_1_, ...), custom_call_target="tpu_custom_call" | custom-call | tf_op jit(solution)/shard_map/pallas_call | solution.py:754
  11.5 0.1 collective-permute-start.4
  11.6 0.3 %collective-permute-start.3 = (f32[11,16,128]{2,1,0:T(8,128)S(1)}, f32[11,16,128]{2,1,0:T(8,128)S(1)}, u32[]{:S(2)}, u32[]{:S(2)}) collective-permute-start(f32[11,16,128]{2,1,0:T(8,128)S(1)} %get-tuple-element.30), channel_id=1, source_target_pairs={{0,4},{1,2},{2,1},{3,7},{4,0},{5,6},{6,5},{7,3},{8,12},{9,10},{10,... | collective-permute-start | bytes 270344 | tf_op jit(solution)/shard_map/ppermute | solution.py:791
  11.8 1.5 %shard_map.31 = (f32[4,9,16,128]{3,2,1,0:T(8,128)S(1)}, f32[9,16,128]{2,1,0:T(8,128)S(1)}, f32[4,5,16,128]{3,2,1,0:T(8,128)S(1)}, f32[5,16,128]{2,1,0:T(8,128)S(...) custom-call(s32[16,128]{1,0:T(8,128)S(1)} %get-tuple-element.29.refs_4_.above.refs_6_, ...), custom_call_target="tpu_custom_call" | custom-call | tf_op jit(solution)/shard_map/pallas_call | solution.py:754
  13.4 0.0 collective-permute-done.4.near
  13.4 0.7 %shard_map.32.other = f32[2,5,16,128]{3,2,1,0:T(8,128)S(1)} custom-call(f32[11,16,128]{2,1,0:T(8,128)S(1)} %collective-permute-done.4.near, f32[4,9,16,128]{3,2,1,0:T(8,128)S(1)} %get-tuple-element.35.refs_0_, f32[9,16,128]{2,1,0:T(8,128)S(1)} %get-tuple-element.36.refs_1_, f32[4,5,16,128]{3,2,1,0:T(8,128)S(1)} %get-tuple-element.37.refs_2_, ...), custom_call_target="tpu_custom_call" | custom-call | tf_op jit(solution)/shard_map/pallas_call | solution.py:754
  14.0 2.1 %collective-permute-done.3.near = f32[11,16,128]{2,1,0:T(8,128)S(1)} collective-permute-done((f32[11,16,128]{2,1,0:T(8,128)S(1)}, f32[11,16,128]{2,1,0:T(8,128)S(1)}, u32[]{:S(2)}, u32[]{:S(2)}) %collective-permute-start.3) | collective-permute-done | bytes 90144 | tf_op jit(solution)/shard_map/ppermute | solution.py:791
  16.1 0.7 %shard_map.33 = (f32[5,16,128]{2,1,0:T(8,128)S(1)}, f32[5,16,128]{2,1,0:T(8,128)S(1)}, f32[5,16,128]{2,1,0:T(8,128)S(1)}, f32[5,16,128]{2,1,0:T(8,128)S(1)}) custom-call(f32[11,16,128]{2,1,0:T(8,128)S(1)} %collective-permute-done.3.near, f32[2,5,16,128]{3,2,1,0:T(8,128)S(1)} %shard_map.32.other, f32[4,9,16,128]{3,2,1,0:T(8,128)S(1)} %get-tuple-element.35.refs_0_, ...), custom_call_target="tpu_custom_call" | custom-call | tf_op jit(solution)/shard_map/pallas_call | solution.py:754
  16.8 2.4 %collective-permute-start.5 = (f32[5,16,128]{2,1,0:T(8,128)S(1)}, f32[5,16,128]{2,1,0:T(8,128)S(1)}, u32[]{:S(2)}, u32[]{:S(2)}) collective-permute-start(f32[5,16,128]{2,1,0:T(8,128)S(1)} %get-tuple-element.41), channel_id=1, source_target_pairs={{0,12},{4,8},{8,4},{12,0},{1,13},{5,9},{9,5},{13,1},{2,14},{6,10},... | collective-permute-start | bytes 122888 | tf_op jit(solution)/shard_map/ppermute | solution.py:772
  19.2 0.0 collective-permute-start.6
  19.2 2.1 %collective-permute-start.7 = (f32[5,16,128]{2,1,0:T(8,128)S(1)}, f32[5,16,128]{2,1,0:T(8,128)S(1)}, u32[]{:S(2)}, u32[]{:S(2)}) collective-permute-start(f32[5,16,128]{2,1,0:T(8,128)S(1)} %get-tuple-element.43), channel_id=1, source_target_pairs={{0,4},{4,0},{8,12},{12,8},{1,5},{5,1},{9,13},{13,9},{2,6},{6,2},{1... | collective-permute-start | bytes 122888 | tf_op jit(solution)/shard_map/ppermute | solution.py:772
  21.3 1.4 %collective-permute-done.5.refs_0_ = f32[5,16,128]{2,1,0:T(8,128)S(1)} collective-permute-done((f32[5,16,128]{2,1,0:T(8,128)S(1)}, f32[5,16,128]{2,1,0:T(8,128)S(1)}, u32[]{:S(2)}, u32[]{:S(2)}) %collective-permute-start.5) | collective-permute-done | bytes 40992 | tf_op jit(solution)/shard_map/ppermute | solution.py:772
  22.7 1.4 %collective-permute-done.6.refs_1_ = f32[5,16,128]{2,1,0:T(8,128)S(1)} collective-permute-done((f32[5,16,128]{2,1,0:T(8,128)S(1)}, f32[5,16,128]{2,1,0:T(8,128)S(1)}, u32[]{:S(2)}, u32[]{:S(2)}) %collective-permute-start.6) | collective-permute-done | bytes 40992 | tf_op jit(solution)/shard_map/ppermute | solution.py:772
  24.1 0.0 collective-permute-done.7.refs_2_
  24.1 0.8 %shard_map.34 = f32[1,5,4,16,128]{4,3,2,1,0:T(8,128)} custom-call(f32[5,16,128]{2,1,0:T(8,128)S(1)} %collective-permute-done.5.refs_0_, f32[5,16,128]{2,1,0:T(8,128)S(1)} %collective-permute-done.6.refs_1_, f32[5,16,128]{2,1,0:T(8,128)S(1)} %collective-permute-done.7.refs_2_, f32[5,16,128]{2,1,0:T(8,128)S(1)} %get-tuple-element.44.refs_3_), custom_call_target="tpu_custom_call" | custom-call | tf_op jit(solution)/shard_map/pallas_call | solution.py:754
Async XLA Ops:
  0.0 0.9 %copy-start = (f32[1,5,4,16,128]{4,3,2,1,0:T(8,128)S(1)}, f32[1,5,4,16,128]{4,3,2,1,0:T(8,128)}, u32[]{:S(2)}) copy-start(f32[1,5,4,16,128]{4,3,2,1,0:T(8,128)} %flow.1) | copy-start | bytes 491524
  1.1 6.7 %collective-permute-start = (f32[6,16,128]{2,1,0:T(8,128)S(1)}, f32[6,16,128]{2,1,0:T(8,128)S(1)}, u32[]{:S(2)}, u32[]{:S(2)}) collective-permute-start(f32[6,16,128]{2,1,0:T(8,128)S(1)} %get-tuple-element.25), channel_id=1, source_target_pairs={{0,8},{4,12},{8,0},{12,4},{1,9},{5,13},{9,1},{13,5},{2,10},{6,14},... | collective-permute-start | bytes 147464 | tf_op jit(solution)/shard_map/ppermute | solution.py:772
  5.2 6.0 %collective-permute-start.1 = (f32[6,16,128]{2,1,0:T(8,128)S(1)}, f32[6,16,128]{2,1,0:T(8,128)S(1)}, u32[]{:S(2)}, u32[]{:S(2)}) collective-permute-start(f32[6,16,128]{2,1,0:T(8,128)S(1)} %get-tuple-element.26), channel_id=1, source_target_pairs={{0,12},{4,8},{8,4},{12,0},{1,13},{5,9},{9,5},{13,1},{2,14},{6,10},... | collective-permute-start | bytes 147464 | tf_op jit(solution)/shard_map/ppermute | solution.py:772
  6.6 0.7 %copy-start.1 = (s32[16]{0:T(128)S(1)}, s32[16]{0:T(128)}, u32[]{:S(2)}) copy-start(s32[16]{0:T(128)} %match.1) | copy-start | bytes 196
  6.6 4.6 %collective-permute-start.2 = (f32[6,16,128]{2,1,0:T(8,128)S(1)}, f32[6,16,128]{2,1,0:T(8,128)S(1)}, u32[]{:S(2)}, u32[]{:S(2)}) collective-permute-start(f32[6,16,128]{2,1,0:T(8,128)S(1)} %get-tuple-element.27), channel_id=1, source_target_pairs={{0,4},{4,0},{8,12},{12,8},{1,5},{5,1},{9,13},{13,9},{2,6},{6,2},{1... | collective-permute-start | bytes 147464 | tf_op jit(solution)/shard_map/ppermute | solution.py:772
  11.5 1.9 %collective-permute-start.4 = (f32[11,16,128]{2,1,0:T(8,128)S(1)}, f32[11,16,128]{2,1,0:T(8,128)S(1)}, u32[]{:S(2)}, u32[]{:S(2)}) collective-permute-start(f32[11,16,128]{2,1,0:T(8,128)S(1)} %get-tuple-element.31), channel_id=1, source_target_pairs={{0,1},{1,0},{2,3},{3,2},{4,5},{5,4},{6,7},{7,6},{8,9},{9,8},{10,11... | collective-permute-start | bytes 270344 | tf_op jit(solution)/shard_map/ppermute | solution.py:790
  11.6 4.6 %collective-permute-start.3 = (f32[11,16,128]{2,1,0:T(8,128)S(1)}, f32[11,16,128]{2,1,0:T(8,128)S(1)}, u32[]{:S(2)}, u32[]{:S(2)}) collective-permute-start(f32[11,16,128]{2,1,0:T(8,128)S(1)} %get-tuple-element.30), channel_id=1, source_target_pairs={{0,4},{1,2},{2,1},{3,7},{4,0},{5,6},{6,5},{7,3},{8,12},{9,10},{10,... | collective-permute-start | bytes 270344 | tf_op jit(solution)/shard_map/ppermute | solution.py:791
  16.8 5.9 %collective-permute-start.5 = (f32[5,16,128]{2,1,0:T(8,128)S(1)}, f32[5,16,128]{2,1,0:T(8,128)S(1)}, u32[]{:S(2)}, u32[]{:S(2)}) collective-permute-start(f32[5,16,128]{2,1,0:T(8,128)S(1)} %get-tuple-element.41), channel_id=1, source_target_pairs={{0,12},{4,8},{8,4},{12,0},{1,13},{5,9},{9,5},{13,1},{2,14},{6,10},... | collective-permute-start | bytes 122888 | tf_op jit(solution)/shard_map/ppermute | solution.py:772
  19.2 4.9 %collective-permute-start.6 = (f32[5,16,128]{2,1,0:T(8,128)S(1)}, f32[5,16,128]{2,1,0:T(8,128)S(1)}, u32[]{:S(2)}, u32[]{:S(2)}) collective-permute-start(f32[5,16,128]{2,1,0:T(8,128)S(1)} %get-tuple-element.42), channel_id=1, source_target_pairs={{0,8},{4,12},{8,0},{12,4},{1,9},{5,13},{9,1},{13,5},{2,10},{6,14},... | collective-permute-start | bytes 122888 | tf_op jit(solution)/shard_map/ppermute | solution.py:772
  19.2 4.9 %collective-permute-start.7 = (f32[5,16,128]{2,1,0:T(8,128)S(1)}, f32[5,16,128]{2,1,0:T(8,128)S(1)}, u32[]{:S(2)}, u32[]{:S(2)}) collective-permute-start(f32[5,16,128]{2,1,0:T(8,128)S(1)} %get-tuple-element.43), channel_id=1, source_target_pairs={{0,4},{4,0},{8,12},{12,8},{1,5},{5,1},{9,13},{13,9},{2,6},{6,2},{1... | collective-permute-start | bytes 122888 | tf_op jit(solution)/shard_map/ppermute | solution.py:772
